TPU v7x, 512 devices: a whole 4x4x16 slice. The times are simulated.
512 devices in a mesh: leaf: 256 (over x, y, z), rep: 2 (over core).
Axes of the slice: x: 4, y: 4, z: 16, core: 2. Of those that a mesh axis runs over, the one named last changes fastest.
Arguments:
- leaf_matrix: bfloat16 [131072, 512], P('leaf')
- leaf_inverse: bfloat16 [131072, 512], P('leaf')
- coupling: bfloat16 [131072, 2048], P('leaf'), may hold values from -0.125 to 0.125
- cubic_coeff: float32 [131072], P('leaf'), may hold values from 0.05 to 0.5
- leaf_load: float32 [131072, 256], P('leaf', 'rep'), may hold values from -6 to 6
- sep_load: float32 [2048, 256], P('leaf', 'rep'), may hold values from -6 to 6
- sep_matrix: float32 [2048, 2048], P(('leaf', 'rep'))
- sep_inverse: float32 [2048, 2048], P(('leaf', 'rep'))
- owner_map: int32 [2048], replicated, may hold values from 0 to 2047, each once
- block_mask: int32 [256, 16], P('leaf'), may hold values 0 or 1
Outputs:
- leaf_solution: float32 [131072, 256], P('leaf', 'rep')
- sep_solution: float32 [2048, 256], P('leaf', 'rep')
Inputs may be any that keep to these rules, and one draw needn't show every extreme that they name: `owner_map`: each of the 2048 separator rows appears exactly once.
All inputs are finite; a program needn't handle non-finite values. No bound on the sum of `block_mask` on one device may be relied on, other than what follows from the above.
Results may differ from a plain program's by a relative error of at most 0.0073.
Values sent between devices are 32-bit elements; how exact they have to be, the bound alone decides.
No kernel may reach another device: no remote copies, remote signals or barrier semaphores. Data moves between devices by JAX's collectives and lax.ppermute only.
A program may use at most 64 MiB of HBM per device.

v0:
```python
import jax
import jax.numpy as jnp
from jax import lax
from jax.sharding import PartitionSpec as P

STEPS = 2
BLOCK = 128


def on_device(
    leaf_matrix,
    leaf_inverse,
    coupling,
    cubic_coeff,
    leaf_load,
    sep_load,
    sep_matrix,
    sep_inverse,
    owner_map,
    block_mask,
):
    width = leaf_matrix.shape[1]
    sep_width = coupling.shape[1]
    cases = leaf_load.shape[1]
    owned = sep_load.shape[0]
    keep_cols = jnp.repeat(block_mask[0], BLOCK).astype(jnp.bfloat16)
    columns = (coupling * keep_cols[None, :])[:, owner_map]
    columns_t = columns.T
    inverse_rows, matrix_rows = (
        lax.all_gather(sep_inverse, "rep", axis=0, tiled=True),
        lax.all_gather(sep_matrix, "rep", axis=0, tiled=True),
    )
    first_row = lax.axis_index("leaf") * owned
    leaf_state = jnp.zeros((width, cases), jnp.float32)
    sep_state = jnp.zeros((sep_width, cases), jnp.float32)
    for newton in range(STEPS):
        resid = leaf_load - jnp.dot(
            leaf_matrix, leaf_state.astype(jnp.bfloat16), preferred_element_type=jnp.float32
        )
        resid = resid - jnp.dot(
            columns, sep_state.astype(jnp.bfloat16), preferred_element_type=jnp.float32
        )
        resid = resid - cubic_coeff[:, None] * leaf_state * leaf_state * leaf_state
        solved = jnp.dot(
            leaf_inverse, resid.astype(jnp.bfloat16), preferred_element_type=jnp.float32
        )
        mixed = (leaf_state + solved).astype(jnp.bfloat16)
        contrib = jnp.dot(columns_t, mixed, preferred_element_type=jnp.float32)
        local_rows = sep_load - jnp.dot(
            matrix_rows,
            sep_state,
            precision=lax.Precision.HIGHEST,
            preferred_element_type=jnp.float32,
        )
        placed = lax.dynamic_update_slice_in_dim(
            jnp.zeros((sep_width, cases), jnp.float32), local_rows, first_row, 0
        )
        rhs_full = lax.psum(placed - contrib, "leaf")
        delta_rows = jnp.dot(
            inverse_rows,
            rhs_full,
            precision=lax.Precision.HIGHEST,
            preferred_element_type=jnp.float32,
        )
        delta = lax.all_gather(delta_rows, "leaf", axis=0, tiled=True)
        sep_state = sep_state + delta
        back = jnp.dot(
            columns, delta.astype(jnp.bfloat16), preferred_element_type=jnp.float32
        ).astype(jnp.bfloat16)
        leaf_state = (
            leaf_state + solved - jnp.dot(leaf_inverse, back, preferred_element_type=jnp.float32)
        )
    sep_rows = lax.dynamic_slice_in_dim(sep_state, first_row, owned, 0)
    return (leaf_state, sep_rows)


def solution(mesh):
    in_specs = (
        P("leaf", None),
        P("leaf", None),
        P("leaf", None),
        P("leaf"),
        P("leaf", "rep"),
        P("leaf", "rep"),
        P(("leaf", "rep"), None),
        P(("leaf", "rep"), None),
        P(),
        P("leaf", None),
    )
    out_specs = (P("leaf", "rep"), P("leaf", "rep"))
    return jax.shard_map(
        on_device, mesh=mesh, in_specs=in_specs, out_specs=out_specs, check_vma=False
    )
```

profile of v0, /device:TPU:6, one launch (start us, length us, event | category | flops | bytes accessed | tf_op | source)
XLA Modules:
  0.0 1236.3 jit_solution(6768864258910992009)
XLA Ops:
  7.2 2.2 all-gather
  9.6 3.9 copy.16
  13.7 1.9 broadcast_multiply_fusion
  15.7 9.2 gather_fusion
  24.8 1.0 fusion
  25.8 1.0 broadcast.20.clone
  27.5 2.2 fusion.10
  29.7 2.9 convolution_subtract_fusion.1
  32.7 1.9 all-gather.1
  34.6 403.0 %all-reduce.3.cloned.1.call-done = f32[2048,128]{1,0:T(8,128)} async-done(((f32[2048,128]{1,0:T(8,128)}), f32[2048,128]{1,0:T(8,128)}) %all-reduce.3.cloned.1.call-update) | async-done | bytes 1048592 | tf_op jit(solution)/shard_map/psum | solution.py:58
  437.6 2.5 convolution_bitcast_fusion.6
  440.1 0.9 copy.17
  441.0 188.0 %all-gather.5.cloned.1.call-done = f32[2048,128]{1,0:T(8,128)} async-done(((f32[8,128]{1,0:T(8,128)}), f32[2048,128]{1,0:T(8,128)}) %all-gather.5.cloned.1.call-update) | async-done | bytes 1048592 | tf_op jit(solution)/shard_map/all_gather | solution.py:65
  629.0 2.0 fusion.15
  631.3 0.8 copy.18
  632.1 1.7 fusion.2
  633.9 1.9 fusion.12
  635.8 1.7 convolution_subtract_fusion
  637.6 396.4 %all-reduce.5.cloned.1.call-done = f32[2048,128]{1,0:T(8,128)} async-done(((f32[2048,128]{1,0:T(8,128)}), f32[2048,128]{1,0:T(8,128)}) %all-reduce.5.cloned.1.call-update) | async-done | bytes 1048592 | tf_op jit(solution)/shard_map/psum | solution.py:58
  1033.9 2.5 convolution_bitcast_fusion.4
  1036.4 188.8 %all-gather.7.cloned.1.call-done = f32[2048,128]{1,0:T(8,128)} async-done(((f32[8,128]{1,0:T(8,128)}), f32[2048,128]{1,0:T(8,128)}) %all-gather.7.cloned.1.call-update) | async-done | bytes 1048592 | tf_op jit(solution)/shard_map/all_gather | solution.py:65
  1225.2 2.4 fusion.1
  1227.6 0.8 copy.19
  1228.5 1.3 dynamic-slice_add_fusion
  (36 shorter events, 1.6 us)
Async XLA Ops:
  7.2 20.4 %copy-start = (bf16[512,512]{1,0:T(8,128)(2,1)S(1)}, bf16[512,512]{1,0:T(8,128)(2,1)}, u32[]{:S(2)}) copy-start(bf16[512,512]{1,0:T(8,128)(2,1)} %param.11) | copy-start | bytes 1572868
  7.2 430.4 %all-reduce.3.cloned.1.call-start = ((), (), s32[]{:S(2)}) async-start(), calls=%async_computation | async-start | bytes 2097152 | tf_op jit(solution)/shard_map/psum | solution.py:58
  9.6 4.0 copy-start.8
  9.6 4.1 copy-start.7
  9.6 4.1 copy-start.6
  15.6 9.2 copy-start.2
  15.6 9.2 copy-start.3
  15.6 11.2 copy-start.5
  24.8 2.7 copy-start.1
  29.7 3.0 copy-start.4
  32.6 596.4 %all-gather.5.cloned.1.call-start = ((), (), s32[]{:S(2)}) async-start(), calls=%async_computation.1 | async-start | bytes 1052672 | tf_op jit(solution)/shard_map/all_gather | solution.py:65
  440.1 593.9 %all-reduce.5.cloned.1.call-start = ((), (), s32[]{:S(2)}) async-start(), calls=%async_computation.2 | async-start | bytes 2097152 | tf_op jit(solution)/shard_map/psum | solution.py:58
  637.5 587.7 %all-gather.7.cloned.1.call-start = ((), (), s32[]{:S(2)}) async-start(), calls=%async_computation.3 | async-start | bytes 1052672 | tf_op jit(solution)/shard_map/all_gather | solution.py:65
Sparse Core Ops, SparseCore 0:
  32.8 404.7 all-reduce.2
  442.4 186.5 all-gather.4
  637.6 396.2 all-reduce.4
  1038.6 186.5 all-gather.6
where the time goes:
time: 1240 us
  waiting for transfers between devices  1180 us (95%)
  matrix products  20.9 us (2%)
  local copies, waits for them, and re-layouts  16.9 us (1%)
  between operations  13.9 us (1%)
    psum x2, waiting for transfers between devices, on_device(): rhs_full = lax.psum(placed - contrib, 'leaf')  799 us
    all_gather x2, waiting for transfers between devices, on_device(): delta = lax.all_gather(delta_rows, 'leaf', axis=0, tiled=True)  377 us
  transfers between devices with their start and end apart: 4, of which 4 were waited for; matrix products, arithmetic and copies ran while one was open for 0% of the time, Pallas kernels for 0%

commit v1 on v0

v1 whole, which is shorter than its diff:
```python
import jax
import jax.numpy as jnp
from jax import lax
from jax.experimental import pallas as pl
from jax.experimental.pallas import tpu as pltpu
from jax.sharding import Mesh, PartitionSpec as P

STEPS = 2
BLOCK = 128
NX, NY, NZ, NC = 4, 4, 16, 2
NXY = NX * NY
TILE = 256
F32 = jnp.float32
BF16 = jnp.bfloat16
VMEM_LIMIT = 48 * 1024 * 1024
HIGHEST = lax.Precision.HIGHEST


def dot(left, right):
    return jnp.dot(left, right, preferred_element_type=F32)


def whole(shape):
    return pl.BlockSpec(shape, lambda *_: (0,) * len(shape))


def params():
    return pltpu.CompilerParams(vmem_limit_bytes=VMEM_LIMIT)


def call(kernel, out, *args):
    return pl.pallas_call(kernel, out_shape=out, compiler_params=params())(*args)


def start_kernel(inverse, coupling, load, keep, owner, columns, solved_out, contrib, masked, mixed_t):
    @pl.when(pl.program_id(0) == 0)
    def _():
        masked[...] = coupling[...] * keep[...]
        solved = dot(inverse[...], load[...].astype(BF16))
        solved_out[...] = solved
        mixed_t[...] = solved.T.astype(BF16)

    rows = lax.broadcasted_iota(jnp.int32, (coupling.shape[1], TILE), 0)
    pick = jnp.where(rows == owner[...], 1.0, 0.0).astype(BF16)
    tile = dot(masked[...], pick).astype(BF16)
    columns[...] = tile
    part = dot(mixed_t[...], tile)
    for i in range(TILE // BLOCK):
        contrib[i] = part[:, i * BLOCK : (i + 1) * BLOCK]


def start(inverse, coupling, load, keep, owner):
    width, sep_width = coupling.shape
    cases = load.shape[1]
    return pl.pallas_call(
        start_kernel,
        grid=(sep_width // TILE,),
        in_specs=[
            whole(inverse.shape),
            whole(coupling.shape),
            whole(load.shape),
            whole(keep.shape),
            pl.BlockSpec((1, TILE), lambda j: (0, j)),
        ],
        out_specs=[
            pl.BlockSpec((width, TILE), lambda j: (0, j)),
            whole(load.shape),
            pl.BlockSpec((TILE // BLOCK, cases, BLOCK), lambda j: (j, 0, 0)),
        ],
        out_shape=[
            jax.ShapeDtypeStruct((width, sep_width), BF16),
            jax.ShapeDtypeStruct(load.shape, F32),
            jax.ShapeDtypeStruct((NXY, cases, BLOCK), F32),
        ],
        scratch_shapes=[pltpu.VMEM((width, sep_width), BF16), pltpu.VMEM((cases, width), BF16)],
        compiler_params=params(),
    )(inverse, coupling, load, keep, owner)


def sum_rows_kernel(parts, local_t, out):
    cases = parts.shape[1]
    total = local_t[...] - jnp.sum(parts[...], axis=0)
    out[...] = total.reshape(NZ, cases // NZ, BLOCK)


def sum_cases_kernel(parts, out):
    out[...] = jnp.broadcast_to(jnp.sum(parts[...], axis=0)[None], out.shape)


def delta_kernel(rhs, inverse_rows, out):
    acc = jnp.zeros(rhs.shape[1:], F32)
    for i in range(NXY):
        acc = acc + lax.dot_general(
            rhs[i],
            inverse_rows[:, i * BLOCK : (i + 1) * BLOCK],
            (((1,), (1,)), ((), ())),
            precision=HIGHEST,
            preferred_element_type=F32,
        )
    out[...] = jnp.broadcast_to(acc[None], out.shape)


def spread_kernel(parts, out):
    cases = parts.shape[0] * parts.shape[1]
    out[...] = jnp.broadcast_to(parts[...].reshape(cases, BLOCK).T[None], out.shape)


def middle_kernel(delta, columns, matrix, inverse, load, cubic, solved_in, state_out, contrib):
    coupled = dot(columns[...], delta[...].astype(BF16))
    state = solved_in[...] - dot(inverse[...], coupled.astype(BF16))
    resid = load[...] - dot(matrix[...], state.astype(BF16)) - coupled
    resid = resid - cubic[...] * state * state * state
    mixed = state + dot(inverse[...], resid.astype(BF16))
    state_out[...] = mixed
    part = dot(mixed.T.astype(BF16), columns[...])
    for i in range(NXY):
        contrib[i] = part[:, i * BLOCK : (i + 1) * BLOCK]


def end_kernel(delta, columns, inverse, mixed, out):
    back = dot(columns[...], delta[...].astype(BF16)).astype(BF16)
    out[...] = mixed[...] - dot(inverse[...], back)


def exchange(parts, axes):
    return lax.all_to_all(parts, axes, 0, 0, tiled=True)


def correction(contrib, local, inverse_rows, place):
    cases = contrib.shape[1]
    case_group = cases // NZ
    local_t = lax.dynamic_update_slice_in_dim(jnp.zeros((BLOCK, cases), F32), local, place, 0).T
    parts = exchange(contrib, ("x", "y"))
    parts = call(sum_rows_kernel, jax.ShapeDtypeStruct((NZ, case_group, BLOCK), F32), parts, local_t)
    parts = exchange(parts, "z")
    rhs = call(sum_cases_kernel, jax.ShapeDtypeStruct((NXY, case_group, BLOCK), F32), parts)
    rhs = exchange(rhs, ("x", "y"))
    delta = call(delta_kernel, jax.ShapeDtypeStruct((NZ, case_group, BLOCK), F32), rhs, inverse_rows)
    delta = exchange(delta, "z")
    delta = call(spread_kernel, jax.ShapeDtypeStruct((NXY, BLOCK, cases), F32), delta)
    return exchange(delta, ("x", "y")).reshape(NXY * BLOCK, cases)


def on_device(
    leaf_matrix,
    leaf_inverse,
    coupling,
    cubic_coeff,
    leaf_load,
    sep_load,
    sep_matrix,
    sep_inverse,
    owner_map,
    block_mask,
):
    owned = sep_load.shape[0]
    inverse_rows = lax.all_gather(sep_inverse, ("z", "c"), axis=0, tiled=True)
    matrix_rows = lax.all_gather(sep_matrix, "c", axis=0, tiled=True)
    place = lax.axis_index("z") * owned
    first_row = lax.axis_index(("x", "y", "z")) * owned
    keep = jnp.repeat(block_mask[0], BLOCK).astype(BF16)[None, :]
    columns, solved, contrib = start(leaf_inverse, coupling, leaf_load, keep, owner_map[None, :])

    delta = correction(contrib, sep_load, inverse_rows, place)
    local = sep_load - jnp.dot(matrix_rows, delta, precision=HIGHEST, preferred_element_type=F32)
    sep_rows = lax.dynamic_slice_in_dim(delta, first_row, owned, 0)
    mixed, contrib = call(
        middle_kernel,
        [jax.ShapeDtypeStruct(leaf_load.shape, F32), jax.ShapeDtypeStruct(contrib.shape, F32)],
        delta,
        columns,
        leaf_matrix,
        leaf_inverse,
        leaf_load,
        cubic_coeff[:, None],
        solved,
    )
    delta = correction(contrib, local, inverse_rows, place)
    leaf_state = call(
        end_kernel, jax.ShapeDtypeStruct(leaf_load.shape, F32), delta, columns, leaf_inverse, mixed
    )
    sep_rows = sep_rows + lax.dynamic_slice_in_dim(delta, first_row, owned, 0)
    return leaf_state, sep_rows


def solution(mesh):
    grid = Mesh(mesh.devices.reshape(NX, NY, NZ, NC), ("x", "y", "z", "c"))
    leaf = ("x", "y", "z")
    in_specs = (
        P(leaf, None),
        P(leaf, None),
        P(leaf, None),
        P(leaf),
        P(leaf, "c"),
        P(leaf, "c"),
        P(leaf + ("c",), None),
        P(leaf + ("c",), None),
        P(),
        P(leaf, None),
    )
    out_specs = (P(leaf, "c"), P(leaf, "c"))
    return jax.shard_map(on_device, mesh=grid, in_specs=in_specs, out_specs=out_specs, check_vma=False)
```

time: 1240 us -> 236 us (0.19)
  waiting for transfers between devices: 1180 us -> 50.9 us
  blocking collectives: 4.05 us -> 94.5 us
  starting transfers between devices: 0.16 us -> 34.1 us
  Pallas kernels: 0 us -> 22.2 us
  matrix products: 20.9 us -> 2.64 us
    psum x2 -> x0, waiting for transfers between devices: 799 us -> none  [on_device(): rhs_full = lax.psum(placed - contrib, 'leaf')]
    all_gather x2 -> x1, waiting for transfers between devices: 377 us -> 4.59 us  [on_device(): inverse_rows = lax.all_gather(sep_inverse, ('z', 'c'), axis=0, tiled=True)]
    all_to_all x0 -> x5, blocking collectives: none -> 92.4 us  [exchange(): return lax.all_to_all(parts, axes, 0, 0, tiled=True)]
    all_to_all x0 -> x5, waiting for transfers between devices: none -> 45.7 us  [exchange(): return lax.all_to_all(parts, axes, 0, 0, tiled=True)]
    all_to_all x0 -> x5, starting transfers between devices: none -> 34.1 us  [exchange(): return lax.all_to_all(parts, axes, 0, 0, tiled=True)]
    pallas_call x0 -> x11, Pallas kernels: none -> 22.2 us  [the longest x10 12 us: call(): pl.pallas_call(kernel, out_shape=out, compiler_params=params())(*args)]
    dot_general x11 -> x1, matrix products: 20.9 us -> 2.64 us  [on_device(): jnp.dot(matrix_rows, delta, precision=HIGHEST, preferred_element_type=F32)]
  transfers between devices with their start and end apart: 4 -> 6, of which waited for: 4 -> 5; matrix products, arithmetic and copies ran while one was open for 0% -> 3% of each run, Pallas kernels for 0% -> 5%
where the time goes in v1:
time: 236 us; the launch traced here: 235 us
  blocking collectives  94.5 us (40%)
  waiting for transfers between devices  50.9 us (22%)
  starting transfers between devices  34.1 us (14%)
  Pallas kernels  22.2 us (9%)
  between operations  14.2 us (6%)
  local copies, waits for them, and re-layouts  14.1 us (6%)
  matrix products  2.64 us (1%)
    all_to_all x5, blocking collectives, exchange(): return lax.all_to_all(parts, axes, 0, 0, tiled=True)  92.4 us
    all_to_all x5, waiting for transfers between devices, exchange(): return lax.all_to_all(parts, axes, 0, 0, tiled=True)  45.7 us
    all_to_all x5, starting transfers between devices, exchange(): return lax.all_to_all(parts, axes, 0, 0, tiled=True)  34.1 us
    unnamed x37, local copies, waits for them, and re-layouts  13.1 us
    pallas_call x10, Pallas kernels, call(): pl.pallas_call(kernel, out_shape=out, compiler_params=params())(*args)  12 us
    pallas_call x1, Pallas kernels, start(): pl.pallas_call(start_kernel, grid=(sep_width // TILE,), in_specs=[whole(i...  10.2 us
  transfers between devices with their start and end apart: 6, of which 5 were waited for; matrix products, arithmetic and copies ran while one was open for 3% of the time, Pallas kernels for 5%

profile of v1, /device:TPU:6, one launch (start us, length us, event | category | flops | bytes accessed | tf_op | source)
XLA Modules:
  0.0 234.6 jit_solution(14947695677457711077)
XLA Ops:
  11.3 10.2 %shard_map.113 = (bf16[512,2048]{1,0:T(8,128)(2,1)S(1)}, f32[512,128]{1,0:T(8,128)S(1)}, f32[16,128,128]{2,1,0:T(8,128)}) custom-call(bf16[512,512]{1,0:T(8,128)(2,1)S(1)} %copy-done.2, bf16[512,2048]{1,0:T(8,128)(2,1)} %coupling.1, f32[512,128]{1,0:T(8,128)S(1)} %copy-done.8, bf16[1,2048]{1,0:T(2,128)(2,1)S(1)} %bitcast.27, s32[1,2048]{1,0:T(1,128)S(1)} %bitcast.28), custom_call_target="tpu_custom_call" | custom-call | tf_op jit(solution)/shard_map/pallas_call | solution.py:55
  21.6 1.4 copy-done
  23.6 9.4 %all-to-all-start = ((f32[16,128,128]{2,1,0:T(8,128)}), f32[16,128,128]{2,1,0:T(8,128)S(1)}, u32[]{:S(2)}, u32[]{:S(2)}) async-start(f32[16,128,128]{2,1,0:T(8,128)} %get-tuple-element.7), calls=%async_computation | async-start | bytes 2097152 | tf_op jit(solution)/shard_map/all_to_all | solution.py:126
  33.5 12.8 %all-to-all-done.parts = f32[16,128,128]{2,1,0:T(8,128)S(1)} async-done(((f32[16,128,128]{2,1,0:T(8,128)}), f32[16,128,128]{2,1,0:T(8,128)S(1)}, u32[]{:S(2)}, u32[]{:S(2)}) %all-to-all-start) | async-done | bytes 1048608 | tf_op jit(solution)/shard_map/all_to_all | solution.py:126
  46.3 28.1 %all_to_all.50.parts = f32[16,8,128]{2,1,0:T(8,128)S(1)} all-to-all(f32[16,8,128]{2,1,0:T(8,128)S(1)} %shard_map.114), channel_id=1, replica_groups=mesh['x'=4,'y'=4,'z'=16,'c'=2] {'z'}, dimensions={0} | all-to-all | bytes 131072 | tf_op jit(solution)/shard_map/all_to_all | solution.py:126
  75.1 5.9 %all-to-all-start.2 = ((f32[16,8,128]{2,1,0:T(8,128)}), f32[16,8,128]{2,1,0:T(8,128)S(1)}, u32[]{:S(2)}, u32[]{:S(2)}) async-start(f32[16,8,128]{2,1,0:T(8,128)} %shard_map.115), calls=%async_computation.2 | async-start | bytes 131072 | tf_op jit(solution)/shard_map/all_to_all | solution.py:126
  81.0 4.6 %all-gather.4.cloned.1.call-done = f32[32,4,2048]{2,1,0:T(4,128)} async-done(((f32[1,4,2048]{2,1,0:T(4,128)}), f32[32,4,2048]{2,1,0:T(4,128)}) %all-gather.4.cloned.1.call-update) | async-done | bytes 1048592 | tf_op jit(solution)/shard_map/all_gather | solution.py:157
  85.6 1.6 reshape.26.inverse_rows
  87.2 1.7 shard_map.116
  88.9 21.0 %all_to_all.51.parts = f32[16,8,128]{2,1,0:T(8,128)S(1)} all-to-all(f32[16,8,128]{2,1,0:T(8,128)S(1)} %shard_map.116), channel_id=1, replica_groups=mesh['x'=4,'y'=4,'z'=16,'c'=2] {'z'}, dimensions={0} | all-to-all | bytes 131072 | tf_op jit(solution)/shard_map/all_to_all | solution.py:126
  111.1 7.1 %all-to-all-start.4 = ((f32[16,128,128]{2,1,0:T(8,128)}), f32[16,128,128]{2,1,0:T(8,128)S(1)}, u32[]{:S(2)}, u32[]{:S(2)}) async-start(f32[16,128,128]{2,1,0:T(8,128)} %copy-done.6), calls=%async_computation.4 | async-start | bytes 2097152 | tf_op jit(solution)/shard_map/all_to_all | solution.py:126
  118.3 13.7 %all-to-all-done.4 = f32[16,128,128]{2,1,0:T(8,128)S(1)} async-done(((f32[16,128,128]{2,1,0:T(8,128)}), f32[16,128,128]{2,1,0:T(8,128)S(1)}, u32[]{:S(2)}, u32[]{:S(2)}) %all-to-all-start.4) | async-done | bytes 1048608 | tf_op jit(solution)/shard_map/all_to_all | solution.py:126
  134.0 4.3 %shard_map.118 = (f32[512,128]{1,0:T(8,128)S(1)}, f32[16,128,128]{2,1,0:T(8,128)S(1)}) custom-call(f32[2048,128]{1,0:T(8,128)S(1)} %bitcast.22, bf16[512,2048]{1,0:T(8,128)(2,1)} %copy-done, bf16[512,512]{1,0:T(8,128)(2,1)S(1)} %copy-done.10, bf16[512,512]{1,0:T(8,128)(2,1)S(1)} %copy-done.3, f32[512,128]{1,0:T(8,128)S(1)} %copy-done.9, ...), custom_call_target="tpu_custom_call" | custom-call | tf_op jit(solution)/shard_map/pallas_call | solution.py:32
  139.3 5.5 %all-to-all-start.5 = ((f32[16,128,128]{2,1,0:T(8,128)}), f32[16,128,128]{2,1,0:T(8,128)S(1)}, u32[]{:S(2)}, u32[]{:S(2)}) async-start(f32[16,128,128]{2,1,0:T(8,128)} %copy-done.7), calls=%async_computation.5 | async-start | bytes 2097152 | tf_op jit(solution)/shard_map/all_to_all | solution.py:126
  144.8 2.1 all-gather.1
  147.5 2.6 %fusion = f32[8,128]{0,1:T(8,128)S(1)} fusion(f32[8,128]{0,1:T(8,128)S(1)} %copy.19, f32[2048,128]{1,0:T(8,128)S(1)} %bitcast.23, f32[8,2048]{1,0:T(8,128)} %reshape.28), kind=kOutput, calls=%fused_computation.1 | convolution fusion | flops 25166848 | bytes 1122304 | tf_op jit(solution)/shard_map/dot_general | solution.py:165
  150.6 8.2 %all-to-all-done.5.parts = f32[16,128,128]{2,1,0:T(8,128)S(1)} async-done(((f32[16,128,128]{2,1,0:T(8,128)}), f32[16,128,128]{2,1,0:T(8,128)S(1)}, u32[]{:S(2)}, u32[]{:S(2)}) %all-to-all-start.5) | async-done | bytes 1048608 | tf_op jit(solution)/shard_map/all_to_all | solution.py:126
  158.9 16.7 %all_to_all.52.parts = f32[16,8,128]{2,1,0:T(8,128)S(1)} all-to-all(f32[16,8,128]{2,1,0:T(8,128)S(1)} %shard_map.119), channel_id=1, replica_groups=mesh['x'=4,'y'=4,'z'=16,'c'=2] {'z'}, dimensions={0} | all-to-all | bytes 131072 | tf_op jit(solution)/shard_map/all_to_all | solution.py:126
  175.6 10.9 %all_to_all.53.rhs = f32[16,8,128]{2,1,0:T(8,128)S(1)} all-to-all(f32[16,8,128]{2,1,0:T(8,128)S(1)} %shard_map.120), channel_id=1, replica_groups=mesh['x'=4,'y'=4,'z'=16,'c'=2] {'x','y'}, dimensions={0} | all-to-all | bytes 131072 | tf_op jit(solution)/shard_map/all_to_all | solution.py:126
  186.5 1.7 shard_map.121
  188.2 15.7 %all_to_all.54.parts = f32[16,8,128]{2,1,0:T(8,128)S(1)} all-to-all(f32[16,8,128]{2,1,0:T(8,128)S(1)} %shard_map.121), channel_id=1, replica_groups=mesh['x'=4,'y'=4,'z'=16,'c'=2] {'z'}, dimensions={0} | all-to-all | bytes 131072 | tf_op jit(solution)/shard_map/all_to_all | solution.py:126
  205.0 6.2 %all-to-all-start.9 = ((f32[16,128,128]{2,1,0:T(8,128)}), f32[16,128,128]{2,1,0:T(8,128)}, u32[]{:S(2)}, u32[]{:S(2)}) async-start(f32[16,128,128]{2,1,0:T(8,128)} %copy-done.5), calls=%async_computation.9 | async-start | bytes 2097152 | tf_op jit(solution)/shard_map/all_to_all | solution.py:126
  211.3 11.1 %all-to-all-done.9 = f32[16,128,128]{2,1,0:T(8,128)} async-done(((f32[16,128,128]{2,1,0:T(8,128)}), f32[16,128,128]{2,1,0:T(8,128)}, u32[]{:S(2)}, u32[]{:S(2)}) %all-to-all-start.9) | async-done | bytes 1048608 | tf_op jit(solution)/shard_map/all_to_all | solution.py:126
  223.4 3.1 %shard_map.123 = f32[512,128]{1,0:T(8,128)} custom-call(f32[2048,128]{1,0:T(8,128)} %bitcast.9.delta, bf16[512,2048]{1,0:T(8,128)(2,1)S(1)} %copy-done.1, bf16[512,512]{1,0:T(8,128)(2,1)S(1)} %copy-done.4, f32[512,128]{1,0:T(8,128)S(1)} %get-tuple-element.11.mixed), custom_call_target="tpu_custom_call" | custom-call | tf_op jit(solution)/shard_map/pallas_call | solution.py:32
  (51 shorter events, 14.9 us)
Async XLA Ops:
  7.2 78.4 %all-gather.4.cloned.1.call-start = ((), (), s32[]{:S(2)}) async-start(), calls=%async_computation.10 | async-start | bytes 1081344 | tf_op jit(solution)/shard_map/all_gather | solution.py:157
  8.6 1.0 copy-start.2
  9.7 0.9 copy-start.8
  10.6 0.7 copy-start.13
  11.3 21.7 %copy-start.14 = (f32[8,128]{1,0:T(8,128)S(1)}, f32[8,128]{1,0:T(8,128)}, u32[]{:S(2)}) copy-start(f32[8,128]{1,0:T(8,128)} %param.15) | copy-start | bytes 12292
  21.6 1.4 copy-start
  22.9 0.7 copy-start.11
  23.6 22.7 %all-to-all-start = ((f32[16,128,128]{2,1,0:T(8,128)}), f32[16,128,128]{2,1,0:T(8,128)S(1)}, u32[]{:S(2)}, u32[]{:S(2)}) async-start(f32[16,128,128]{2,1,0:T(8,128)} %get-tuple-element.7), calls=%async_computation | async-start | bytes 2097152 | tf_op jit(solution)/shard_map/all_to_all | solution.py:126
  75.1 12.1 %all-to-all-start.2 = ((f32[16,8,128]{2,1,0:T(8,128)}), f32[16,8,128]{2,1,0:T(8,128)S(1)}, u32[]{:S(2)}, u32[]{:S(2)}) async-start(f32[16,8,128]{2,1,0:T(8,128)} %shard_map.115), calls=%async_computation.2 | async-start | bytes 131072 | tf_op jit(solution)/shard_map/all_to_all | solution.py:126
  87.2 31.0 %copy-start.15 = (f32[512]{0:T(512)S(1)}, f32[512]{0:T(512)}, u32[]{:S(2)}) copy-start(f32[512]{0:T(512)} %param.13) | copy-start | bytes 6148
  88.9 43.1 %copy-start.3 = (bf16[512,512]{1,0:T(8,128)(2,1)S(1)}, bf16[512,512]{1,0:T(8,128)(2,1)}, u32[]{:S(2)}) copy-start(bf16[512,512]{1,0:T(8,128)(2,1)} %inverse.5) | copy-start | bytes 1572868
  88.9 43.1 %copy-start.9 = (f32[512,128]{1,0:T(8,128)S(1)}, f32[512,128]{1,0:T(8,128)}, u32[]{:S(2)}) copy-start(f32[512,128]{1,0:T(8,128)} %load.3) | copy-start | bytes 786436
  110.1 1.0 copy-start.6
  111.1 20.9 %all-to-all-start.4 = ((f32[16,128,128]{2,1,0:T(8,128)}), f32[16,128,128]{2,1,0:T(8,128)S(1)}, u32[]{:S(2)}, u32[]{:S(2)}) async-start(f32[16,128,128]{2,1,0:T(8,128)} %copy-done.6), calls=%async_computation.4 | async-start | bytes 2097152 | tf_op jit(solution)/shard_map/all_to_all | solution.py:126
  132.0 1.0 copy-start.10
  133.1 0.9 copy-start.12
  138.4 1.0 copy-start.7
  139.3 19.4 %all-to-all-start.5 = ((f32[16,128,128]{2,1,0:T(8,128)}), f32[16,128,128]{2,1,0:T(8,128)S(1)}, u32[]{:S(2)}, u32[]{:S(2)}) async-start(f32[16,128,128]{2,1,0:T(8,128)} %copy-done.7), calls=%async_computation.5 | async-start | bytes 2097152 | tf_op jit(solution)/shard_map/all_to_all | solution.py:126
  188.2 34.1 %copy-start.1 = (bf16[512,2048]{1,0:T(8,128)(2,1)S(1)}, bf16[512,2048]{1,0:T(8,128)(2,1)}, u32[]{:S(2)}) copy-start(bf16[512,2048]{1,0:T(8,128)(2,1)} %copy-done) | copy-start | bytes 6291460
  204.0 1.0 copy-start.5
  205.0 17.3 %all-to-all-start.9 = ((f32[16,128,128]{2,1,0:T(8,128)}), f32[16,128,128]{2,1,0:T(8,128)}, u32[]{:S(2)}, u32[]{:S(2)}) async-start(f32[16,128,128]{2,1,0:T(8,128)} %copy-done.5), calls=%async_computation.9 | async-start | bytes 2097152 | tf_op jit(solution)/shard_map/all_to_all | solution.py:126
  222.3 1.0 copy-start.4
Sparse Core Ops, SparseCore 0:
  10.1 75.4 all-gather.3

commit v2 on v1

v2 whole, which is shorter than its diff:
```python
import jax
import jax.numpy as jnp
from jax import lax
from jax.experimental import pallas as pl
from jax.experimental.pallas import tpu as pltpu
from jax.sharding import Mesh, PartitionSpec as P

BLOCK = 128
NX, NY, NZ, NC = 4, 4, 16, 2
NXY = NX * NY
OWN = 4
TILE = 512
START_MIB = 24
MIDDLE_MIB = 14
F32 = jnp.float32
BF16 = jnp.bfloat16
HIGHEST = lax.Precision.HIGHEST
MIB = 1024 * 1024
HBM = pl.BlockSpec(memory_space=pltpu.HBM)
SMEM = pl.BlockSpec(memory_space=pltpu.SMEM)
VMEM = pl.BlockSpec(memory_space=pltpu.VMEM)
DMA = pltpu.SemaphoreType.DMA


def dot(left, right):
    return jnp.dot(left, right, preferred_element_type=F32)


def f32(*shape):
    return jax.ShapeDtypeStruct(shape, F32)


def far(shape, dtype=F32):
    return pltpu.HBM(shape, dtype)


def call(kernel, out_shape, out_specs, in_specs, scratch, limit, *args):
    args = [pltpu.with_memory_space_constraint(x, pltpu.HBM) if spec is HBM else x for spec, x in zip(in_specs, args)]
    return pl.pallas_call(
        kernel,
        out_shape=out_shape,
        out_specs=out_specs,
        in_specs=in_specs,
        scratch_shapes=scratch,
        compiler_params=pltpu.CompilerParams(vmem_limit_bytes=limit * MIB),
    )(*args)


def fetch(sources, targets, sems):
    copies = [pltpu.make_async_copy(s, t, sems.at[i]) for i, (s, t) in enumerate(zip(sources, targets))]
    for copy in copies:
        copy.start()
    return copies


def send_tile(part, tile, scratch, contrib, sems):
    count = part.shape[1] // BLOCK
    first = tile * count
    for i in range(count):
        scratch[first + i] = part[:, i * BLOCK : (i + 1) * BLOCK]
    rows = pl.ds(first, count)
    copy = pltpu.make_async_copy(scratch.at[rows], contrib.at[rows], sems.at[tile])
    copy.start()
    return copy


def start_kernel(
    mask_in, inverse_in, load_in, owner_in, coupling_in, columns_out, solved_out, contrib,
    mask, inverse, load, owner, coupling, columns, solved, part_buf, in_sems, out_sems, part_sems,
):
    waits = fetch(
        (mask_in, inverse_in, load_in, owner_in, coupling_in), (mask, inverse, load, owner, coupling), in_sems
    )
    for wait in waits[:3]:
        wait.wait()
    solved[...] = dot(inverse[...], load[...].astype(BF16))
    copies = [pltpu.make_async_copy(solved, solved_out, out_sems.at[0])]
    copies[0].start()
    mixed_t = solved[...].T.astype(BF16)
    for wait in waits[3:]:
        wait.wait()
    for i in range(coupling.shape[1] // BLOCK):
        cols = slice(i * BLOCK, (i + 1) * BLOCK)
        coupling[:, cols] = jnp.where(mask[0, i] != 0, coupling[:, cols], jnp.zeros((), BF16))
    for tile in range(coupling.shape[1] // TILE):
        cols = pl.ds(tile * TILE, TILE)
        rows = lax.broadcasted_iota(jnp.int32, (coupling.shape[1], TILE), 0)
        pick = (rows == owner[:, cols]).astype(BF16)
        picked = dot(coupling[...], pick).astype(BF16)
        columns[:, cols] = picked
        copy = pltpu.make_async_copy(columns.at[:, cols], columns_out.at[:, cols], out_sems.at[1 + tile])
        copy.start()
        copies.append(copy)
        copies.append(send_tile(dot(mixed_t, picked), tile, part_buf, contrib, part_sems))
    for copy in copies:
        copy.wait()


def start(mask, inverse, coupling, load, owner):
    width, sep_width = coupling.shape
    cases = load.shape[1]
    tiles = sep_width // TILE
    return call(
        start_kernel,
        [far((width, sep_width), BF16), far((width, cases)), far((NXY, cases, BLOCK))],
        [HBM, HBM, HBM],
        [HBM] * 5,
        [
            pltpu.SMEM(mask.shape, jnp.int32),
            pltpu.VMEM(inverse.shape, BF16),
            pltpu.VMEM(load.shape, F32),
            pltpu.VMEM(owner.shape, jnp.int32),
            pltpu.VMEM(coupling.shape, BF16),
            pltpu.VMEM(coupling.shape, BF16),
            pltpu.VMEM(load.shape, F32),
            pltpu.VMEM((NXY, cases, BLOCK), F32),
            DMA((5,)),
            DMA((1 + tiles,)),
            DMA((tiles,)),
        ],
        START_MIB,
        mask, inverse, load, owner, coupling,
    )


def pack_sum_kernel(parts, local_t, packed, out, buf, sem):
    group = parts.shape[1] // NZ
    total = local_t[...] - jnp.sum(parts[...], axis=0)
    for z in range(NZ):
        buf[z, :group] = total[z * group : (z + 1) * group]
        buf[z, group:] = packed[...]
    copy = pltpu.make_async_copy(buf, out, sem)
    copy.start()
    copy.wait()


def sum_rows_kernel(parts, local_t, out):
    total = local_t[...] - jnp.sum(parts[...], axis=0)
    out[...] = total.reshape(out.shape)


def sum_cases_kernel(parts, out):
    total = jnp.sum(parts[:, : out.shape[1]], axis=0)
    out[...] = jnp.broadcast_to(total[None], out.shape)


def delta_kernel(core, rhs, mine, other, out):
    group, sub = rhs.shape[1], OWN
    acc_mine = jnp.zeros((2 * group, BLOCK), F32)
    acc_other = jnp.zeros((2 * group, BLOCK), F32)
    for i in range(NXY // 2):
        left = rhs[2 * i : 2 * i + 2].reshape(2 * group, BLOCK)
        rows = slice(group + 2 * sub * i, group + 2 * sub * (i + 1))
        acc_mine = acc_mine + rows_dot(left, mine[:, rows].reshape(BLOCK, BLOCK))
        acc_other = acc_other + rows_dot(left, other[:, rows].reshape(BLOCK, BLOCK))
    low = lax.broadcasted_iota(jnp.int32, (group, BLOCK), 1) % (2 * sub) < sub

    def pair(acc):
        return jnp.where(low, acc[:group] + pltpu.roll(acc[group:], BLOCK - sub, 1), 0.0)

    own, far = pair(acc_mine), pair(acc_other)
    first = core[0] == 0
    total = jnp.where(first, own, far) + pltpu.roll(jnp.where(first, far, own), sub, 1)
    out[...] = jnp.broadcast_to(total[None], out.shape)


def rows_dot(left, rows):
    return lax.dot_general(
        left, rows, (((1,), (1,)), ((), ())), precision=HIGHEST, preferred_element_type=F32
    )


def spread_kernel(parts, out, buf, sems):
    buf[...] = parts[...].reshape(buf.shape[1], BLOCK).T
    copies = [pltpu.make_async_copy(buf, out.at[i], sems.at[i]) for i in range(NXY)]
    for copy in copies:
        copy.start()
    for copy in copies:
        copy.wait()


def coupled_product(columns_in, columns, delta, sems):
    width, sep_width = columns.shape
    total = jnp.zeros((width, delta.shape[1]), F32)
    for tile in range(sep_width // TILE):
        cols = pl.ds(tile * TILE, TILE)
        pltpu.make_async_copy(columns_in.at[:, cols], columns.at[:, cols], sems.at[tile]).wait()
        total = total + dot(columns[:, cols], delta[cols, :].astype(BF16))
    return total


def fetch_columns(columns_in, columns, sems):
    for tile in range(columns.shape[1] // TILE):
        cols = pl.ds(tile * TILE, TILE)
        pltpu.make_async_copy(columns_in.at[:, cols], columns.at[:, cols], sems.at[tile]).start()


def middle_kernel(
    delta, cubic, columns_in, inverse_in, solved_in, matrix_in, load_in, state_out, contrib,
    columns, inverse, solved, matrix, load, mixed, part_buf, col_sems, in_sems, out_sem, part_sems,
):
    fetch_columns(columns_in, columns, col_sems)
    waits = fetch((inverse_in, solved_in, matrix_in, load_in), (inverse, solved, matrix, load), in_sems)
    coupled = coupled_product(columns_in, columns, delta, col_sems)
    waits[0].wait()
    waits[1].wait()
    state = solved[...] - dot(inverse[...], coupled.astype(BF16))
    waits[2].wait()
    waits[3].wait()
    resid = load[...] - dot(matrix[...], state.astype(BF16)) - coupled
    resid = resid - cubic[...] * state * state * state
    mixed[...] = state + dot(inverse[...], resid.astype(BF16))
    copies = [pltpu.make_async_copy(mixed, state_out, out_sem)]
    copies[0].start()
    mixed_t = mixed[...].T.astype(BF16)
    for tile in range(columns.shape[1] // TILE):
        part = dot(mixed_t, columns[:, tile * TILE : (tile + 1) * TILE])
        copies.append(send_tile(part, tile, part_buf, contrib, part_sems))
    for copy in copies:
        copy.wait()


def end_kernel(delta, columns_in, inverse_in, mixed_in, out, columns, inverse, mixed, state, col_sems, in_sems, out_sems):
    fetch_columns(columns_in, columns, col_sems)
    waits = fetch((inverse_in, mixed_in), (inverse, mixed), in_sems)
    back = coupled_product(columns_in, columns, delta, col_sems).astype(BF16)
    for wait in waits:
        wait.wait()
    count = out_sems.shape[0]
    rows = state.shape[0] // count
    copies = []
    for i in range(count):
        part = pl.ds(i * rows, rows)
        state[part, :] = mixed[part, :] - dot(inverse[part, :], back)
        copy = pltpu.make_async_copy(state.at[part], out.at[part], out_sems.at[i])
        copy.start()
        copies.append(copy)
    for copy in copies:
        copy.wait()


def exchange(parts, axes):
    return lax.all_to_all(parts, axes, 0, 0, tiled=True)


def correction(contrib, local, place, core, packed, rows):
    cases = contrib.shape[1]
    group = cases // NZ
    local_t = lax.dynamic_update_slice_in_dim(jnp.zeros((BLOCK, cases), F32), local, place, 0).T
    parts = exchange(contrib, ("x", "y"))
    if rows is None:
        sent = (NZ, group + packed.shape[0], BLOCK)
        parts = call(
            pack_sum_kernel, far(sent), HBM, [VMEM] * 3, [pltpu.VMEM(sent, F32), DMA], 8, parts, local_t, packed
        )
        parts = exchange(parts, "z")
        rows = (parts, lax.ppermute(parts, "c", [(0, 1), (1, 0)]))
    else:
        parts = call(sum_rows_kernel, f32(NZ, group, BLOCK), VMEM, [VMEM] * 2, [], 8, parts, local_t)
        parts = exchange(parts, "z")
    rhs = call(sum_cases_kernel, f32(NXY, group, BLOCK), VMEM, [VMEM], [], 4, parts)
    rhs = exchange(rhs, ("x", "y"))
    delta = call(delta_kernel, f32(NZ, group, BLOCK), VMEM, [SMEM] + [VMEM] * 3, [], 8, core, rhs, *rows)
    delta = exchange(delta, "z")
    delta = call(
        spread_kernel,
        far((NXY, BLOCK, cases)),
        HBM,
        [VMEM],
        [pltpu.VMEM((BLOCK, cases), F32), DMA((NXY,))],
        4,
        delta,
    )
    return exchange(delta, ("x", "y")).reshape(NXY * BLOCK, cases), rows


def on_device(
    leaf_matrix,
    leaf_inverse,
    coupling,
    cubic_coeff,
    leaf_load,
    sep_load,
    sep_matrix,
    sep_inverse,
    owner_map,
    block_mask,
):
    owned, cases = sep_load.shape
    width, sep_width = coupling.shape
    matrix_rows = lax.all_gather(sep_matrix, "c", axis=0, tiled=True)
    packed = sep_inverse.reshape(OWN, NXY, BLOCK).transpose(1, 0, 2).reshape(OWN * NXY, BLOCK)
    core = lax.axis_index("c").astype(jnp.int32)[None]
    place = lax.axis_index("z") * owned
    first_row = lax.axis_index(("x", "y", "z")) * owned
    columns, solved, contrib = start(block_mask, leaf_inverse, coupling, leaf_load, owner_map[None, :])

    delta, rows = correction(contrib, sep_load, place, core, packed, None)
    local = sep_load - jnp.dot(matrix_rows, delta, precision=HIGHEST, preferred_element_type=F32)
    sep_rows = lax.dynamic_slice_in_dim(delta, first_row, owned, 0)
    tiles = sep_width // TILE
    mixed, contrib = call(
        middle_kernel,
        [far((width, cases)), far((NXY, cases, BLOCK))],
        [HBM, HBM],
        [VMEM, VMEM] + [HBM] * 5,
        [
            pltpu.VMEM(columns.shape, BF16),
            pltpu.VMEM(leaf_inverse.shape, BF16),
            pltpu.VMEM(solved.shape, F32),
            pltpu.VMEM(leaf_matrix.shape, BF16),
            pltpu.VMEM(leaf_load.shape, F32),
            pltpu.VMEM(solved.shape, F32),
            pltpu.VMEM((NXY, cases, BLOCK), F32),
            DMA((tiles,)),
            DMA((4,)),
            DMA,
            DMA((tiles,)),
        ],
        MIDDLE_MIB,
        delta, cubic_coeff[:, None], columns, leaf_inverse, solved, leaf_matrix, leaf_load,
    )
    delta, rows = correction(contrib, local, place, core, packed, rows)
    leaf_state = call(
        end_kernel,
        far((width, cases)),
        HBM,
        [VMEM] + [HBM] * 3,
        [
            pltpu.VMEM(columns.shape, BF16),
            pltpu.VMEM(leaf_inverse.shape, BF16),
            pltpu.VMEM(mixed.shape, F32),
            pltpu.VMEM(mixed.shape, F32),
            DMA((tiles,)),
            DMA((2,)),
            DMA((2,)),
        ],
        MIDDLE_MIB,
        delta, columns, leaf_inverse, mixed,
    )
    sep_rows = sep_rows + lax.dynamic_slice_in_dim(delta, first_row, owned, 0)
    return leaf_state, sep_rows


def solution(mesh):
    grid = Mesh(mesh.devices.reshape(NX, NY, NZ, NC), ("x", "y", "z", "c"))
    leaf = ("x", "y", "z")
    in_specs = (
        P(leaf, None),
        P(leaf, None),
        P(leaf, None),
        P(leaf),
        P(leaf, "c"),
        P(leaf, "c"),
        P(leaf + ("c",), None),
        P(leaf + ("c",), None),
        P(),
        P(leaf, None),
    )
    out_specs = (P(leaf, "c"), P(leaf, "c"))
    return jax.shard_map(on_device, mesh=grid, in_specs=in_specs, out_specs=out_specs, check_vma=False)
```

time: 236 us -> 226 us (0.958)
  blocking collectives: 94.5 us -> 109 us
  between operations: 14.2 us -> 0.78 us
  local copies, waits for them, and re-layouts: 14.1 us -> 1.12 us
  Pallas kernels: 22.2 us -> 24.7 us
    all_to_all x5, blocking collectives: 92.4 us -> 107 us  [exchange(): return lax.all_to_all(parts, axes, 0, 0, tiled=True)]
    unnamed x37 -> x10, local copies, waits for them, and re-layouts: 13.1 us -> 0.14 us
    all_to_all x5, waiting for transfers between devices: 45.7 us -> 51.9 us  [exchange(): return lax.all_to_all(parts, axes, 0, 0, tiled=True)]
    all_gather x1 -> x0, waiting for transfers between devices: 4.59 us -> none  [on_device(): inverse_rows = lax.all_gather(sep_inverse, ('z', 'c'), axis=0, tiled=True)]
    pallas_call x11, Pallas kernels: 22.2 us -> 24.7 us  [call(): pl.pallas_call(kernel, out_shape=out_shape, out_specs=out_specs, in_specs...]
  transfers between devices with their start and end apart: 6 -> 6, of which waited for: 5 -> 5; matrix products, arithmetic and copies ran while one was open for 3% -> 1% of each run, Pallas kernels for 5% -> 0%
where the time goes in v2:
time: 226 us; the launch traced here: 224 us
  blocking collectives  109 us (48%)
  waiting for transfers between devices  51.9 us (23%)
  starting transfers between devices  34.2 us (15%)
  Pallas kernels  24.7 us (11%)
    all_to_all x5, blocking collectives, exchange(): return lax.all_to_all(parts, axes, 0, 0, tiled=True)  107 us
    all_to_all x5, waiting for transfers between devices, exchange(): return lax.all_to_all(parts, axes, 0, 0, tiled=True)  51.9 us
    all_to_all x5, starting transfers between devices, exchange(): return lax.all_to_all(parts, axes, 0, 0, tiled=True)  32.3 us
    pallas_call x11, Pallas kernels, call(): pl.pallas_call(kernel, out_shape=out_shape, out_specs=out_specs, in_specs...  24.7 us
  transfers between devices with their start and end apart: 6, of which 5 were waited for; matrix products, arithmetic and copies ran while one was open for 1% of the time, Pallas kernels for 0%

profile of v2, /device:TPU:6, one launch (start us, length us, event | category | flops | bytes accessed | tf_op | source)
XLA Modules:
  0.0 224.1 jit_solution(13662798269445968008)
XLA Ops:
  0.7 8.1 %shard_map.113 = (bf16[512,2048]{1,0:T(8,128)(2,1)}, f32[512,128]{1,0:T(8,128)}, f32[16,128,128]{2,1,0:T(8,128)}) custom-call(s32[1,16]{1,0:T(1,128)} %mask_in.1, bf16[512,512]{1,0:T(8,128)(2,1)} %inverse_in.5, f32[512,128]{1,0:T(8,128)} %load_in.3, s32[1,2048]{1,0:T(1,128)} %bitcast.28, bf16[512,2048]{1,0:T(8,128)(2,1)} %coupling_in.1), custom_call_target="tpu_custom_call" | custom-call | tf_op jit(solution)/shard_map/pallas_call | solution.py:39
  8.8 9.4 %all-to-all-start = ((f32[16,128,128]{2,1,0:T(8,128)}), f32[16,128,128]{2,1,0:T(8,128)S(1)}, u32[]{:S(2)}, u32[]{:S(2)}) async-start(f32[16,128,128]{2,1,0:T(8,128)} %get-tuple-element.7), calls=%async_computation | async-start | bytes 2097152 | tf_op jit(solution)/shard_map/all_to_all | solution.py:243
  18.7 12.8 %all-to-all-done.parts = f32[16,128,128]{2,1,0:T(8,128)S(1)} async-done(((f32[16,128,128]{2,1,0:T(8,128)}), f32[16,128,128]{2,1,0:T(8,128)S(1)}, u32[]{:S(2)}, u32[]{:S(2)}) %all-to-all-start) | async-done | bytes 1048608 | tf_op jit(solution)/shard_map/all_to_all | solution.py:243
  32.3 48.7 %all_to_all.50.parts.mine = f32[16,72,128]{2,1,0:T(8,128)S(1)} all-to-all(f32[16,72,128]{2,1,0:T(8,128)} %shard_map.114), channel_id=1, replica_groups=mesh['x'=4,'y'=4,'z'=16,'c'=2] {'z'}, dimensions={0} | all-to-all | bytes 1179648 | tf_op jit(solution)/shard_map/all_to_all | solution.py:243
  81.0 1.9 collective-permute-start
  83.5 5.9 %all-to-all-start.2 = ((f32[16,8,128]{2,1,0:T(8,128)}), f32[16,8,128]{2,1,0:T(8,128)S(1)}, u32[]{:S(2)}, u32[]{:S(2)}) async-start(f32[16,8,128]{2,1,0:T(8,128)} %shard_map.115), calls=%async_computation.2 | async-start | bytes 131072 | tf_op jit(solution)/shard_map/all_to_all | solution.py:243
  89.5 5.6 %all-to-all-done.2.rhs = f32[16,8,128]{2,1,0:T(8,128)S(1)} async-done(((f32[16,8,128]{2,1,0:T(8,128)}), f32[16,8,128]{2,1,0:T(8,128)S(1)}, u32[]{:S(2)}, u32[]{:S(2)}) %all-to-all-start.2) | async-done | bytes 65568 | tf_op jit(solution)/shard_map/all_to_all | solution.py:243
  95.1 1.9 shard_map.116
  97.0 15.8 %all_to_all.51.parts = f32[16,8,128]{2,1,0:T(8,128)S(1)} all-to-all(f32[16,8,128]{2,1,0:T(8,128)S(1)} %shard_map.116), channel_id=1, replica_groups=mesh['x'=4,'y'=4,'z'=16,'c'=2] {'z'}, dimensions={0} | all-to-all | bytes 131072 | tf_op jit(solution)/shard_map/all_to_all | solution.py:243
  112.8 1.2 shard_map.117
  114.0 5.6 %all-to-all-start.4 = ((f32[16,128,128]{2,1,0:T(8,128)}), f32[16,128,128]{2,1,0:T(8,128)S(1)}, u32[]{:S(2)}, u32[]{:S(2)}) async-start(f32[16,128,128]{2,1,0:T(8,128)} %shard_map.117), calls=%async_computation.4 | async-start | bytes 2097152 | tf_op jit(solution)/shard_map/all_to_all | solution.py:243
  119.8 12.9 %all-to-all-done.4 = f32[16,128,128]{2,1,0:T(8,128)S(1)} async-done(((f32[16,128,128]{2,1,0:T(8,128)}), f32[16,128,128]{2,1,0:T(8,128)S(1)}, u32[]{:S(2)}, u32[]{:S(2)}) %all-to-all-start.4) | async-done | bytes 1048608 | tf_op jit(solution)/shard_map/all_to_all | solution.py:243
  132.7 5.3 %shard_map.118 = (f32[512,128]{1,0:T(8,128)}, f32[16,128,128]{2,1,0:T(8,128)}) custom-call(f32[2048,128]{1,0:T(8,128)S(1)} %bitcast.19, f32[512,1]{1,0:T(8,128)S(1)} %copy.23.cubic, bf16[512,2048]{1,0:T(8,128)(2,1)} %get-tuple-element.8.columns_in, bf16[512,512]{1,0:T(8,128)(2,1)} %inverse_in.5, f32[512,128]{1,0:T(8,128)} %get-tuple-element.9.solved_in, ...), custom_call_target="tpu_custom_call" | custom-call | tf_op jit(solution)/shard_map/pallas_call | solution.py:39
  138.0 5.7 %all-to-all-start.5 = ((f32[16,128,128]{2,1,0:T(8,128)}), f32[16,128,128]{2,1,0:T(8,128)S(1)}, u32[]{:S(2)}, u32[]{:S(2)}) async-start(f32[16,128,128]{2,1,0:T(8,128)} %get-tuple-element.10), calls=%async_computation.5 | async-start | bytes 2097152 | tf_op jit(solution)/shard_map/all_to_all | solution.py:243
  143.7 1.9 all-gather
  145.5 1.8 fusion
  147.8 9.6 %all-to-all-done.5.parts = f32[16,128,128]{2,1,0:T(8,128)S(1)} async-done(((f32[16,128,128]{2,1,0:T(8,128)}), f32[16,128,128]{2,1,0:T(8,128)S(1)}, u32[]{:S(2)}, u32[]{:S(2)}) %all-to-all-start.5) | async-done | bytes 1048608 | tf_op jit(solution)/shard_map/all_to_all | solution.py:243
  157.4 16.3 %all_to_all.52.parts = f32[16,8,128]{2,1,0:T(8,128)S(1)} all-to-all(f32[16,8,128]{2,1,0:T(8,128)S(1)} %shard_map.119), channel_id=1, replica_groups=mesh['x'=4,'y'=4,'z'=16,'c'=2] {'z'}, dimensions={0} | all-to-all | bytes 131072 | tf_op jit(solution)/shard_map/all_to_all | solution.py:243
  173.7 10.9 %all_to_all.53.rhs = f32[16,8,128]{2,1,0:T(8,128)S(1)} all-to-all(f32[16,8,128]{2,1,0:T(8,128)S(1)} %shard_map.120), channel_id=1, replica_groups=mesh['x'=4,'y'=4,'z'=16,'c'=2] {'x','y'}, dimensions={0} | all-to-all | bytes 131072 | tf_op jit(solution)/shard_map/all_to_all | solution.py:243
  184.6 1.9 shard_map.121
  186.5 15.5 %all_to_all.54.parts = f32[16,8,128]{2,1,0:T(8,128)S(1)} all-to-all(f32[16,8,128]{2,1,0:T(8,128)S(1)} %shard_map.121), channel_id=1, replica_groups=mesh['x'=4,'y'=4,'z'=16,'c'=2] {'z'}, dimensions={0} | all-to-all | bytes 131072 | tf_op jit(solution)/shard_map/all_to_all | solution.py:243
  203.2 5.6 %all-to-all-start.9 = ((f32[16,128,128]{2,1,0:T(8,128)}), f32[16,128,128]{2,1,0:T(8,128)S(1)}, u32[]{:S(2)}, u32[]{:S(2)}) async-start(f32[16,128,128]{2,1,0:T(8,128)} %shard_map.122), calls=%async_computation.9 | async-start | bytes 2097152 | tf_op jit(solution)/shard_map/all_to_all | solution.py:243
  208.9 11.0 %all-to-all-done.9 = f32[16,128,128]{2,1,0:T(8,128)S(1)} async-done(((f32[16,128,128]{2,1,0:T(8,128)}), f32[16,128,128]{2,1,0:T(8,128)S(1)}, u32[]{:S(2)}, u32[]{:S(2)}) %all-to-all-start.9) | async-done | bytes 1048608 | tf_op jit(solution)/shard_map/all_to_all | solution.py:243
  219.8 3.6 %shard_map.123 = f32[512,128]{1,0:T(8,128)} custom-call(f32[2048,128]{1,0:T(8,128)S(1)} %bitcast.22, bf16[512,2048]{1,0:T(8,128)(2,1)} %get-tuple-element.8.columns_in, bf16[512,512]{1,0:T(8,128)(2,1)} %inverse_in.5, f32[512,128]{1,0:T(8,128)} %get-tuple-element.11.mixed_in), custom_call_target="tpu_custom_call" | custom-call | tf_op jit(solution)/shard_map/pallas_call | solution.py:39
  (22 shorter events, 4.5 us)
Async XLA Ops:
  0.6 17.5 %copy-start.2 = (f32[8,128]{1,0:T(8,128)S(1)}, f32[8,128]{1,0:T(8,128)}, u32[]{:S(2)}) copy-start(f32[8,128]{1,0:T(8,128)} %param.15) | copy-start | bytes 12292
  0.6 30.8 %copy-start = (f32[4,2048]{1,0:T(4,128)S(1)}, f32[4,2048]{1,0:T(4,128)}, u32[]{:S(2)}) copy-start(f32[4,2048]{1,0:T(4,128)} %param.17) | copy-start | bytes 98308
  8.8 22.7 %all-to-all-start = ((f32[16,128,128]{2,1,0:T(8,128)}), f32[16,128,128]{2,1,0:T(8,128)S(1)}, u32[]{:S(2)}, u32[]{:S(2)}) async-start(f32[16,128,128]{2,1,0:T(8,128)} %get-tuple-element.7), calls=%async_computation | async-start | bytes 2097152 | tf_op jit(solution)/shard_map/all_to_all | solution.py:243
  81.0 14.1 %collective-permute-start = (f32[16,72,128]{2,1,0:T(8,128)S(1)}, f32[16,72,128]{2,1,0:T(8,128)S(1)}, u32[]{:S(2)}, u32[]{:S(2)}) collective-permute-start(f32[16,72,128]{2,1,0:T(8,128)S(1)} %all_to_all.50.parts.mine), channel_id=1, source_target_pairs={{0,1},{1,0},{2,3},{3,2},{4,5},{5,4},{6,7},{7,6},{8,9},{9,8},{10,11... | collective-permute-start | bytes 1769480 | tf_op jit(solution)/shard_map/ppermute | solution.py:257
  83.5 11.6 %all-to-all-start.2 = ((f32[16,8,128]{2,1,0:T(8,128)}), f32[16,8,128]{2,1,0:T(8,128)S(1)}, u32[]{:S(2)}, u32[]{:S(2)}) async-start(f32[16,8,128]{2,1,0:T(8,128)} %shard_map.115), calls=%async_computation.2 | async-start | bytes 131072 | tf_op jit(solution)/shard_map/all_to_all | solution.py:243
  95.1 24.5 %copy-start.3 = (f32[512]{0:T(512)S(1)}, f32[512]{0:T(512)}, u32[]{:S(2)}) copy-start(f32[512]{0:T(512)} %param.13) | copy-start | bytes 6148
  114.0 18.7 %all-to-all-start.4 = ((f32[16,128,128]{2,1,0:T(8,128)}), f32[16,128,128]{2,1,0:T(8,128)S(1)}, u32[]{:S(2)}, u32[]{:S(2)}) async-start(f32[16,128,128]{2,1,0:T(8,128)} %shard_map.117), calls=%async_computation.4 | async-start | bytes 2097152 | tf_op jit(solution)/shard_map/all_to_all | solution.py:243
  138.0 5.7 %copy-start.1 = (f32[4,2048]{1,0:T(4,128)S(1)}, f32[4,2048]{1,0:T(4,128)}, u32[]{:S(2)}) copy-start(f32[4,2048]{1,0:T(4,128)} %param.16) | copy-start | bytes 98308
  138.0 19.4 %all-to-all-start.5 = ((f32[16,128,128]{2,1,0:T(8,128)}), f32[16,128,128]{2,1,0:T(8,128)S(1)}, u32[]{:S(2)}, u32[]{:S(2)}) async-start(f32[16,128,128]{2,1,0:T(8,128)} %get-tuple-element.10), calls=%async_computation.5 | async-start | bytes 2097152 | tf_op jit(solution)/shard_map/all_to_all | solution.py:243
  203.2 16.6 %all-to-all-start.9 = ((f32[16,128,128]{2,1,0:T(8,128)}), f32[16,128,128]{2,1,0:T(8,128)S(1)}, u32[]{:S(2)}, u32[]{:S(2)}) async-start(f32[16,128,128]{2,1,0:T(8,128)} %shard_map.122), calls=%async_computation.9 | async-start | bytes 2097152 | tf_op jit(solution)/shard_map/all_to_all | solution.py:243

commit v3 on v2

--- a/solution.py
+++ b/solution.py
@@ -9,6 +9,8 @@
 NX, NY, NZ, NC = 4, 4, 16, 2
 NXY = NX * NY
 OWN = 4
+SPLIT = 2
+PART = OWN // SPLIT
 TILE = 512
 START_MIB = 24
 MIDDLE_MIB = 14
@@ -123,12 +125,18 @@
     )
 
 
+def case_group(total, z):
+    group = total.shape[0] * SPLIT // NZ
+    first = z // SPLIT * group
+    return total[first : first + group]
+
+
 def pack_sum_kernel(parts, local_t, packed, out, buf, sem):
-    group = parts.shape[1] // NZ
+    group = parts.shape[1] * SPLIT // NZ
     total = local_t[...] - jnp.sum(parts[...], axis=0)
     for z in range(NZ):
-        buf[z, :group] = total[z * group : (z + 1) * group]
-        buf[z, group:] = packed[...]
+        buf[z, :group] = case_group(total, z)
+        buf[z, group:] = packed[z % SPLIT]
     copy = pltpu.make_async_copy(buf, out, sem)
     copy.start()
     copy.wait()
@@ -136,7 +144,8 @@
 
 def sum_rows_kernel(parts, local_t, out):
     total = local_t[...] - jnp.sum(parts[...], axis=0)
-    out[...] = total.reshape(out.shape)
+    for z in range(NZ):
+        out[z] = case_group(total, z)
 
 
 def sum_cases_kernel(parts, out):
@@ -145,23 +154,30 @@
 
 
 def delta_kernel(core, rhs, mine, other, out):
-    group, sub = rhs.shape[1], OWN
-    acc_mine = jnp.zeros((2 * group, BLOCK), F32)
-    acc_other = jnp.zeros((2 * group, BLOCK), F32)
-    for i in range(NXY // 2):
-        left = rhs[2 * i : 2 * i + 2].reshape(2 * group, BLOCK)
-        rows = slice(group + 2 * sub * i, group + 2 * sub * (i + 1))
+    cases = rhs.shape[1]
+    span = BLOCK // (NZ * PART)
+    base = mine.shape[1] - NXY * PART
+    acc_mine = jnp.zeros((span * cases, BLOCK), F32)
+    acc_other = jnp.zeros((span * cases, BLOCK), F32)
+    for i in range(NXY // span):
+        left = rhs[span * i : span * (i + 1)].reshape(span * cases, BLOCK)
+        rows = slice(base + 8 * i, base + 8 * (i + 1))
         acc_mine = acc_mine + rows_dot(left, mine[:, rows].reshape(BLOCK, BLOCK))
         acc_other = acc_other + rows_dot(left, other[:, rows].reshape(BLOCK, BLOCK))
-    low = lax.broadcasted_iota(jnp.int32, (group, BLOCK), 1) % (2 * sub) < sub
-
-    def pair(acc):
-        return jnp.where(low, acc[:group] + pltpu.roll(acc[group:], BLOCK - sub, 1), 0.0)
-
-    own, far = pair(acc_mine), pair(acc_other)
+    low = lax.broadcasted_iota(jnp.int32, (cases, BLOCK), 1) % 8 < PART
+
+    def fold(acc):
+        total = acc[:cases]
+        for j in range(1, span):
+            total = total + pltpu.roll(acc[j * cases : (j + 1) * cases], BLOCK - PART * j, 1)
+        return jnp.where(low, total, 0.0)
+
+    own, far_rows = fold(acc_mine), fold(acc_other)
     first = core[0] == 0
-    total = jnp.where(first, own, far) + pltpu.roll(jnp.where(first, far, own), sub, 1)
-    out[...] = jnp.broadcast_to(total[None], out.shape)
+    total = jnp.where(first, own, far_rows) + pltpu.roll(jnp.where(first, far_rows, own), OWN, 1)
+    half = cases // SPLIT
+    tile = total[:half] + pltpu.roll(total[half:], PART, 1)
+    out[...] = jnp.broadcast_to(tile[None], out.shape)
 
 
 def rows_dot(left, rows):
@@ -170,8 +186,14 @@
     )
 
 
-def spread_kernel(parts, out, buf, sems):
-    buf[...] = parts[...].reshape(buf.shape[1], BLOCK).T
+def spread_kernel(parts, out, cases_buf, buf, sems):
+    half = parts.shape[1]
+    low = lax.broadcasted_iota(jnp.int32, (half, BLOCK), 1) % (2 * PART) < PART
+    for i in range(NZ // SPLIT):
+        even, odd = parts[SPLIT * i], parts[SPLIT * i + 1]
+        cases_buf[2 * half * i : 2 * half * i + half] = jnp.where(low, even, pltpu.roll(odd, PART, 1))
+        cases_buf[2 * half * i + half : 2 * half * (i + 1)] = jnp.where(low, pltpu.roll(even, BLOCK - PART, 1), odd)
+    buf[...] = cases_buf[...].T
     copies = [pltpu.make_async_copy(buf, out.at[i], sems.at[i]) for i in range(NXY)]
     for copy in copies:
         copy.start()
@@ -245,29 +267,33 @@
 
 def correction(contrib, local, place, core, packed, rows):
     cases = contrib.shape[1]
-    group = cases // NZ
+    group = cases * SPLIT // NZ
     local_t = lax.dynamic_update_slice_in_dim(jnp.zeros((BLOCK, cases), F32), local, place, 0).T
     parts = exchange(contrib, ("x", "y"))
-    if rows is None:
-        sent = (NZ, group + packed.shape[0], BLOCK)
+    first = rows is None
+    if first:
+        sent = (NZ, group + packed.shape[1], BLOCK)
         parts = call(
             pack_sum_kernel, far(sent), HBM, [VMEM] * 3, [pltpu.VMEM(sent, F32), DMA], 8, parts, local_t, packed
         )
-        parts = exchange(parts, "z")
-        rows = (parts, lax.ppermute(parts, "c", [(0, 1), (1, 0)]))
     else:
         parts = call(sum_rows_kernel, f32(NZ, group, BLOCK), VMEM, [VMEM] * 2, [], 8, parts, local_t)
-        parts = exchange(parts, "z")
+    parts = exchange(parts, "z")
     rhs = call(sum_cases_kernel, f32(NXY, group, BLOCK), VMEM, [VMEM], [], 4, parts)
+    if first:
+        parts, rhs = lax.optimization_barrier((parts, rhs))
+        rows = (parts, lax.ppermute(parts, "c", [(0, 1), (1, 0)]))
     rhs = exchange(rhs, ("x", "y"))
-    delta = call(delta_kernel, f32(NZ, group, BLOCK), VMEM, [SMEM] + [VMEM] * 3, [], 8, core, rhs, *rows)
+    delta = call(
+        delta_kernel, f32(NZ, group // SPLIT, BLOCK), VMEM, [SMEM] + [VMEM] * 3, [], 8, core, rhs, *rows
+    )
     delta = exchange(delta, "z")
     delta = call(
         spread_kernel,
         far((NXY, BLOCK, cases)),
         HBM,
         [VMEM],
-        [pltpu.VMEM((BLOCK, cases), F32), DMA((NXY,))],
+        [pltpu.VMEM((cases, BLOCK), F32), pltpu.VMEM((BLOCK, cases), F32), DMA((NXY,))],
         4,
         delta,
     )
@@ -289,7 +315,7 @@
     owned, cases = sep_load.shape
     width, sep_width = coupling.shape
     matrix_rows = lax.all_gather(sep_matrix, "c", axis=0, tiled=True)
-    packed = sep_inverse.reshape(OWN, NXY, BLOCK).transpose(1, 0, 2).reshape(OWN * NXY, BLOCK)
+    packed = sep_inverse.reshape(SPLIT, PART, NXY, BLOCK).transpose(0, 2, 1, 3).reshape(SPLIT, NXY * PART, BLOCK)
     core = lax.axis_index("c").astype(jnp.int32)[None]
     place = lax.axis_index("z") * owned
     first_row = lax.axis_index(("x", "y", "z")) * owned

time: 226 us -> 219 us (0.969)
  blocking collectives: 109 us -> 102 us
    all_to_all x5, blocking collectives: 107 us -> 100 us  [exchange(): return lax.all_to_all(parts, axes, 0, 0, tiled=True)]
where the time goes in v3:
time: 219 us; the launch traced here: 217 us
  blocking collectives  102 us (47%)
  waiting for transfers between devices  52 us (24%)
  starting transfers between devices  34.7 us (16%)
  Pallas kernels  23.7 us (11%)
    all_to_all x5, blocking collectives, exchange(): return lax.all_to_all(parts, axes, 0, 0, tiled=True)  100 us
    all_to_all x5, waiting for transfers between devices, exchange(): return lax.all_to_all(parts, axes, 0, 0, tiled=True)  52 us
    all_to_all x5, starting transfers between devices, exchange(): return lax.all_to_all(parts, axes, 0, 0, tiled=True)  32.8 us
    pallas_call x11, Pallas kernels, call(): pl.pallas_call(kernel, out_shape=out_shape, out_specs=out_specs, in_specs...  23.7 us
  transfers between devices with their start and end apart: 6, of which 5 were waited for; matrix products, arithmetic and copies ran while one was open for 1% of the time, Pallas kernels for 0%

profile of v3, /device:TPU:6, one launch (start us, length us, event | category | flops | bytes accessed | tf_op | source)
XLA Modules:
  0.0 216.8 jit_solution(8861550455946096037)
XLA Ops:
  0.7 8.1 %shard_map.113 = (bf16[512,2048]{1,0:T(8,128)(2,1)}, f32[512,128]{1,0:T(8,128)}, f32[16,128,128]{2,1,0:T(8,128)}) custom-call(s32[1,16]{1,0:T(1,128)} %mask_in.1, bf16[512,512]{1,0:T(8,128)(2,1)} %inverse_in.5, f32[512,128]{1,0:T(8,128)} %load_in.3, s32[1,2048]{1,0:T(1,128)} %bitcast.31, bf16[512,2048]{1,0:T(8,128)(2,1)} %coupling_in.1), custom_call_target="tpu_custom_call" | custom-call | tf_op jit(solution)/shard_map/pallas_call | solution.py:41
  8.8 9.4 %all-to-all-start = ((f32[16,128,128]{2,1,0:T(8,128)}), f32[16,128,128]{2,1,0:T(8,128)S(1)}, u32[]{:S(2)}, u32[]{:S(2)}) async-start(f32[16,128,128]{2,1,0:T(8,128)} %get-tuple-element.9), calls=%async_computation | async-start | bytes 2097152 | tf_op jit(solution)/shard_map/all_to_all | solution.py:265
  18.7 12.7 %all-to-all-done.parts = f32[16,128,128]{2,1,0:T(8,128)S(1)} async-done(((f32[16,128,128]{2,1,0:T(8,128)}), f32[16,128,128]{2,1,0:T(8,128)S(1)}, u32[]{:S(2)}, u32[]{:S(2)}) %all-to-all-start) | async-done | bytes 1048608 | tf_op jit(solution)/shard_map/all_to_all | solution.py:265
  32.3 36.9 %all_to_all.50.parts.mine = f32[16,48,128]{2,1,0:T(8,128)S(1)} all-to-all(f32[16,48,128]{2,1,0:T(8,128)} %shard_map.114), channel_id=1, replica_groups=mesh['x'=4,'y'=4,'z'=16,'c'=2] {'z'}, dimensions={0} | all-to-all | bytes 786432 | tf_op jit(solution)/shard_map/all_to_all | solution.py:265
  69.8 1.9 collective-permute-start
  71.7 6.4 %all-to-all-start.2 = ((f32[16,16,128]{2,1,0:T(8,128)}), f32[16,16,128]{2,1,0:T(8,128)S(1)}, u32[]{:S(2)}, u32[]{:S(2)}) async-start(f32[16,16,128]{2,1,0:T(8,128)} %shard_map.115), calls=%async_computation.2 | async-start | bytes 262144 | tf_op jit(solution)/shard_map/all_to_all | solution.py:265
  78.1 5.9 %all-to-all-done.2.rhs = f32[16,16,128]{2,1,0:T(8,128)S(1)} async-done(((f32[16,16,128]{2,1,0:T(8,128)}), f32[16,16,128]{2,1,0:T(8,128)S(1)}, u32[]{:S(2)}, u32[]{:S(2)}) %all-to-all-start.2) | async-done | bytes 131104 | tf_op jit(solution)/shard_map/all_to_all | solution.py:265
  84.0 1.3 shard_map.116
  85.3 18.7 %all_to_all.51.parts = f32[16,8,128]{2,1,0:T(8,128)S(1)} all-to-all(f32[16,8,128]{2,1,0:T(8,128)S(1)} %shard_map.116), channel_id=1, replica_groups=mesh['x'=4,'y'=4,'z'=16,'c'=2] {'z'}, dimensions={0} | all-to-all | bytes 131072 | tf_op jit(solution)/shard_map/all_to_all | solution.py:265
  103.9 1.3 shard_map.117
  105.2 5.7 %all-to-all-start.4 = ((f32[16,128,128]{2,1,0:T(8,128)}), f32[16,128,128]{2,1,0:T(8,128)S(1)}, u32[]{:S(2)}, u32[]{:S(2)}) async-start(f32[16,128,128]{2,1,0:T(8,128)} %shard_map.117), calls=%async_computation.4 | async-start | bytes 2097152 | tf_op jit(solution)/shard_map/all_to_all | solution.py:265
  111.1 12.9 %all-to-all-done.4 = f32[16,128,128]{2,1,0:T(8,128)S(1)} async-done(((f32[16,128,128]{2,1,0:T(8,128)}), f32[16,128,128]{2,1,0:T(8,128)S(1)}, u32[]{:S(2)}, u32[]{:S(2)}) %all-to-all-start.4) | async-done | bytes 1048608 | tf_op jit(solution)/shard_map/all_to_all | solution.py:265
  124.0 5.3 %shard_map.118 = (f32[512,128]{1,0:T(8,128)}, f32[16,128,128]{2,1,0:T(8,128)}) custom-call(f32[2048,128]{1,0:T(8,128)S(1)} %bitcast.20, f32[512,1]{1,0:T(8,128)S(1)} %copy.23.cubic, bf16[512,2048]{1,0:T(8,128)(2,1)} %get-tuple-element.12.columns_in, bf16[512,512]{1,0:T(8,128)(2,1)} %inverse_in.5, f32[512,128]{1,0:T(8,128)} %get-tuple-element.13.solved_in, ...), custom_call_target="tpu_custom_call" | custom-call | tf_op jit(solution)/shard_map/pallas_call | solution.py:41
  129.3 5.7 %all-to-all-start.5 = ((f32[16,128,128]{2,1,0:T(8,128)}), f32[16,128,128]{2,1,0:T(8,128)S(1)}, u32[]{:S(2)}, u32[]{:S(2)}) async-start(f32[16,128,128]{2,1,0:T(8,128)} %get-tuple-element.14), calls=%async_computation.5 | async-start | bytes 2097152 | tf_op jit(solution)/shard_map/all_to_all | solution.py:265
  135.0 1.9 all-gather
  136.9 1.8 fusion
  139.1 9.3 %all-to-all-done.5.parts = f32[16,128,128]{2,1,0:T(8,128)S(1)} async-done(((f32[16,128,128]{2,1,0:T(8,128)}), f32[16,128,128]{2,1,0:T(8,128)S(1)}, u32[]{:S(2)}, u32[]{:S(2)}) %all-to-all-start.5) | async-done | bytes 1048608 | tf_op jit(solution)/shard_map/all_to_all | solution.py:265
  148.4 16.8 %all_to_all.52.parts = f32[16,16,128]{2,1,0:T(8,128)S(1)} all-to-all(f32[16,16,128]{2,1,0:T(8,128)S(1)} %shard_map.119), channel_id=1, replica_groups=mesh['x'=4,'y'=4,'z'=16,'c'=2] {'z'}, dimensions={0} | all-to-all | bytes 262144 | tf_op jit(solution)/shard_map/all_to_all | solution.py:265
  165.2 11.4 %all_to_all.53.rhs = f32[16,16,128]{2,1,0:T(8,128)S(1)} all-to-all(f32[16,16,128]{2,1,0:T(8,128)S(1)} %shard_map.120), channel_id=1, replica_groups=mesh['x'=4,'y'=4,'z'=16,'c'=2] {'x','y'}, dimensions={0} | all-to-all | bytes 262144 | tf_op jit(solution)/shard_map/all_to_all | solution.py:265
  176.7 1.3 shard_map.121
  178.0 16.5 %all_to_all.54.parts = f32[16,8,128]{2,1,0:T(8,128)S(1)} all-to-all(f32[16,8,128]{2,1,0:T(8,128)S(1)} %shard_map.121), channel_id=1, replica_groups=mesh['x'=4,'y'=4,'z'=16,'c'=2] {'z'}, dimensions={0} | all-to-all | bytes 131072 | tf_op jit(solution)/shard_map/all_to_all | solution.py:265
  195.7 5.6 %all-to-all-start.9 = ((f32[16,128,128]{2,1,0:T(8,128)}), f32[16,128,128]{2,1,0:T(8,128)S(1)}, u32[]{:S(2)}, u32[]{:S(2)}) async-start(f32[16,128,128]{2,1,0:T(8,128)} %shard_map.122), calls=%async_computation.9 | async-start | bytes 2097152 | tf_op jit(solution)/shard_map/all_to_all | solution.py:265
  201.3 11.3 %all-to-all-done.9 = f32[16,128,128]{2,1,0:T(8,128)S(1)} async-done(((f32[16,128,128]{2,1,0:T(8,128)}), f32[16,128,128]{2,1,0:T(8,128)S(1)}, u32[]{:S(2)}, u32[]{:S(2)}) %all-to-all-start.9) | async-done | bytes 1048608 | tf_op jit(solution)/shard_map/all_to_all | solution.py:265
  212.6 3.6 %shard_map.123 = f32[512,128]{1,0:T(8,128)} custom-call(f32[2048,128]{1,0:T(8,128)S(1)} %bitcast.23, bf16[512,2048]{1,0:T(8,128)(2,1)} %get-tuple-element.12.columns_in, bf16[512,512]{1,0:T(8,128)(2,1)} %inverse_in.5, f32[512,128]{1,0:T(8,128)} %get-tuple-element.15.mixed_in), custom_call_target="tpu_custom_call" | custom-call | tf_op jit(solution)/shard_map/pallas_call | solution.py:41
  (24 shorter events, 4.6 us)
Async XLA Ops:
  0.6 17.5 %copy-start.1 = (f32[4,2048]{1,0:T(4,128)S(1)}, f32[4,2048]{1,0:T(4,128)}, u32[]{:S(2)}) copy-start(f32[4,2048]{1,0:T(4,128)} %param.17) | copy-start | bytes 98308
  0.6 17.5 %copy-start.2 = (f32[8,128]{1,0:T(8,128)S(1)}, f32[8,128]{1,0:T(8,128)}, u32[]{:S(2)}) copy-start(f32[8,128]{1,0:T(8,128)} %param.15) | copy-start | bytes 12292
  8.8 22.7 %all-to-all-start = ((f32[16,128,128]{2,1,0:T(8,128)}), f32[16,128,128]{2,1,0:T(8,128)S(1)}, u32[]{:S(2)}, u32[]{:S(2)}) async-start(f32[16,128,128]{2,1,0:T(8,128)} %get-tuple-element.9), calls=%async_computation | async-start | bytes 2097152 | tf_op jit(solution)/shard_map/all_to_all | solution.py:265
  69.8 14.1 %collective-permute-start = (f32[16,48,128]{2,1,0:T(8,128)S(1)}, f32[16,48,128]{2,1,0:T(8,128)S(1)}, u32[]{:S(2)}, u32[]{:S(2)}) collective-permute-start(f32[16,48,128]{2,1,0:T(8,128)S(1)} %all_to_all.50.parts.mine), channel_id=1, source_target_pairs={{0,1},{1,0},{2,3},{3,2},{4,5},{5,4},{6,7},{7,6},{8,9},{9,8},{10,11... | collective-permute-start | bytes 1179656 | tf_op jit(solution)/shard_map/ppermute | solution.py:285
  71.7 12.2 %all-to-all-start.2 = ((f32[16,16,128]{2,1,0:T(8,128)}), f32[16,16,128]{2,1,0:T(8,128)S(1)}, u32[]{:S(2)}, u32[]{:S(2)}) async-start(f32[16,16,128]{2,1,0:T(8,128)} %shard_map.115), calls=%async_computation.2 | async-start | bytes 262144 | tf_op jit(solution)/shard_map/all_to_all | solution.py:265
  84.0 27.0 %copy-start.3 = (f32[512]{0:T(512)S(1)}, f32[512]{0:T(512)}, u32[]{:S(2)}) copy-start(f32[512]{0:T(512)} %param.13) | copy-start | bytes 6148
  105.2 18.8 %all-to-all-start.4 = ((f32[16,128,128]{2,1,0:T(8,128)}), f32[16,128,128]{2,1,0:T(8,128)S(1)}, u32[]{:S(2)}, u32[]{:S(2)}) async-start(f32[16,128,128]{2,1,0:T(8,128)} %shard_map.117), calls=%async_computation.4 | async-start | bytes 2097152 | tf_op jit(solution)/shard_map/all_to_all | solution.py:265
  129.3 5.7 %copy-start = (f32[4,2048]{1,0:T(4,128)S(1)}, f32[4,2048]{1,0:T(4,128)}, u32[]{:S(2)}) copy-start(f32[4,2048]{1,0:T(4,128)} %param.16) | copy-start | bytes 98308
  129.3 19.1 %all-to-all-start.5 = ((f32[16,128,128]{2,1,0:T(8,128)}), f32[16,128,128]{2,1,0:T(8,128)S(1)}, u32[]{:S(2)}, u32[]{:S(2)}) async-start(f32[16,128,128]{2,1,0:T(8,128)} %get-tuple-element.14), calls=%async_computation.5 | async-start | bytes 2097152 | tf_op jit(solution)/shard_map/all_to_all | solution.py:265
  195.7 16.9 %all-to-all-start.9 = ((f32[16,128,128]{2,1,0:T(8,128)}), f32[16,128,128]{2,1,0:T(8,128)S(1)}, u32[]{:S(2)}, u32[]{:S(2)}) async-start(f32[16,128,128]{2,1,0:T(8,128)} %shard_map.122), calls=%async_computation.9 | async-start | bytes 2097152 | tf_op jit(solution)/shard_map/all_to_all | solution.py:265

commit v4 on v3

v4 whole, which is shorter than its diff:
```python
import jax
import jax.numpy as jnp
from jax import lax
from jax.experimental import pallas as pl
from jax.experimental.pallas import tpu as pltpu
from jax.sharding import Mesh, PartitionSpec as P

BLOCK = 128
NX, NY, NZ, NC = 4, 4, 16, 2
NXY = NX * NY
OWN = 4
SPLIT = 2
PART = OWN // SPLIT
TILE = 512
OUT_TILES = 4
START_MIB = 16
PERMUTE_MIB = 32
MIDDLE_MIB = 14
F32 = jnp.float32
BF16 = jnp.bfloat16
HIGHEST = lax.Precision.HIGHEST
MIB = 1024 * 1024
HBM = pl.BlockSpec(memory_space=pltpu.HBM)
SMEM = pl.BlockSpec(memory_space=pltpu.SMEM)
VMEM = pl.BlockSpec(memory_space=pltpu.VMEM)
DMA = pltpu.SemaphoreType.DMA


def dot(left, right):
    return jnp.dot(left, right, preferred_element_type=F32)


def f32(*shape):
    return jax.ShapeDtypeStruct(shape, F32)


def far(shape, dtype=F32):
    return pltpu.HBM(shape, dtype)


def call(kernel, out_shape, out_specs, in_specs, scratch, limit, *args):
    args = [pltpu.with_memory_space_constraint(x, pltpu.HBM) if spec is HBM else x for spec, x in zip(in_specs, args)]
    return pl.pallas_call(
        kernel,
        out_shape=out_shape,
        out_specs=out_specs,
        in_specs=in_specs,
        scratch_shapes=scratch,
        compiler_params=pltpu.CompilerParams(vmem_limit_bytes=limit * MIB),
    )(*args)


def fetch(sources, targets, sems):
    copies = [pltpu.make_async_copy(s, t, sems.at[i]) for i, (s, t) in enumerate(zip(sources, targets))]
    for copy in copies:
        copy.start()
    return copies


def send_tile(part, tile, scratch, contrib, sems):
    count = part.shape[1] // BLOCK
    first = tile * count
    for i in range(count):
        scratch[first + i] = part[:, i * BLOCK : (i + 1) * BLOCK]
    rows = pl.ds(first, count)
    copy = pltpu.make_async_copy(scratch.at[rows], contrib.at[rows], sems.at[tile])
    copy.start()
    return copy


def masked(mask, coupling):
    for i in range(coupling.shape[1] // BLOCK):
        cols = slice(i * BLOCK, (i + 1) * BLOCK)
        coupling[:, cols] = jnp.where(mask[0, i] != 0, coupling[:, cols], jnp.zeros((), BF16))


def picks(owner, tile, size):
    rows = lax.broadcasted_iota(jnp.int32, (owner.shape[1], size), 0)
    return (rows == owner[:, tile * size : (tile + 1) * size]).astype(BF16)


def split3(x):
    high = x.astype(BF16)
    rest = x - high.astype(F32)
    mid = rest.astype(BF16)
    return [high, mid, (rest - mid.astype(F32)).astype(BF16)]


def start_kernel(
    first, mask_in, inverse_in, load_in, owner_in, sep_in, coupling_in, solved_out, contrib,
    mask, inverse, load, owner, sep, coupling, solved, part_buf, in_sems, out_sem, part_sems,
):
    waits = fetch(
        (mask_in, inverse_in, load_in, owner_in, sep_in, coupling_in),
        (mask, inverse, load, owner, sep, coupling),
        in_sems,
    )
    for wait in waits[1:3]:
        wait.wait()
    solved[...] = dot(inverse[...], load[...].astype(BF16))
    copies = [pltpu.make_async_copy(solved, solved_out, out_sem)]
    copies[0].start()
    mixed_t = solved[...].T.astype(BF16)
    for wait in waits[:1] + waits[3:]:
        wait.wait()
    masked(mask, coupling)
    own, sep_width = sep.shape[0], coupling.shape[1]
    size = sep_width // part_sems.shape[0]
    index = lax.broadcasted_iota(jnp.int32, (own, size), 0)
    target = jnp.zeros((own, size), jnp.int32)
    for j in range(own):
        target = jnp.where(index == j, owner[0, first[0] + j], target)
    for tile in range(part_sems.shape[0]):
        lanes = lax.broadcasted_iota(jnp.int32, (own, size), 1) + tile * size
        place = (lanes == target).astype(F32)
        loads = lax.dot_general(
            sep[...], place, (((0,), (0,)), ((), ())), precision=HIGHEST, preferred_element_type=F32
        )
        part = dot(mixed_t, coupling[:, tile * size : (tile + 1) * size]) - loads
        copies.append(send_tile(part, tile, part_buf, contrib, part_sems))
    for copy in copies:
        copy.wait()


def start(first, mask, inverse, coupling, load, owner, sep):
    cases = load.shape[1]
    return call(
        start_kernel,
        [far(load.shape), far((NXY, cases, BLOCK))],
        [HBM] * 2,
        [SMEM] + [HBM] * 6,
        [
            pltpu.SMEM(mask.shape, jnp.int32),
            pltpu.VMEM(inverse.shape, BF16),
            pltpu.VMEM(load.shape, F32),
            pltpu.SMEM(owner.shape, jnp.int32),
            pltpu.VMEM(sep.shape, F32),
            pltpu.VMEM(coupling.shape, BF16),
            pltpu.VMEM(load.shape, F32),
            pltpu.VMEM((NXY, cases, BLOCK), F32),
            DMA((6,)),
            DMA,
            DMA((OUT_TILES,)),
        ],
        START_MIB,
        first, mask, inverse, load, owner, sep, coupling,
    )


def permute_kernel(
    mask_in, owner_in, own_in, coupling_in, after, columns_out, packed,
    mask, owner, own, coupling, columns, in_sems, out_sems,
):
    waits = fetch((mask_in, owner_in, own_in, coupling_in), (mask, owner, own, coupling), in_sems)
    for wait in waits:
        wait.wait()
    masked(mask, coupling)
    terms = jnp.concatenate([x.astype(F32) for x in split3(own[...])], axis=0).astype(BF16)
    rows = jnp.zeros((3 * OWN, owner.shape[1]), F32)
    copies = []
    for tile in range(coupling.shape[1] // TILE):
        cols = pl.ds(tile * TILE, TILE)
        pick = picks(owner, tile, TILE)
        columns[:, cols] = dot(coupling[...], pick).astype(BF16)
        copy = pltpu.make_async_copy(columns.at[:, cols], columns_out.at[:, cols], out_sems.at[tile])
        copy.start()
        copies.append(copy)
        rows = rows + lax.dot_general(
            terms[:, tile * TILE : (tile + 1) * TILE], pick, (((1,), (1,)), ((), ())), preferred_element_type=F32
        )
    rows = rows[:OWN] + rows[OWN : 2 * OWN] + rows[2 * OWN :]
    for k in range(SPLIT):
        for t in range(NXY):
            packed[k, t * PART : (t + 1) * PART] = rows[k * PART : (k + 1) * PART, t * BLOCK : (t + 1) * BLOCK]
    for copy in copies:
        copy.wait()


def permute(mask, owner, own, coupling, after):
    return call(
        permute_kernel,
        [far(coupling.shape, BF16), f32(SPLIT, NXY * PART, BLOCK)],
        [HBM, VMEM],
        [HBM] * 5,
        [
            pltpu.SMEM(mask.shape, jnp.int32),
            pltpu.VMEM(owner.shape, jnp.int32),
            pltpu.VMEM(own.shape, F32),
            pltpu.VMEM(coupling.shape, BF16),
            pltpu.VMEM(coupling.shape, BF16),
            DMA((4,)),
            DMA((coupling.shape[1] // TILE,)),
        ],
        PERMUTE_MIB,
        mask, owner, own, coupling, after,
    )


def reorder_kernel(owner_in, mine, other, after, mine_out, other_out, token, owner, terms, sem):
    copy = pltpu.make_async_copy(owner_in, owner, sem)
    copy.start()
    span, count = BLOCK // (NZ * PART), NZ * PART
    token[...] = jnp.zeros(token.shape, F32)
    left = lax.broadcasted_iota(jnp.int32, (BLOCK, BLOCK), 0)
    right = lax.broadcasted_iota(jnp.int32, (BLOCK, BLOCK), 1)

    def by_block(k):
        return (k // PART) % span * count + k // (span * PART) * PART + k % PART

    gather = (left == by_block(right)).astype(BF16)
    scatter = (right == by_block(left)).astype(F32)
    base = mine.shape[1] - NXY * PART
    for n, source in enumerate((mine, other)):
        for i in range(NXY // span):
            tile = source[:, base + 8 * i : base + 8 * (i + 1)].reshape(BLOCK, BLOCK)
            for m, term in enumerate(split3(tile)):
                moved = dot(gather, term).astype(BF16)
                for j in range(span):
                    row = (2 * m + n) * count
                    col = (span * i + j) * BLOCK
                    terms[row : row + count, col : col + BLOCK] = moved[j * count : (j + 1) * count]
    copy.wait()
    size = span * BLOCK
    for i in range(NXY // span):
        part = dot(terms[...], picks(owner, i, size))
        part = part[: 2 * count] + part[2 * count : 4 * count] + part[4 * count :]
        for n, out in enumerate((mine_out, other_out)):
            stack = jnp.concatenate(
                [part[n * count : (n + 1) * count, j * BLOCK : (j + 1) * BLOCK] for j in range(span)], axis=0
            )
            tile = jnp.dot(scatter, stack, precision=HIGHEST, preferred_element_type=F32)
            out[:, 8 * i : 8 * (i + 1)] = tile.reshape(NZ, 8, BLOCK)


def reorder(owner, mine, other, after):
    shape = (NZ, NXY * PART, BLOCK)
    return call(
        reorder_kernel,
        [f32(*shape)] * 2 + [f32(8, BLOCK)],
        [VMEM] * 3,
        [HBM, VMEM, VMEM, HBM],
        [pltpu.VMEM(owner.shape, jnp.int32), pltpu.VMEM((6 * NZ * PART, NXY * BLOCK), BF16), DMA],
        PERMUTE_MIB,
        owner, mine, other, after,
    )


def case_group(total, z):
    group = total.shape[0] * SPLIT // NZ
    first = z // SPLIT * group
    return total[first : first + group]


def pack_sum_kernel(parts, packed, out, buf, sem):
    group = parts.shape[1] * SPLIT // NZ
    total = -jnp.sum(parts[...], axis=0)
    for z in range(NZ):
        buf[z, :group] = case_group(total, z)
        buf[z, group:] = packed[z % SPLIT]
    copy = pltpu.make_async_copy(buf, out, sem)
    copy.start()
    copy.wait()


def sum_rows_kernel(parts, local_t, out):
    total = local_t[...] - jnp.sum(parts[...], axis=0)
    for z in range(NZ):
        out[z] = case_group(total, z)


def sum_cases_kernel(parts, out):
    total = jnp.sum(parts[:, : out.shape[1]], axis=0)
    out[...] = jnp.broadcast_to(total[None], out.shape)


def delta_kernel(core, rhs, mine, other, out):
    cases = rhs.shape[1]
    span = BLOCK // (NZ * PART)
    base = mine.shape[1] - NXY * PART
    acc_mine = jnp.zeros((span * cases, BLOCK), F32)
    acc_other = jnp.zeros((span * cases, BLOCK), F32)
    for i in range(NXY // span):
        left = rhs[span * i : span * (i + 1)].reshape(span * cases, BLOCK)
        rows = slice(base + 8 * i, base + 8 * (i + 1))
        acc_mine = acc_mine + rows_dot(left, mine[:, rows].reshape(BLOCK, BLOCK))
        acc_other = acc_other + rows_dot(left, other[:, rows].reshape(BLOCK, BLOCK))
    low = lax.broadcasted_iota(jnp.int32, (cases, BLOCK), 1) % 8 < PART

    def fold(acc):
        total = acc[:cases]
        for j in range(1, span):
            total = total + pltpu.roll(acc[j * cases : (j + 1) * cases], BLOCK - PART * j, 1)
        return jnp.where(low, total, 0.0)

    own, far_rows = fold(acc_mine), fold(acc_other)
    first = core[0] == 0
    total = jnp.where(first, own, far_rows) + pltpu.roll(jnp.where(first, far_rows, own), OWN, 1)
    half = cases // SPLIT
    tile = total[:half] + pltpu.roll(total[half:], PART, 1)
    out[...] = jnp.broadcast_to(tile[None], out.shape)


def rows_dot(left, rows):
    return lax.dot_general(
        left, rows, (((1,), (1,)), ((), ())), precision=HIGHEST, preferred_element_type=F32
    )


def spread_kernel(parts, out, cases_buf, buf, sems):
    half = parts.shape[1]
    low = lax.broadcasted_iota(jnp.int32, (half, BLOCK), 1) % (2 * PART) < PART
    for i in range(NZ // SPLIT):
        even, odd = parts[SPLIT * i], parts[SPLIT * i + 1]
        cases_buf[2 * half * i : 2 * half * i + half] = jnp.where(low, even, pltpu.roll(odd, PART, 1))
        cases_buf[2 * half * i + half : 2 * half * (i + 1)] = jnp.where(low, pltpu.roll(even, BLOCK - PART, 1), odd)
    buf[...] = cases_buf[...].T
    copies = [pltpu.make_async_copy(buf, out.at[i], sems.at[i]) for i in range(NXY)]
    for copy in copies:
        copy.start()
    for copy in copies:
        copy.wait()


def near_kernel(columns, after, out, sem):
    copy = pltpu.make_async_copy(columns.at[:, : out.shape[1]], out, sem)
    copy.start()
    copy.wait()


def near(columns, after):
    width, sep_width = columns.shape
    half = jax.ShapeDtypeStruct((width, sep_width // 2), BF16)
    return call(near_kernel, half, VMEM, [HBM] * 2, [DMA], 4, columns, after)


def coupled_product(low, high, delta):
    half = low.shape[1]
    return dot(low[...], delta[:half, :].astype(BF16)), lambda: dot(high[...], delta[half:, :].astype(BF16))


def own_rows(first, delta, count):
    return delta[pl.ds(pl.multiple_of(first[0], 8), count), :]


def middle_kernel(
    first, delta, cubic, low, after, columns_in, inverse_in, solved_in, matrix_in, load_in, state_out, contrib, sep_out,
    high, inverse, solved, matrix, load, mixed, part_buf, in_sems, out_sem, part_sems,
):
    half = low.shape[1]
    waits = fetch(
        (columns_in.at[:, half:], inverse_in, solved_in, matrix_in, load_in),
        (high, inverse, solved, matrix, load),
        in_sems,
    )
    sep_out[...] = own_rows(first, delta, sep_out.shape[0])
    coupled, rest = coupled_product(low, high, delta)
    waits[0].wait()
    coupled = coupled + rest()
    waits[1].wait()
    waits[2].wait()
    state = solved[...] - dot(inverse[...], coupled.astype(BF16))
    waits[3].wait()
    waits[4].wait()
    resid = load[...] - dot(matrix[...], state.astype(BF16)) - coupled
    resid = resid - cubic[...] * state * state * state
    mixed[...] = state + dot(inverse[...], resid.astype(BF16))
    copies = [pltpu.make_async_copy(mixed, state_out, out_sem)]
    copies[0].start()
    mixed_t = mixed[...].T.astype(BF16)
    count = part_sems.shape[0]
    size = 2 * half // count
    for i in range(count):
        source, at = (low, i) if i < count // 2 else (high, i - count // 2)
        part = dot(mixed_t, source[:, at * size : (at + 1) * size])
        copies.append(send_tile(part, i, part_buf, contrib, part_sems))
    for copy in copies:
        copy.wait()


def end_kernel(
    first, delta, low, sep_in, columns_in, inverse_in, mixed_in, out, sep_out,
    high, inverse, mixed, state, in_sems, out_sems,
):
    waits = fetch((columns_in.at[:, low.shape[1] :], inverse_in, mixed_in), (high, inverse, mixed), in_sems)
    sep_out[...] = sep_in[...] + own_rows(first, delta, sep_out.shape[0])
    back, rest = coupled_product(low, high, delta)
    waits[0].wait()
    back = (back + rest()).astype(BF16)
    waits[1].wait()
    waits[2].wait()
    count = out_sems.shape[0]
    rows = state.shape[0] // count
    copies = []
    for i in range(count):
        part = pl.ds(i * rows, rows)
        state[part, :] = mixed[part, :] - dot(inverse[part, :], back)
        copy = pltpu.make_async_copy(state.at[part], out.at[part], out_sems.at[i])
        copy.start()
        copies.append(copy)
    for copy in copies:
        copy.wait()


def exchange(parts, axes):
    return lax.all_to_all(parts, axes, 0, 0, tiled=True)


def correction(contrib, local, place, core, packed, rows, owner, columns):
    cases = contrib.shape[1]
    group = cases * SPLIT // NZ
    parts = exchange(contrib, ("x", "y"))
    first = rows is None
    if first:
        sent = (NZ, group + packed.shape[1], BLOCK)
        parts = call(pack_sum_kernel, far(sent), HBM, [VMEM] * 2, [pltpu.VMEM(sent, F32), DMA], 8, parts, packed)
    else:
        local_t = lax.dynamic_update_slice_in_dim(jnp.zeros((BLOCK, cases), F32), local, place, 0).T
        parts = call(sum_rows_kernel, f32(NZ, group, BLOCK), VMEM, [VMEM] * 2, [], 8, parts, local_t)
    parts = exchange(parts, "z")
    rhs = call(sum_cases_kernel, f32(NXY, group, BLOCK), VMEM, [VMEM], [], 4, parts)
    if first:
        parts, rhs = lax.optimization_barrier((parts, rhs))
        rows = (parts, lax.ppermute(parts, "c", [(0, 1), (1, 0)]))
    rhs = exchange(rhs, ("x", "y"))
    delta = call(
        delta_kernel, f32(NZ, group // SPLIT, BLOCK), VMEM, [SMEM] + [VMEM] * 3, [], 8, core, rhs, *rows
    )
    delta = exchange(delta, "z")
    delta = call(
        spread_kernel,
        far((NXY, BLOCK, cases)),
        HBM,
        [VMEM],
        [pltpu.VMEM((cases, BLOCK), F32), pltpu.VMEM((BLOCK, cases), F32), DMA((NXY,))],
        4,
        delta,
    )
    low = near(columns, delta)
    if first:
        rows = list(reorder(owner, *rows, delta))
    return exchange(delta, ("x", "y")).reshape(NXY * BLOCK, cases), rows, low


def on_device(
    leaf_matrix,
    leaf_inverse,
    coupling,
    cubic_coeff,
    leaf_load,
    sep_load,
    sep_matrix,
    sep_inverse,
    owner_map,
    block_mask,
):
    owned, cases = sep_load.shape
    width, sep_width = coupling.shape
    matrix_rows = lax.all_gather(sep_matrix, "c", axis=0, tiled=True)
    core = lax.axis_index("c").astype(jnp.int32)[None]
    place = lax.axis_index("z") * owned
    first = (lax.axis_index(("x", "y", "z")) * owned).astype(jnp.int32)[None]
    owner = owner_map[None, :]
    solved, contrib = start(first, block_mask, leaf_inverse, coupling, leaf_load, owner, sep_load)
    columns, packed = permute(block_mask, owner, sep_inverse, coupling, solved)

    delta, rows, low = correction(contrib, None, place, core, packed, None, owner, columns)
    local = sep_load - jnp.dot(matrix_rows, delta, precision=HIGHEST, preferred_element_type=F32)
    high = pltpu.VMEM((width, sep_width // 2), BF16)
    square = pltpu.VMEM(leaf_matrix.shape, BF16)
    state = pltpu.VMEM((width, cases), F32)
    mixed, contrib, sep_rows = call(
        middle_kernel,
        [far((width, cases)), far((NXY, cases, BLOCK)), f32(owned, cases)],
        [HBM, HBM, VMEM],
        [SMEM] + [VMEM] * 4 + [HBM] * 5,
        [high, square, state, square, state, state, pltpu.VMEM((NXY, cases, BLOCK), F32)]
        + [DMA((5,)), DMA, DMA((OUT_TILES,))],
        MIDDLE_MIB,
        first, delta, cubic_coeff[:, None], low, rows.pop(), columns, leaf_inverse, solved, leaf_matrix, leaf_load,
    )
    delta, rows, low = correction(contrib, local, place, core, None, rows, owner, columns)
    return call(
        end_kernel,
        [far((width, cases)), f32(owned, cases)],
        [HBM, VMEM],
        [SMEM] + [VMEM] * 3 + [HBM] * 3,
        [high, square, state, state, DMA((3,)), DMA((2,))],
        MIDDLE_MIB,
        first, delta, low, sep_rows, columns, leaf_inverse, mixed,
    )


def solution(mesh):
    grid = Mesh(mesh.devices.reshape(NX, NY, NZ, NC), ("x", "y", "z", "c"))
    leaf = ("x", "y", "z")
    in_specs = (
        P(leaf, None),
        P(leaf, None),
        P(leaf, None),
        P(leaf),
        P(leaf, "c"),
        P(leaf, "c"),
        P(leaf + ("c",), None),
        P(leaf + ("c",), None),
        P(),
        P(leaf, None),
    )
    out_specs = (P(leaf, "c"), P(leaf, "c"))
    return jax.shard_map(on_device, mesh=grid, in_specs=in_specs, out_specs=out_specs, check_vma=False)
```

time: 219 us -> 214 us (0.977)
  waiting for transfers between devices: 52 us -> 35.5 us
  Pallas kernels: 23.7 us -> 35.9 us
    all_to_all x5, waiting for transfers between devices: 52 us -> 35.5 us  [exchange(): return lax.all_to_all(parts, axes, 0, 0, tiled=True)]
    pallas_call x11 -> x15, Pallas kernels: 23.7 us -> 35.9 us  [call(): pl.pallas_call(kernel, out_shape=out_shape, out_specs=out_specs, in_specs...]
  transfers between devices with their start and end apart: 6 -> 6, of which waited for: 5 -> 5; matrix products, arithmetic and copies ran while one was open for 1% -> 1% of each run, Pallas kernels for 0% -> 8%
where the time goes in v4:
time: 214 us; the launch traced here: 212 us
  blocking collectives  102 us (48%)
  Pallas kernels  35.9 us (17%)
  waiting for transfers between devices  35.5 us (17%)
  starting transfers between devices  34.8 us (16%)
    all_to_all x5, blocking collectives, exchange(): return lax.all_to_all(parts, axes, 0, 0, tiled=True)  100 us
    pallas_call x15, Pallas kernels, call(): pl.pallas_call(kernel, out_shape=out_shape, out_specs=out_specs, in_specs...  35.9 us
    all_to_all x5, waiting for transfers between devices, exchange(): return lax.all_to_all(parts, axes, 0, 0, tiled=True)  35.5 us
    all_to_all x5, starting transfers between devices, exchange(): return lax.all_to_all(parts, axes, 0, 0, tiled=True)  32.9 us
  transfers between devices with their start and end apart: 6, of which 5 were waited for; matrix products, arithmetic and copies ran while one was open for 1% of the time, Pallas kernels for 8%

profile of v4, /device:TPU:6, one launch (start us, length us, event | category | flops | bytes accessed | tf_op | source)
XLA Modules:
  0.0 212.3 jit_solution(2331104930165949371)
XLA Ops:
  0.6 4.4 %shard_map.113 = (f32[512,128]{1,0:T(8,128)}, f32[16,128,128]{2,1,0:T(8,128)}) custom-call(s32[1]{0:T(128)} %bitcast.first, s32[1,16]{1,0:T(1,128)} %mask_in.3, bf16[512,512]{1,0:T(8,128)(2,1)} %inverse_in.5, f32[512,128]{1,0:T(8,128)} %load_in.3, s32[1,2048]{1,0:T(1,128)} %bitcast.18, f32[8,128]{1,0:T(8,128)} %sep_in.1, bf16[512,2048]{1,0:T(8,128)(2,1)} %coupling_in.3), custom_call_target="tpu_custom_call" | custom-call | tf_op jit(solution)/shard_map/pallas_call | solution.py:43
  5.0 9.4 %all-to-all-start = ((f32[16,128,128]{2,1,0:T(8,128)}), f32[16,128,128]{2,1,0:T(8,128)S(1)}, u32[]{:S(2)}, u32[]{:S(2)}) async-start(f32[16,128,128]{2,1,0:T(8,128)} %get-tuple-element.14), calls=%async_computation | async-start | bytes 2097152 | tf_op jit(solution)/shard_map/all_to_all | solution.py:405
  14.4 9.5 %shard_map.114 = (bf16[512,2048]{1,0:T(8,128)(2,1)}, f32[2,32,128]{2,1,0:T(8,128)S(1)}) custom-call(s32[1,16]{1,0:T(1,128)} %mask_in.3, s32[1,2048]{1,0:T(1,128)} %bitcast.19, f32[4,2048]{1,0:T(4,128)} %own_in.1, bf16[512,2048]{1,0:T(8,128)(2,1)} %coupling_in.3, f32[512,128]{1,0:T(8,128)} %get-tuple-element.15.after.solved_in), custom_call_target="tpu_custom_call" | custom-call | tf_op jit(solution)/shard_map/pallas_call | solution.py:43
  23.9 3.8 %all-to-all-done.parts = f32[16,128,128]{2,1,0:T(8,128)S(1)} async-done(((f32[16,128,128]{2,1,0:T(8,128)}), f32[16,128,128]{2,1,0:T(8,128)S(1)}, u32[]{:S(2)}, u32[]{:S(2)}) %all-to-all-start) | async-done | bytes 1048608 | tf_op jit(solution)/shard_map/all_to_all | solution.py:405
  28.5 36.9 %all_to_all.50.parts.mine = f32[16,48,128]{2,1,0:T(8,128)S(1)} all-to-all(f32[16,48,128]{2,1,0:T(8,128)} %shard_map.115), channel_id=1, replica_groups=mesh['x'=4,'y'=4,'z'=16,'c'=2] {'z'}, dimensions={0} | all-to-all | bytes 786432 | tf_op jit(solution)/shard_map/all_to_all | solution.py:405
  66.1 1.9 collective-permute-start
  68.0 6.4 %all-to-all-start.2 = ((f32[16,16,128]{2,1,0:T(8,128)}), f32[16,16,128]{2,1,0:T(8,128)S(1)}, u32[]{:S(2)}, u32[]{:S(2)}) async-start(f32[16,16,128]{2,1,0:T(8,128)} %shard_map.116), calls=%async_computation.2 | async-start | bytes 262144 | tf_op jit(solution)/shard_map/all_to_all | solution.py:405
  74.4 5.9 %all-to-all-done.2.rhs = f32[16,16,128]{2,1,0:T(8,128)S(1)} async-done(((f32[16,16,128]{2,1,0:T(8,128)}), f32[16,16,128]{2,1,0:T(8,128)S(1)}, u32[]{:S(2)}, u32[]{:S(2)}) %all-to-all-start.2) | async-done | bytes 131104 | tf_op jit(solution)/shard_map/all_to_all | solution.py:405
  80.2 1.3 shard_map.117
  81.6 18.7 %all_to_all.51.parts = f32[16,8,128]{2,1,0:T(8,128)S(1)} all-to-all(f32[16,8,128]{2,1,0:T(8,128)S(1)} %shard_map.117), channel_id=1, replica_groups=mesh['x'=4,'y'=4,'z'=16,'c'=2] {'z'}, dimensions={0} | all-to-all | bytes 131072 | tf_op jit(solution)/shard_map/all_to_all | solution.py:405
  101.5 5.7 %all-to-all-start.4 = ((f32[16,128,128]{2,1,0:T(8,128)}), f32[16,128,128]{2,1,0:T(8,128)S(1)}, u32[]{:S(2)}, u32[]{:S(2)}) async-start(f32[16,128,128]{2,1,0:T(8,128)} %shard_map.118.after), calls=%async_computation.4 | async-start | bytes 2097152 | tf_op jit(solution)/shard_map/all_to_all | solution.py:405
  108.6 3.9 %shard_map.120 = (f32[16,32,128]{2,1,0:T(8,128)S(1)}, f32[16,32,128]{2,1,0:T(8,128)S(1)}, f32[8,128]{1,0:T(8,128)S(1)}) custom-call(s32[1,2048]{1,0:T(1,128)} %bitcast.20, f32[16,48,128]{2,1,0:T(8,128)S(1)} %all_to_all.50.parts.mine, f32[16,48,128]{2,1,0:T(8,128)S(1)} %collective-permute-done.other, f32[16,128,128]{2,1,0:T(8,128)} %shard_map.118.after), custom_call_target="tpu_custom_call" | custom-call | tf_op jit(solution)/shard_map/pallas_call | solution.py:43
  113.3 7.0 %all-to-all-done.4 = f32[16,128,128]{2,1,0:T(8,128)S(1)} async-done(((f32[16,128,128]{2,1,0:T(8,128)}), f32[16,128,128]{2,1,0:T(8,128)S(1)}, u32[]{:S(2)}, u32[]{:S(2)}) %all-to-all-start.4) | async-done | bytes 1048608 | tf_op jit(solution)/shard_map/all_to_all | solution.py:405
  120.3 5.0 %shard_map.121 = (f32[512,128]{1,0:T(8,128)}, f32[16,128,128]{2,1,0:T(8,128)}, f32[8,128]{1,0:T(8,128)S(1)}) custom-call(s32[1]{0:T(128)} %bitcast.first, f32[2048,128]{1,0:T(8,128)S(1)} %bitcast.14, f32[512,1]{1,0:T(8,128)S(1)} %copy.17.cubic, bf16[512,1024]{1,0:T(8,128)(2,1)S(1)} %shard_map.119.low, f32[8,128]{1,0:T(8,128)S(1)} %get-tuple-element.20.after, ...), custom_call_target="tpu_custom_call" | custom-call | tf_op jit(solution)/shard_map/pallas_call | solution.py:43
  125.3 5.7 %all-to-all-start.5 = ((f32[16,128,128]{2,1,0:T(8,128)}), f32[16,128,128]{2,1,0:T(8,128)S(1)}, u32[]{:S(2)}, u32[]{:S(2)}) async-start(f32[16,128,128]{2,1,0:T(8,128)} %get-tuple-element.21), calls=%async_computation.5 | async-start | bytes 2097152 | tf_op jit(solution)/shard_map/all_to_all | solution.py:405
  131.2 1.9 all-gather
  133.1 1.8 fusion
  135.3 8.9 %all-to-all-done.5.parts = f32[16,128,128]{2,1,0:T(8,128)S(1)} async-done(((f32[16,128,128]{2,1,0:T(8,128)}), f32[16,128,128]{2,1,0:T(8,128)S(1)}, u32[]{:S(2)}, u32[]{:S(2)}) %all-to-all-start.5) | async-done | bytes 1048608 | tf_op jit(solution)/shard_map/all_to_all | solution.py:405
  144.3 16.8 %all_to_all.52.parts = f32[16,16,128]{2,1,0:T(8,128)S(1)} all-to-all(f32[16,16,128]{2,1,0:T(8,128)S(1)} %shard_map.122), channel_id=1, replica_groups=mesh['x'=4,'y'=4,'z'=16,'c'=2] {'z'}, dimensions={0} | all-to-all | bytes 262144 | tf_op jit(solution)/shard_map/all_to_all | solution.py:405
  161.2 11.5 %all_to_all.53.rhs = f32[16,16,128]{2,1,0:T(8,128)S(1)} all-to-all(f32[16,16,128]{2,1,0:T(8,128)S(1)} %shard_map.123), channel_id=1, replica_groups=mesh['x'=4,'y'=4,'z'=16,'c'=2] {'x','y'}, dimensions={0} | all-to-all | bytes 262144 | tf_op jit(solution)/shard_map/all_to_all | solution.py:405
  174.0 16.3 %all_to_all.54.parts = f32[16,8,128]{2,1,0:T(8,128)S(1)} all-to-all(f32[16,8,128]{2,1,0:T(8,128)S(1)} %shard_map.124), channel_id=1, replica_groups=mesh['x'=4,'y'=4,'z'=16,'c'=2] {'z'}, dimensions={0} | all-to-all | bytes 131072 | tf_op jit(solution)/shard_map/all_to_all | solution.py:405
  191.6 5.7 %all-to-all-start.9 = ((f32[16,128,128]{2,1,0:T(8,128)}), f32[16,128,128]{2,1,0:T(8,128)S(1)}, u32[]{:S(2)}, u32[]{:S(2)}) async-start(f32[16,128,128]{2,1,0:T(8,128)} %shard_map.125.after), calls=%async_computation.9 | async-start | bytes 2097152 | tf_op jit(solution)/shard_map/all_to_all | solution.py:405
  198.5 9.9 %all-to-all-done.9 = f32[16,128,128]{2,1,0:T(8,128)S(1)} async-done(((f32[16,128,128]{2,1,0:T(8,128)}), f32[16,128,128]{2,1,0:T(8,128)S(1)}, u32[]{:S(2)}, u32[]{:S(2)}) %all-to-all-start.9) | async-done | bytes 1048608 | tf_op jit(solution)/shard_map/all_to_all | solution.py:405
  208.4 3.8 %shard_map.127 = (f32[512,128]{1,0:T(8,128)}, f32[8,128]{1,0:T(8,128)}) custom-call(s32[1]{0:T(128)} %bitcast.first, f32[2048,128]{1,0:T(8,128)S(1)} %bitcast.16, bf16[512,1024]{1,0:T(8,128)(2,1)S(1)} %shard_map.126.low, f32[8,128]{1,0:T(8,128)S(1)} %get-tuple-element.24.sep_in, bf16[512,2048]{1,0:T(8,128)(2,1)} %get-tuple-element.19.columns.columns_in, ...), custom_call_target="tpu_custom_call" | custom-call | tf_op jit(solution)/shard_map/pallas_call | solution.py:43
  (25 shorter events, 9.3 us)
Async XLA Ops:
  5.0 22.7 %all-to-all-start = ((f32[16,128,128]{2,1,0:T(8,128)}), f32[16,128,128]{2,1,0:T(8,128)S(1)}, u32[]{:S(2)}, u32[]{:S(2)}) async-start(f32[16,128,128]{2,1,0:T(8,128)} %get-tuple-element.14), calls=%async_computation | async-start | bytes 2097152 | tf_op jit(solution)/shard_map/all_to_all | solution.py:405
  66.1 14.2 %collective-permute-start = (f32[16,48,128]{2,1,0:T(8,128)S(1)}, f32[16,48,128]{2,1,0:T(8,128)S(1)}, u32[]{:S(2)}, u32[]{:S(2)}) collective-permute-start(f32[16,48,128]{2,1,0:T(8,128)S(1)} %all_to_all.50.parts.mine), channel_id=1, source_target_pairs={{0,1},{1,0},{2,3},{3,2},{4,5},{5,4},{6,7},{7,6},{8,9},{9,8},{10,11... | collective-permute-start | bytes 1179656 | tf_op jit(solution)/shard_map/ppermute | solution.py:423
  68.0 12.2 %all-to-all-start.2 = ((f32[16,16,128]{2,1,0:T(8,128)}), f32[16,16,128]{2,1,0:T(8,128)S(1)}, u32[]{:S(2)}, u32[]{:S(2)}) async-start(f32[16,16,128]{2,1,0:T(8,128)} %shard_map.116), calls=%async_computation.2 | async-start | bytes 262144 | tf_op jit(solution)/shard_map/all_to_all | solution.py:405
  80.2 27.0 %copy-start.4 = (f32[512]{0:T(512)S(1)}, f32[512]{0:T(512)}, u32[]{:S(2)}) copy-start(f32[512]{0:T(512)} %param.13) | copy-start | bytes 6148
  101.5 18.8 %all-to-all-start.4 = ((f32[16,128,128]{2,1,0:T(8,128)}), f32[16,128,128]{2,1,0:T(8,128)S(1)}, u32[]{:S(2)}, u32[]{:S(2)}) async-start(f32[16,128,128]{2,1,0:T(8,128)} %shard_map.118.after), calls=%async_computation.4 | async-start | bytes 2097152 | tf_op jit(solution)/shard_map/all_to_all | solution.py:405
  112.6 0.7 copy-start
  125.3 5.8 %copy-start.3 = (f32[8,128]{1,0:T(8,128)S(1)}, f32[8,128]{1,0:T(8,128)}, u32[]{:S(2)}) copy-start(f32[8,128]{1,0:T(8,128)} %sep_in.1) | copy-start | bytes 12292
  125.3 5.9 %copy-start.2 = (f32[4,2048]{1,0:T(4,128)S(1)}, f32[4,2048]{1,0:T(4,128)}, u32[]{:S(2)}) copy-start(f32[4,2048]{1,0:T(4,128)} %param.16) | copy-start | bytes 98308
  125.3 18.9 %all-to-all-start.5 = ((f32[16,128,128]{2,1,0:T(8,128)}), f32[16,128,128]{2,1,0:T(8,128)S(1)}, u32[]{:S(2)}, u32[]{:S(2)}) async-start(f32[16,128,128]{2,1,0:T(8,128)} %get-tuple-element.21), calls=%async_computation.5 | async-start | bytes 2097152 | tf_op jit(solution)/shard_map/all_to_all | solution.py:405
  131.1 41.6 %copy-start.1 = (f32[16,32,128]{2,1,0:T(8,128)S(1)}, f32[16,32,128]{2,1,0:T(8,128)}, u32[]{:S(2)}) copy-start(f32[16,32,128]{2,1,0:T(8,128)} %copy-done) | copy-start | bytes 786436
  191.6 16.8 %all-to-all-start.9 = ((f32[16,128,128]{2,1,0:T(8,128)}), f32[16,128,128]{2,1,0:T(8,128)S(1)}, u32[]{:S(2)}, u32[]{:S(2)}) async-start(f32[16,128,128]{2,1,0:T(8,128)} %shard_map.125.after), calls=%async_computation.9 | async-start | bytes 2097152 | tf_op jit(solution)/shard_map/all_to_all | solution.py:405

commit v5 on v4

--- a/solution.py
+++ b/solution.py
@@ -86,6 +86,10 @@
     return [high, mid, (rest - mid.astype(F32)).astype(BF16)]
 
 
+def join(terms):
+    return jnp.concatenate([x.astype(F32) for x in terms], axis=0).astype(BF16)
+
+
 def start_kernel(
     first, mask_in, inverse_in, load_in, owner_in, sep_in, coupling_in, solved_out, contrib,
     mask, inverse, load, owner, sep, coupling, solved, part_buf, in_sems, out_sem, part_sems,
@@ -103,8 +107,8 @@
     mixed_t = solved[...].T.astype(BF16)
     for wait in waits[:1] + waits[3:]:
         wait.wait()
-    masked(mask, coupling)
     own, sep_width = sep.shape[0], coupling.shape[1]
+    loads_in = join(split3(sep[...]))
     size = sep_width // part_sems.shape[0]
     index = lax.broadcasted_iota(jnp.int32, (own, size), 0)
     target = jnp.zeros((own, size), jnp.int32)
@@ -114,9 +118,14 @@
         lanes = lax.broadcasted_iota(jnp.int32, (own, size), 1) + tile * size
         place = (lanes == target).astype(F32)
         loads = lax.dot_general(
-            sep[...], place, (((0,), (0,)), ((), ())), precision=HIGHEST, preferred_element_type=F32
+            loads_in, join([place] * 3), (((0,), (0,)), ((), ())), preferred_element_type=F32
         )
-        part = dot(mixed_t, coupling[:, tile * size : (tile + 1) * size]) - loads
+        part = dot(mixed_t, coupling[:, tile * size : (tile + 1) * size])
+        count = size // BLOCK
+        kept = [
+            jnp.where(mask[0, tile * count + i] != 0, part[:, i * BLOCK : (i + 1) * BLOCK], 0.0) for i in range(count)
+        ]
+        part = jnp.concatenate(kept, axis=1) - loads
         copies.append(send_tile(part, tile, part_buf, contrib, part_sems))
     for copy in copies:
         copy.wait()
@@ -155,7 +164,7 @@
     for wait in waits:
         wait.wait()
     masked(mask, coupling)
-    terms = jnp.concatenate([x.astype(F32) for x in split3(own[...])], axis=0).astype(BF16)
+    terms = join(split3(own[...]))
     rows = jnp.zeros((3 * OWN, owner.shape[1]), F32)
     copies = []
     for tile in range(coupling.shape[1] // TILE):
@@ -251,15 +260,12 @@
     return total[first : first + group]
 
 
-def pack_sum_kernel(parts, packed, out, buf, sem):
+def pack_sum_kernel(parts, packed, out):
     group = parts.shape[1] * SPLIT // NZ
     total = -jnp.sum(parts[...], axis=0)
     for z in range(NZ):
-        buf[z, :group] = case_group(total, z)
-        buf[z, group:] = packed[z % SPLIT]
-    copy = pltpu.make_async_copy(buf, out, sem)
-    copy.start()
-    copy.wait()
+        out[z, :group] = case_group(total, z)
+        out[z, group:] = packed[z % SPLIT]
 
 
 def sum_rows_kernel(parts, local_t, out):
@@ -280,7 +286,7 @@
     acc_mine = jnp.zeros((span * cases, BLOCK), F32)
     acc_other = jnp.zeros((span * cases, BLOCK), F32)
     for i in range(NXY // span):
-        left = rhs[span * i : span * (i + 1)].reshape(span * cases, BLOCK)
+        left = split3(rhs[span * i : span * (i + 1)].reshape(span * cases, BLOCK))
         rows = slice(base + 8 * i, base + 8 * (i + 1))
         acc_mine = acc_mine + rows_dot(left, mine[:, rows].reshape(BLOCK, BLOCK))
         acc_other = acc_other + rows_dot(left, other[:, rows].reshape(BLOCK, BLOCK))
@@ -301,9 +307,15 @@
 
 
 def rows_dot(left, rows):
-    return lax.dot_general(
-        left, rows, (((1,), (1,)), ((), ())), precision=HIGHEST, preferred_element_type=F32
-    )
+    count = left[0].shape[0]
+    total = jnp.zeros((count, rows.shape[0]), F32)
+    for i, term in enumerate(split3(rows)):
+        part = lax.dot_general(
+            jnp.concatenate(left[: 3 - i], axis=0), term, (((1,), (1,)), ((), ())), preferred_element_type=F32
+        )
+        for j in range(3 - i):
+            total = total + part[j * count : (j + 1) * count]
+    return total
 
 
 def spread_kernel(parts, out, cases_buf, buf, sems):
@@ -327,10 +339,9 @@
     copy.wait()
 
 
-def near(columns, after):
-    width, sep_width = columns.shape
-    half = jax.ShapeDtypeStruct((width, sep_width // 2), BF16)
-    return call(near_kernel, half, VMEM, [HBM] * 2, [DMA], 4, columns, after)
+def near(columns, count, after):
+    out = jax.ShapeDtypeStruct((columns.shape[0], count), BF16)
+    return call(near_kernel, out, VMEM, [HBM] * 2, [DMA], 4, columns, after)
 
 
 def coupled_product(low, high, delta):
@@ -378,16 +389,13 @@
 
 
 def end_kernel(
-    first, delta, low, sep_in, columns_in, inverse_in, mixed_in, out, sep_out,
-    high, inverse, mixed, state, in_sems, out_sems,
+    first, delta, columns, sep_in, inverse_in, mixed_in, out, sep_out, inverse, mixed, state, in_sems, out_sems
 ):
-    waits = fetch((columns_in.at[:, low.shape[1] :], inverse_in, mixed_in), (high, inverse, mixed), in_sems)
+    waits = fetch((inverse_in, mixed_in), (inverse, mixed), in_sems)
     sep_out[...] = sep_in[...] + own_rows(first, delta, sep_out.shape[0])
-    back, rest = coupled_product(low, high, delta)
-    waits[0].wait()
-    back = (back + rest()).astype(BF16)
-    waits[1].wait()
-    waits[2].wait()
+    back = dot(columns[...], delta[...].astype(BF16)).astype(BF16)
+    for wait in waits:
+        wait.wait()
     count = out_sems.shape[0]
     rows = state.shape[0] // count
     copies = []
@@ -412,7 +420,7 @@
     first = rows is None
     if first:
         sent = (NZ, group + packed.shape[1], BLOCK)
-        parts = call(pack_sum_kernel, far(sent), HBM, [VMEM] * 2, [pltpu.VMEM(sent, F32), DMA], 8, parts, packed)
+        parts = call(pack_sum_kernel, f32(*sent), VMEM, [VMEM] * 2, [], 8, parts, packed)
     else:
         local_t = lax.dynamic_update_slice_in_dim(jnp.zeros((BLOCK, cases), F32), local, place, 0).T
         parts = call(sum_rows_kernel, f32(NZ, group, BLOCK), VMEM, [VMEM] * 2, [], 8, parts, local_t)
@@ -435,7 +443,7 @@
         4,
         delta,
     )
-    low = near(columns, delta)
+    low = near(columns, columns.shape[1] // (2 if first else 1), delta)
     if first:
         rows = list(reorder(owner, *rows, delta))
     return exchange(delta, ("x", "y")).reshape(NXY * BLOCK, cases), rows, low
@@ -483,10 +491,10 @@
         end_kernel,
         [far((width, cases)), f32(owned, cases)],
         [HBM, VMEM],
-        [SMEM] + [VMEM] * 3 + [HBM] * 3,
-        [high, square, state, state, DMA((3,)), DMA((2,))],
+        [SMEM] + [VMEM] * 3 + [HBM] * 2,
+        [square, state, state, DMA((2,)), DMA((2,))],
         MIDDLE_MIB,
-        first, delta, low, sep_rows, columns, leaf_inverse, mixed,
+        first, delta, low, sep_rows, leaf_inverse, mixed,
     )
 
 

time: 214 us -> 211 us (0.986)
  Pallas kernels: 35.9 us -> 33.3 us
    pallas_call x15, Pallas kernels: 35.9 us -> 33.3 us  [call(): pl.pallas_call(kernel, out_shape=out_shape, out_specs=out_specs, in_specs...]
where the time goes in v5:
time: 211 us; the launch traced here: 209 us
  blocking collectives  102 us (48%)
  waiting for transfers between devices  35.1 us (17%)
  starting transfers between devices  34.8 us (16%)
  Pallas kernels  33.3 us (16%)
    all_to_all x5, blocking collectives, exchange(): return lax.all_to_all(parts, axes, 0, 0, tiled=True)  100 us
    all_to_all x5, waiting for transfers between devices, exchange(): return lax.all_to_all(parts, axes, 0, 0, tiled=True)  35.1 us
    pallas_call x15, Pallas kernels, call(): pl.pallas_call(kernel, out_shape=out_shape, out_specs=out_specs, in_specs...  33.3 us
    all_to_all x5, starting transfers between devices, exchange(): return lax.all_to_all(parts, axes, 0, 0, tiled=True)  32.9 us
  transfers between devices with their start and end apart: 6, of which 5 were waited for; matrix products, arithmetic and copies ran while one was open for 1% of the time, Pallas kernels for 8%

profile of v5, /device:TPU:6, one launch (start us, length us, event | category | flops | bytes accessed | tf_op | source)
XLA Modules:
  0.0 209.2 jit_solution(9530543541104071910)
XLA Ops:
  0.6 3.4 %shard_map.113 = (f32[512,128]{1,0:T(8,128)}, f32[16,128,128]{2,1,0:T(8,128)}) custom-call(s32[1]{0:T(128)} %bitcast.first, s32[1,16]{1,0:T(1,128)} %mask_in.3, bf16[512,512]{1,0:T(8,128)(2,1)} %inverse_in.5, f32[512,128]{1,0:T(8,128)} %load_in.3, s32[1,2048]{1,0:T(1,128)} %bitcast.18, f32[8,128]{1,0:T(8,128)} %sep_in.1, bf16[512,2048]{1,0:T(8,128)(2,1)} %coupling_in.3), custom_call_target="tpu_custom_call" | custom-call | tf_op jit(solution)/shard_map/pallas_call | solution.py:43
  4.1 9.4 %all-to-all-start = ((f32[16,128,128]{2,1,0:T(8,128)}), f32[16,128,128]{2,1,0:T(8,128)S(1)}, u32[]{:S(2)}, u32[]{:S(2)}) async-start(f32[16,128,128]{2,1,0:T(8,128)} %get-tuple-element.14), calls=%async_computation | async-start | bytes 2097152 | tf_op jit(solution)/shard_map/all_to_all | solution.py:413
  13.4 9.5 %shard_map.114 = (bf16[512,2048]{1,0:T(8,128)(2,1)}, f32[2,32,128]{2,1,0:T(8,128)S(1)}) custom-call(s32[1,16]{1,0:T(1,128)} %mask_in.3, s32[1,2048]{1,0:T(1,128)} %bitcast.19, f32[4,2048]{1,0:T(4,128)} %own_in.1, bf16[512,2048]{1,0:T(8,128)(2,1)} %coupling_in.3, f32[512,128]{1,0:T(8,128)} %get-tuple-element.15.after.solved_in), custom_call_target="tpu_custom_call" | custom-call | tf_op jit(solution)/shard_map/pallas_call | solution.py:43
  23.0 3.8 %all-to-all-done.parts = f32[16,128,128]{2,1,0:T(8,128)S(1)} async-done(((f32[16,128,128]{2,1,0:T(8,128)}), f32[16,128,128]{2,1,0:T(8,128)S(1)}, u32[]{:S(2)}, u32[]{:S(2)}) %all-to-all-start) | async-done | bytes 1048608 | tf_op jit(solution)/shard_map/all_to_all | solution.py:413
  26.8 36.7 %all_to_all.50.parts.mine = f32[16,48,128]{2,1,0:T(8,128)S(1)} all-to-all(f32[16,48,128]{2,1,0:T(8,128)S(1)} %shard_map.115), channel_id=1, replica_groups=mesh['x'=4,'y'=4,'z'=16,'c'=2] {'z'}, dimensions={0} | all-to-all | bytes 786432 | tf_op jit(solution)/shard_map/all_to_all | solution.py:413
  64.1 1.9 collective-permute-start
  66.0 6.4 %all-to-all-start.2 = ((f32[16,16,128]{2,1,0:T(8,128)}), f32[16,16,128]{2,1,0:T(8,128)S(1)}, u32[]{:S(2)}, u32[]{:S(2)}) async-start(f32[16,16,128]{2,1,0:T(8,128)} %shard_map.116), calls=%async_computation.2 | async-start | bytes 262144 | tf_op jit(solution)/shard_map/all_to_all | solution.py:413
  72.4 5.9 %all-to-all-done.2.rhs = f32[16,16,128]{2,1,0:T(8,128)S(1)} async-done(((f32[16,16,128]{2,1,0:T(8,128)}), f32[16,16,128]{2,1,0:T(8,128)S(1)}, u32[]{:S(2)}, u32[]{:S(2)}) %all-to-all-start.2) | async-done | bytes 131104 | tf_op jit(solution)/shard_map/all_to_all | solution.py:413
  79.1 18.7 %all_to_all.51.parts = f32[16,8,128]{2,1,0:T(8,128)S(1)} all-to-all(f32[16,8,128]{2,1,0:T(8,128)S(1)} %shard_map.117), channel_id=1, replica_groups=mesh['x'=4,'y'=4,'z'=16,'c'=2] {'z'}, dimensions={0} | all-to-all | bytes 131072 | tf_op jit(solution)/shard_map/all_to_all | solution.py:413
  99.1 5.7 %all-to-all-start.4 = ((f32[16,128,128]{2,1,0:T(8,128)}), f32[16,128,128]{2,1,0:T(8,128)S(1)}, u32[]{:S(2)}, u32[]{:S(2)}) async-start(f32[16,128,128]{2,1,0:T(8,128)} %shard_map.118.after), calls=%async_computation.4 | async-start | bytes 2097152 | tf_op jit(solution)/shard_map/all_to_all | solution.py:413
  106.2 3.9 %shard_map.120 = (f32[16,32,128]{2,1,0:T(8,128)S(1)}, f32[16,32,128]{2,1,0:T(8,128)S(1)}, f32[8,128]{1,0:T(8,128)S(1)}) custom-call(s32[1,2048]{1,0:T(1,128)} %bitcast.20, f32[16,48,128]{2,1,0:T(8,128)S(1)} %all_to_all.50.parts.mine, f32[16,48,128]{2,1,0:T(8,128)S(1)} %collective-permute-done.other, f32[16,128,128]{2,1,0:T(8,128)} %shard_map.118.after), custom_call_target="tpu_custom_call" | custom-call | tf_op jit(solution)/shard_map/pallas_call | solution.py:43
  110.8 7.0 %all-to-all-done.4 = f32[16,128,128]{2,1,0:T(8,128)S(1)} async-done(((f32[16,128,128]{2,1,0:T(8,128)}), f32[16,128,128]{2,1,0:T(8,128)S(1)}, u32[]{:S(2)}, u32[]{:S(2)}) %all-to-all-start.4) | async-done | bytes 1048608 | tf_op jit(solution)/shard_map/all_to_all | solution.py:413
  117.8 5.0 %shard_map.121 = (f32[512,128]{1,0:T(8,128)}, f32[16,128,128]{2,1,0:T(8,128)}, f32[8,128]{1,0:T(8,128)S(1)}) custom-call(s32[1]{0:T(128)} %bitcast.first, f32[2048,128]{1,0:T(8,128)S(1)} %bitcast.14, f32[512,1]{1,0:T(8,128)S(1)} %copy.17.cubic, bf16[512,1024]{1,0:T(8,128)(2,1)S(1)} %shard_map.119.low, f32[8,128]{1,0:T(8,128)S(1)} %get-tuple-element.20.after, ...), custom_call_target="tpu_custom_call" | custom-call | tf_op jit(solution)/shard_map/pallas_call | solution.py:43
  122.9 5.7 %all-to-all-start.5 = ((f32[16,128,128]{2,1,0:T(8,128)}), f32[16,128,128]{2,1,0:T(8,128)S(1)}, u32[]{:S(2)}, u32[]{:S(2)}) async-start(f32[16,128,128]{2,1,0:T(8,128)} %get-tuple-element.21), calls=%async_computation.5 | async-start | bytes 2097152 | tf_op jit(solution)/shard_map/all_to_all | solution.py:413
  128.8 1.9 all-gather
  130.6 1.8 fusion
  132.9 8.9 %all-to-all-done.5.parts = f32[16,128,128]{2,1,0:T(8,128)S(1)} async-done(((f32[16,128,128]{2,1,0:T(8,128)}), f32[16,128,128]{2,1,0:T(8,128)S(1)}, u32[]{:S(2)}, u32[]{:S(2)}) %all-to-all-start.5) | async-done | bytes 1048608 | tf_op jit(solution)/shard_map/all_to_all | solution.py:413
  141.9 16.9 %all_to_all.52.parts = f32[16,16,128]{2,1,0:T(8,128)S(1)} all-to-all(f32[16,16,128]{2,1,0:T(8,128)S(1)} %shard_map.122), channel_id=1, replica_groups=mesh['x'=4,'y'=4,'z'=16,'c'=2] {'z'}, dimensions={0} | all-to-all | bytes 262144 | tf_op jit(solution)/shard_map/all_to_all | solution.py:413
  158.8 11.5 %all_to_all.53.rhs = f32[16,16,128]{2,1,0:T(8,128)S(1)} all-to-all(f32[16,16,128]{2,1,0:T(8,128)S(1)} %shard_map.123), channel_id=1, replica_groups=mesh['x'=4,'y'=4,'z'=16,'c'=2] {'x','y'}, dimensions={0} | all-to-all | bytes 262144 | tf_op jit(solution)/shard_map/all_to_all | solution.py:413
  171.0 16.4 %all_to_all.54.parts = f32[16,8,128]{2,1,0:T(8,128)S(1)} all-to-all(f32[16,8,128]{2,1,0:T(8,128)S(1)} %shard_map.124), channel_id=1, replica_groups=mesh['x'=4,'y'=4,'z'=16,'c'=2] {'z'}, dimensions={0} | all-to-all | bytes 131072 | tf_op jit(solution)/shard_map/all_to_all | solution.py:413
  188.7 5.7 %all-to-all-start.9 = ((f32[16,128,128]{2,1,0:T(8,128)}), f32[16,128,128]{2,1,0:T(8,128)S(1)}, u32[]{:S(2)}, u32[]{:S(2)}) async-start(f32[16,128,128]{2,1,0:T(8,128)} %shard_map.125.after), calls=%async_computation.9 | async-start | bytes 2097152 | tf_op jit(solution)/shard_map/all_to_all | solution.py:413
  194.4 1.6 shard_map.126.columns
  196.0 9.5 %all-to-all-done.9 = f32[16,128,128]{2,1,0:T(8,128)S(1)} async-done(((f32[16,128,128]{2,1,0:T(8,128)}), f32[16,128,128]{2,1,0:T(8,128)S(1)}, u32[]{:S(2)}, u32[]{:S(2)}) %all-to-all-start.9) | async-done | bytes 1048608 | tf_op jit(solution)/shard_map/all_to_all | solution.py:413
  205.5 3.5 %shard_map.127 = (f32[512,128]{1,0:T(8,128)}, f32[8,128]{1,0:T(8,128)}) custom-call(s32[1]{0:T(128)} %bitcast.first, f32[2048,128]{1,0:T(8,128)S(1)} %bitcast.16, bf16[512,2048]{1,0:T(8,128)(2,1)S(1)} %shard_map.126.columns, f32[8,128]{1,0:T(8,128)S(1)} %get-tuple-element.24.sep_in, bf16[512,512]{1,0:T(8,128)(2,1)} %inverse_in.5, ...), custom_call_target="tpu_custom_call" | custom-call | tf_op jit(solution)/shard_map/pallas_call | solution.py:43
  (25 shorter events, 7.6 us)
Async XLA Ops:
  4.1 22.7 %all-to-all-start = ((f32[16,128,128]{2,1,0:T(8,128)}), f32[16,128,128]{2,1,0:T(8,128)S(1)}, u32[]{:S(2)}, u32[]{:S(2)}) async-start(f32[16,128,128]{2,1,0:T(8,128)} %get-tuple-element.14), calls=%async_computation | async-start | bytes 2097152 | tf_op jit(solution)/shard_map/all_to_all | solution.py:413
  64.1 14.2 %collective-permute-start = (f32[16,48,128]{2,1,0:T(8,128)S(1)}, f32[16,48,128]{2,1,0:T(8,128)S(1)}, u32[]{:S(2)}, u32[]{:S(2)}) collective-permute-start(f32[16,48,128]{2,1,0:T(8,128)S(1)} %all_to_all.50.parts.mine), channel_id=1, source_target_pairs={{0,1},{1,0},{2,3},{3,2},{4,5},{5,4},{6,7},{7,6},{8,9},{9,8},{10,11... | collective-permute-start | bytes 1179656 | tf_op jit(solution)/shard_map/ppermute | solution.py:431
  66.0 12.2 %all-to-all-start.2 = ((f32[16,16,128]{2,1,0:T(8,128)}), f32[16,16,128]{2,1,0:T(8,128)S(1)}, u32[]{:S(2)}, u32[]{:S(2)}) async-start(f32[16,16,128]{2,1,0:T(8,128)} %shard_map.116), calls=%async_computation.2 | async-start | bytes 262144 | tf_op jit(solution)/shard_map/all_to_all | solution.py:413
  78.3 26.5 %copy-start.4 = (f32[512]{0:T(512)S(1)}, f32[512]{0:T(512)}, u32[]{:S(2)}) copy-start(f32[512]{0:T(512)} %param.13) | copy-start | bytes 6148
  99.1 18.8 %all-to-all-start.4 = ((f32[16,128,128]{2,1,0:T(8,128)}), f32[16,128,128]{2,1,0:T(8,128)S(1)}, u32[]{:S(2)}, u32[]{:S(2)}) async-start(f32[16,128,128]{2,1,0:T(8,128)} %shard_map.118.after), calls=%async_computation.4 | async-start | bytes 2097152 | tf_op jit(solution)/shard_map/all_to_all | solution.py:413
  110.1 0.7 copy-start
  122.9 5.8 %copy-start.3 = (f32[8,128]{1,0:T(8,128)S(1)}, f32[8,128]{1,0:T(8,128)}, u32[]{:S(2)}) copy-start(f32[8,128]{1,0:T(8,128)} %sep_in.1) | copy-start | bytes 12292
  122.9 5.9 %copy-start.2 = (f32[4,2048]{1,0:T(4,128)S(1)}, f32[4,2048]{1,0:T(4,128)}, u32[]{:S(2)}) copy-start(f32[4,2048]{1,0:T(4,128)} %param.16) | copy-start | bytes 98308
  122.9 18.9 %all-to-all-start.5 = ((f32[16,128,128]{2,1,0:T(8,128)}), f32[16,128,128]{2,1,0:T(8,128)S(1)}, u32[]{:S(2)}, u32[]{:S(2)}) async-start(f32[16,128,128]{2,1,0:T(8,128)} %get-tuple-element.21), calls=%async_computation.5 | async-start | bytes 2097152 | tf_op jit(solution)/shard_map/all_to_all | solution.py:413
  128.6 41.6 %copy-start.1 = (f32[16,32,128]{2,1,0:T(8,128)S(1)}, f32[16,32,128]{2,1,0:T(8,128)}, u32[]{:S(2)}) copy-start(f32[16,32,128]{2,1,0:T(8,128)} %copy-done) | copy-start | bytes 786436
  188.7 16.8 %all-to-all-start.9 = ((f32[16,128,128]{2,1,0:T(8,128)}), f32[16,128,128]{2,1,0:T(8,128)S(1)}, u32[]{:S(2)}, u32[]{:S(2)}) async-start(f32[16,128,128]{2,1,0:T(8,128)} %shard_map.125.after), calls=%async_computation.9 | async-start | bytes 2097152 | tf_op jit(solution)/shard_map/all_to_all | solution.py:413

commit v6 on v5

--- a/solution.py
+++ b/solution.py
@@ -157,7 +157,7 @@
 
 
 def permute_kernel(
-    mask_in, owner_in, own_in, coupling_in, after, columns_out, packed,
+    mask_in, owner_in, own_in, coupling_in, after, columns_out, columns_again, packed,
     mask, owner, own, coupling, columns, in_sems, out_sems,
 ):
     waits = fetch((mask_in, owner_in, own_in, coupling_in), (mask, owner, own, coupling), in_sems)
@@ -171,9 +171,10 @@
         cols = pl.ds(tile * TILE, TILE)
         pick = picks(owner, tile, TILE)
         columns[:, cols] = dot(coupling[...], pick).astype(BF16)
-        copy = pltpu.make_async_copy(columns.at[:, cols], columns_out.at[:, cols], out_sems.at[tile])
-        copy.start()
-        copies.append(copy)
+        for i, out in enumerate((columns_out, columns_again)):
+            copy = pltpu.make_async_copy(columns.at[:, cols], out.at[:, cols], out_sems.at[i, tile])
+            copy.start()
+            copies.append(copy)
         rows = rows + lax.dot_general(
             terms[:, tile * TILE : (tile + 1) * TILE], pick, (((1,), (1,)), ((), ())), preferred_element_type=F32
         )
@@ -188,8 +189,8 @@
 def permute(mask, owner, own, coupling, after):
     return call(
         permute_kernel,
-        [far(coupling.shape, BF16), f32(SPLIT, NXY * PART, BLOCK)],
-        [HBM, VMEM],
+        [far(coupling.shape, BF16)] * 2 + [f32(SPLIT, NXY * PART, BLOCK)],
+        [HBM, HBM, VMEM],
         [HBM] * 5,
         [
             pltpu.SMEM(mask.shape, jnp.int32),
@@ -198,7 +199,7 @@
             pltpu.VMEM(coupling.shape, BF16),
             pltpu.VMEM(coupling.shape, BF16),
             DMA((4,)),
-            DMA((coupling.shape[1] // TILE,)),
+            DMA((2, coupling.shape[1] // TILE)),
         ],
         PERMUTE_MIB,
         mask, owner, own, coupling, after,
@@ -268,7 +269,7 @@
         out[z, group:] = packed[z % SPLIT]
 
 
-def sum_rows_kernel(parts, local_t, out):
+def sum_rows_kernel(parts, local_t, after, out):
     total = local_t[...] - jnp.sum(parts[...], axis=0)
     for z in range(NZ):
         out[z] = case_group(total, z)
@@ -318,35 +319,18 @@
     return total
 
 
-def spread_kernel(parts, out, cases_buf, buf, sems):
+def unpacked(parts, cases_buf):
     half = parts.shape[1]
     low = lax.broadcasted_iota(jnp.int32, (half, BLOCK), 1) % (2 * PART) < PART
     for i in range(NZ // SPLIT):
         even, odd = parts[SPLIT * i], parts[SPLIT * i + 1]
         cases_buf[2 * half * i : 2 * half * i + half] = jnp.where(low, even, pltpu.roll(odd, PART, 1))
         cases_buf[2 * half * i + half : 2 * half * (i + 1)] = jnp.where(low, pltpu.roll(even, BLOCK - PART, 1), odd)
-    buf[...] = cases_buf[...].T
-    copies = [pltpu.make_async_copy(buf, out.at[i], sems.at[i]) for i in range(NXY)]
-    for copy in copies:
-        copy.start()
-    for copy in copies:
-        copy.wait()
-
-
-def near_kernel(columns, after, out, sem):
-    copy = pltpu.make_async_copy(columns.at[:, : out.shape[1]], out, sem)
-    copy.start()
-    copy.wait()
-
-
-def near(columns, count, after):
-    out = jax.ShapeDtypeStruct((columns.shape[0], count), BF16)
-    return call(near_kernel, out, VMEM, [HBM] * 2, [DMA], 4, columns, after)
-
-
-def coupled_product(low, high, delta):
-    half = low.shape[1]
-    return dot(low[...], delta[:half, :].astype(BF16)), lambda: dot(high[...], delta[half:, :].astype(BF16))
+    return cases_buf[...].T
+
+
+def spread_kernel(parts, out, cases_buf):
+    out[...] = jnp.broadcast_to(unpacked(parts, cases_buf)[None], out.shape)
 
 
 def own_rows(first, delta, count):
@@ -354,48 +338,31 @@
 
 
 def middle_kernel(
-    first, delta, cubic, low, after, columns_in, inverse_in, solved_in, matrix_in, load_in, state_out, contrib, sep_out,
-    high, inverse, solved, matrix, load, mixed, part_buf, in_sems, out_sem, part_sems,
+    first, delta, cubic_row, columns, inverse, solved, matrix, load, mixed_out, contrib, sep_out,
+    mixed, part_buf, mixed_sem, part_sems,
 ):
-    half = low.shape[1]
-    waits = fetch(
-        (columns_in.at[:, half:], inverse_in, solved_in, matrix_in, load_in),
-        (high, inverse, solved, matrix, load),
-        in_sems,
-    )
     sep_out[...] = own_rows(first, delta, sep_out.shape[0])
-    coupled, rest = coupled_product(low, high, delta)
-    waits[0].wait()
-    coupled = coupled + rest()
-    waits[1].wait()
-    waits[2].wait()
+    cubic = jnp.broadcast_to(cubic_row[...], (8, cubic_row.shape[1])).T[:, :1]
+    coupled = dot(columns[...], delta[...].astype(BF16))
     state = solved[...] - dot(inverse[...], coupled.astype(BF16))
-    waits[3].wait()
-    waits[4].wait()
     resid = load[...] - dot(matrix[...], state.astype(BF16)) - coupled
-    resid = resid - cubic[...] * state * state * state
+    resid = resid - cubic * state * state * state
     mixed[...] = state + dot(inverse[...], resid.astype(BF16))
-    copies = [pltpu.make_async_copy(mixed, state_out, out_sem)]
-    copies[0].start()
     mixed_t = mixed[...].T.astype(BF16)
     count = part_sems.shape[0]
-    size = 2 * half // count
+    size = columns.shape[1] // count
+    copies = [pltpu.make_async_copy(mixed, mixed_out, mixed_sem)]
+    copies[0].start()
     for i in range(count):
-        source, at = (low, i) if i < count // 2 else (high, i - count // 2)
-        part = dot(mixed_t, source[:, at * size : (at + 1) * size])
+        part = dot(mixed_t, columns[:, i * size : (i + 1) * size])
         copies.append(send_tile(part, i, part_buf, contrib, part_sems))
     for copy in copies:
         copy.wait()
 
 
-def end_kernel(
-    first, delta, columns, sep_in, inverse_in, mixed_in, out, sep_out, inverse, mixed, state, in_sems, out_sems
-):
-    waits = fetch((inverse_in, mixed_in), (inverse, mixed), in_sems)
+def end_kernel(first, delta, sep_in, columns, inverse, mixed, out, sep_out, state, out_sems):
     sep_out[...] = sep_in[...] + own_rows(first, delta, sep_out.shape[0])
     back = dot(columns[...], delta[...].astype(BF16)).astype(BF16)
-    for wait in waits:
-        wait.wait()
     count = out_sems.shape[0]
     rows = state.shape[0] // count
     copies = []
@@ -413,7 +380,7 @@
     return lax.all_to_all(parts, axes, 0, 0, tiled=True)
 
 
-def correction(contrib, local, place, core, packed, rows, owner, columns):
+def correction(contrib, local, place, core, packed, rows, owner):
     cases = contrib.shape[1]
     group = cases * SPLIT // NZ
     parts = exchange(contrib, ("x", "y"))
@@ -423,7 +390,8 @@
         parts = call(pack_sum_kernel, f32(*sent), VMEM, [VMEM] * 2, [], 8, parts, packed)
     else:
         local_t = lax.dynamic_update_slice_in_dim(jnp.zeros((BLOCK, cases), F32), local, place, 0).T
-        parts = call(sum_rows_kernel, f32(NZ, group, BLOCK), VMEM, [VMEM] * 2, [], 8, parts, local_t)
+        *rows, token = reorder(owner, *rows, contrib)
+        parts = call(sum_rows_kernel, f32(NZ, group, BLOCK), VMEM, [VMEM] * 3, [], 8, parts, local_t, token)
     parts = exchange(parts, "z")
     rhs = call(sum_cases_kernel, f32(NXY, group, BLOCK), VMEM, [VMEM], [], 4, parts)
     if first:
@@ -435,18 +403,9 @@
     )
     delta = exchange(delta, "z")
     delta = call(
-        spread_kernel,
-        far((NXY, BLOCK, cases)),
-        HBM,
-        [VMEM],
-        [pltpu.VMEM((cases, BLOCK), F32), pltpu.VMEM((BLOCK, cases), F32), DMA((NXY,))],
-        4,
-        delta,
-    )
-    low = near(columns, columns.shape[1] // (2 if first else 1), delta)
-    if first:
-        rows = list(reorder(owner, *rows, delta))
-    return exchange(delta, ("x", "y")).reshape(NXY * BLOCK, cases), rows, low
+        spread_kernel, f32(NXY, BLOCK, cases), VMEM, [VMEM], [pltpu.VMEM((cases, BLOCK), F32)], 4, delta
+    )
+    return exchange(delta, ("x", "y")).reshape(NXY * BLOCK, cases), rows
 
 
 def on_device(
@@ -469,32 +428,28 @@
     first = (lax.axis_index(("x", "y", "z")) * owned).astype(jnp.int32)[None]
     owner = owner_map[None, :]
     solved, contrib = start(first, block_mask, leaf_inverse, coupling, leaf_load, owner, sep_load)
-    columns, packed = permute(block_mask, owner, sep_inverse, coupling, solved)
-
-    delta, rows, low = correction(contrib, None, place, core, packed, None, owner, columns)
+    columns, columns_again, packed = permute(block_mask, owner, sep_inverse, coupling, solved)
+
+    delta, rows = correction(contrib, None, place, core, packed, None, owner)
     local = sep_load - jnp.dot(matrix_rows, delta, precision=HIGHEST, preferred_element_type=F32)
-    high = pltpu.VMEM((width, sep_width // 2), BF16)
-    square = pltpu.VMEM(leaf_matrix.shape, BF16)
-    state = pltpu.VMEM((width, cases), F32)
     mixed, contrib, sep_rows = call(
         middle_kernel,
         [far((width, cases)), far((NXY, cases, BLOCK)), f32(owned, cases)],
         [HBM, HBM, VMEM],
-        [SMEM] + [VMEM] * 4 + [HBM] * 5,
-        [high, square, state, square, state, state, pltpu.VMEM((NXY, cases, BLOCK), F32)]
-        + [DMA((5,)), DMA, DMA((OUT_TILES,))],
+        [SMEM] + [VMEM] * 7,
+        [pltpu.VMEM((width, cases), F32), pltpu.VMEM((NXY, cases, BLOCK), F32), DMA, DMA((OUT_TILES,))],
         MIDDLE_MIB,
-        first, delta, cubic_coeff[:, None], low, rows.pop(), columns, leaf_inverse, solved, leaf_matrix, leaf_load,
-    )
-    delta, rows, low = correction(contrib, local, place, core, None, rows, owner, columns)
+        first, delta, cubic_coeff[None, :], columns, leaf_inverse, solved, leaf_matrix, leaf_load,
+    )
+    delta, rows = correction(contrib, local, place, core, None, rows, owner)
     return call(
         end_kernel,
         [far((width, cases)), f32(owned, cases)],
         [HBM, VMEM],
-        [SMEM] + [VMEM] * 3 + [HBM] * 2,
-        [square, state, state, DMA((2,)), DMA((2,))],
+        [SMEM] + [VMEM] * 5,
+        [pltpu.VMEM((width, cases), F32), DMA((2,))],
         MIDDLE_MIB,
-        first, delta, low, sep_rows, leaf_inverse, mixed,
+        first, delta, sep_rows, columns_again, leaf_inverse, mixed,
     )
 
 

time: 211 us -> 207 us (0.981)
  blocking collectives: 102 us -> 140 us
  waiting for transfers between devices: 35.1 us -> 10.7 us
  starting transfers between devices: 34.8 us -> 23.3 us
  Pallas kernels: 33.3 us -> 26 us
    all_to_all x5 -> x7, blocking collectives: 100 us -> 138 us  [exchange(): return lax.all_to_all(parts, axes, 0, 0, tiled=True)]
    all_to_all x5 -> x3, waiting for transfers between devices: 35.1 us -> 10.7 us  [exchange(): return lax.all_to_all(parts, axes, 0, 0, tiled=True)]
    all_to_all x5 -> x3, starting transfers between devices: 32.9 us -> 21.4 us  [exchange(): return lax.all_to_all(parts, axes, 0, 0, tiled=True)]
    pallas_call x15 -> x13, Pallas kernels: 33.3 us -> 26 us  [call(): pl.pallas_call(kernel, out_shape=out_shape, out_specs=out_specs, in_specs...]
  transfers between devices with their start and end apart: 6 -> 4, of which waited for: 5 -> 3; matrix products, arithmetic and copies ran while one was open for 1% -> 2% of each run, Pallas kernels for 8% -> 7%
where the time goes in v6:
time: 207 us; the launch traced here: 206 us
  blocking collectives  140 us (68%)
  Pallas kernels  26 us (13%)
  starting transfers between devices  23.3 us (11%)
  waiting for transfers between devices  10.7 us (5%)
  matrix products  2.44 us (1%)
  local copies, waits for them, and re-layouts  2.14 us (1%)
    all_to_all x7, blocking collectives, exchange(): return lax.all_to_all(parts, axes, 0, 0, tiled=True)  138 us
    pallas_call x13, Pallas kernels, call(): pl.pallas_call(kernel, out_shape=out_shape, out_specs=out_specs, in_specs...  26 us
    all_to_all x3, starting transfers between devices, exchange(): return lax.all_to_all(parts, axes, 0, 0, tiled=True)  21.4 us
    all_to_all x3, waiting for transfers between devices, exchange(): return lax.all_to_all(parts, axes, 0, 0, tiled=True)  10.7 us
  transfers between devices with their start and end apart: 4, of which 3 were waited for; matrix products, arithmetic and copies ran while one was open for 2% of the time, Pallas kernels for 7%

profile of v6, /device:TPU:6, one launch (start us, length us, event | category | flops | bytes accessed | tf_op | source)
XLA Modules:
  0.0 205.8 jit_solution(963830478756629762)
XLA Ops:
  0.6 3.4 %shard_map.113 = (f32[512,128]{1,0:T(8,128)}, f32[16,128,128]{2,1,0:T(8,128)}) custom-call(s32[1]{0:T(128)} %bitcast.first, s32[1,16]{1,0:T(1,128)} %mask_in.3, bf16[512,512]{1,0:T(8,128)(2,1)} %inverse.3, f32[512,128]{1,0:T(8,128)} %load.1, s32[1,2048]{1,0:T(1,128)} %bitcast.19, f32[8,128]{1,0:T(8,128)} %sep_in.1, bf16[512,2048]{1,0:T(8,128)(2,1)} %coupling_in.3), custom_call_target="tpu_custom_call" | custom-call | tf_op jit(solution)/shard_map/pallas_call | solution.py:43
  4.1 9.4 %all-to-all-start = ((f32[16,128,128]{2,1,0:T(8,128)}), f32[16,128,128]{2,1,0:T(8,128)S(1)}, u32[]{:S(2)}, u32[]{:S(2)}) async-start(f32[16,128,128]{2,1,0:T(8,128)} %get-tuple-element.15), calls=%async_computation | async-start | bytes 2097152 | tf_op jit(solution)/shard_map/all_to_all | solution.py:380
  13.4 9.7 %shard_map.114 = (bf16[512,2048]{1,0:T(8,128)(2,1)}, bf16[512,2048]{1,0:T(8,128)(2,1)}, f32[2,32,128]{2,1,0:T(8,128)S(1)}) custom-call(s32[1,16]{1,0:T(1,128)} %mask_in.3, s32[1,2048]{1,0:T(1,128)} %bitcast.20, f32[4,2048]{1,0:T(4,128)} %own_in.1, bf16[512,2048]{1,0:T(8,128)(2,1)} %coupling_in.3, f32[512,128]{1,0:T(8,128)} %get-tuple-element.16.after.solved), custom_call_target="tpu_custom_call" | custom-call | tf_op jit(solution)/shard_map/pallas_call | solution.py:43
  23.1 3.6 %all-to-all-done.parts = f32[16,128,128]{2,1,0:T(8,128)S(1)} async-done(((f32[16,128,128]{2,1,0:T(8,128)}), f32[16,128,128]{2,1,0:T(8,128)S(1)}, u32[]{:S(2)}, u32[]{:S(2)}) %all-to-all-start) | async-done | bytes 1048608 | tf_op jit(solution)/shard_map/all_to_all | solution.py:380
  26.8 36.7 %all_to_all.50.parts.mine = f32[16,48,128]{2,1,0:T(8,128)S(1)} all-to-all(f32[16,48,128]{2,1,0:T(8,128)S(1)} %shard_map.115), channel_id=1, replica_groups=mesh['x'=4,'y'=4,'z'=16,'c'=2] {'z'}, dimensions={0} | all-to-all | bytes 786432 | tf_op jit(solution)/shard_map/all_to_all | solution.py:380
  64.1 1.9 collective-permute-start
  66.1 6.4 %all-to-all-start.2 = ((f32[16,16,128]{2,1,0:T(8,128)}), f32[16,16,128]{2,1,0:T(8,128)S(1)}, u32[]{:S(2)}, u32[]{:S(2)}) async-start(f32[16,16,128]{2,1,0:T(8,128)} %shard_map.116), calls=%async_computation.2 | async-start | bytes 262144 | tf_op jit(solution)/shard_map/all_to_all | solution.py:380
  72.4 5.9 %all-to-all-done.2.rhs = f32[16,16,128]{2,1,0:T(8,128)S(1)} async-done(((f32[16,16,128]{2,1,0:T(8,128)}), f32[16,16,128]{2,1,0:T(8,128)S(1)}, u32[]{:S(2)}, u32[]{:S(2)}) %all-to-all-start.2) | async-done | bytes 131104 | tf_op jit(solution)/shard_map/all_to_all | solution.py:380
  78.4 0.8 shard_map.117
  79.2 18.8 %all_to_all.51.parts = f32[16,8,128]{2,1,0:T(8,128)S(1)} all-to-all(f32[16,8,128]{2,1,0:T(8,128)S(1)} %shard_map.117), channel_id=1, replica_groups=mesh['x'=4,'y'=4,'z'=16,'c'=2] {'z'}, dimensions={0} | all-to-all | bytes 131072 | tf_op jit(solution)/shard_map/all_to_all | solution.py:380
  98.2 18.4 %all_to_all.52 = f32[16,128,128]{2,1,0:T(8,128)S(1)} all-to-all(f32[16,128,128]{2,1,0:T(8,128)S(1)} %shard_map.118), channel_id=1, replica_groups=mesh['x'=4,'y'=4,'z'=16,'c'=2] {'x','y'}, dimensions={0} | all-to-all | bytes 2097152 | tf_op jit(solution)/shard_map/all_to_all | solution.py:380
  116.6 3.6 %shard_map.119 = (f32[512,128]{1,0:T(8,128)}, f32[16,128,128]{2,1,0:T(8,128)}, f32[8,128]{1,0:T(8,128)S(1)}) custom-call(s32[1]{0:T(128)} %bitcast.first, f32[2048,128]{1,0:T(8,128)S(1)} %bitcast.14, f32[1,512]{1,0:T(1,128)S(1)} %bitcast.18, bf16[512,2048]{1,0:T(8,128)(2,1)S(1)} %copy-done.2, bf16[512,512]{1,0:T(8,128)(2,1)S(1)} %copy-done, ...), custom_call_target="tpu_custom_call" | custom-call | tf_op jit(solution)/shard_map/pallas_call | solution.py:43
  120.3 5.7 %all-to-all-start.5 = ((f32[16,128,128]{2,1,0:T(8,128)}), f32[16,128,128]{2,1,0:T(8,128)S(1)}, u32[]{:S(2)}, u32[]{:S(2)}) async-start(f32[16,128,128]{2,1,0:T(8,128)} %get-tuple-element.21.after), calls=%async_computation.5 | async-start | bytes 2097152 | tf_op jit(solution)/shard_map/all_to_all | solution.py:380
  126.0 2.2 %all-gather = f32[2,4,2048]{2,1,0:T(4,128)} all-gather(f32[1,4,2048]{2,1,0:T(4,128)S(1)} %bitcast.22), channel_id=1, replica_groups=mesh['x'=4,'y'=4,'z'=16,'c'=2] {'c'}, dimensions={0}, use_global_device_ids=true | all-gather | bytes 98304 | tf_op jit(solution)/shard_map/all_gather | solution.py:425
  128.2 0.9 reshape.13
  129.1 2.4 %fusion = f32[8,128]{0,1:T(8,128)} fusion(f32[8,128]{0,1:T(8,128)S(1)} %copy.15, f32[2048,128]{1,0:T(8,128)S(1)} %bitcast.15, f32[8,2048]{1,0:T(8,128)S(1)} %reshape.13), kind=kOutput, calls=%fused_computation.1 | convolution fusion | flops 25166848 | bytes 1122304 | tf_op jit(solution)/shard_map/dot_general | solution.py:434
  131.5 1.1 dynamic_update_slice.3
  132.6 3.9 %shard_map.120 = (f32[16,32,128]{2,1,0:T(8,128)S(1)}, f32[16,32,128]{2,1,0:T(8,128)S(1)}, f32[8,128]{1,0:T(8,128)S(1)}) custom-call(s32[1,2048]{1,0:T(1,128)} %bitcast.21, f32[16,48,128]{2,1,0:T(8,128)S(1)} %all_to_all.50.parts.mine, f32[16,48,128]{2,1,0:T(8,128)S(1)} %collective-permute-done.other, f32[16,128,128]{2,1,0:T(8,128)} %get-tuple-element.21.after), custom_call_target="tpu_custom_call" | custom-call | tf_op jit(solution)/shard_map/pallas_call | solution.py:43
  136.6 1.3 all-to-all-done.5.parts
  137.9 17.3 %all_to_all.53.parts = f32[16,16,128]{2,1,0:T(8,128)S(1)} all-to-all(f32[16,16,128]{2,1,0:T(8,128)S(1)} %shard_map.121), channel_id=1, replica_groups=mesh['x'=4,'y'=4,'z'=16,'c'=2] {'z'}, dimensions={0} | all-to-all | bytes 262144 | tf_op jit(solution)/shard_map/all_to_all | solution.py:380
  155.2 12.4 %all_to_all.54.rhs = f32[16,16,128]{2,1,0:T(8,128)S(1)} all-to-all(f32[16,16,128]{2,1,0:T(8,128)S(1)} %shard_map.122), channel_id=1, replica_groups=mesh['x'=4,'y'=4,'z'=16,'c'=2] {'x','y'}, dimensions={0} | all-to-all | bytes 262144 | tf_op jit(solution)/shard_map/all_to_all | solution.py:380
  168.4 16.7 %all_to_all.55.parts = f32[16,8,128]{2,1,0:T(8,128)S(1)} all-to-all(f32[16,8,128]{2,1,0:T(8,128)S(1)} %shard_map.123), channel_id=1, replica_groups=mesh['x'=4,'y'=4,'z'=16,'c'=2] {'z'}, dimensions={0} | all-to-all | bytes 131072 | tf_op jit(solution)/shard_map/all_to_all | solution.py:380
  185.4 17.9 %all_to_all.56 = f32[16,128,128]{2,1,0:T(8,128)S(1)} all-to-all(f32[16,128,128]{2,1,0:T(8,128)S(1)} %shard_map.124), channel_id=1, replica_groups=mesh['x'=4,'y'=4,'z'=16,'c'=2] {'x','y'}, dimensions={0} | all-to-all | bytes 2097152 | tf_op jit(solution)/shard_map/all_to_all | solution.py:380
  203.2 2.4 %shard_map.125 = (f32[512,128]{1,0:T(8,128)}, f32[8,128]{1,0:T(8,128)}) custom-call(s32[1]{0:T(128)} %bitcast.first, f32[2048,128]{1,0:T(8,128)S(1)} %bitcast.16, f32[8,128]{1,0:T(8,128)S(1)} %get-tuple-element.25.sep_in, bf16[512,2048]{1,0:T(8,128)(2,1)S(1)} %copy-done.1, bf16[512,512]{1,0:T(8,128)(2,1)S(1)} %copy-done, f32[512,128]{1,0:T(8,128)S(1)} %copy-done.6), custom_call_target="tpu_custom_call" | custom-call | tf_op jit(solution)/shard_map/pallas_call | solution.py:43
  (30 shorter events, 2.3 us)
Async XLA Ops:
  4.1 22.7 %all-to-all-start = ((f32[16,128,128]{2,1,0:T(8,128)}), f32[16,128,128]{2,1,0:T(8,128)S(1)}, u32[]{:S(2)}, u32[]{:S(2)}) async-start(f32[16,128,128]{2,1,0:T(8,128)} %get-tuple-element.15), calls=%async_computation | async-start | bytes 2097152 | tf_op jit(solution)/shard_map/all_to_all | solution.py:380
  64.1 14.2 %collective-permute-start = (f32[16,48,128]{2,1,0:T(8,128)S(1)}, f32[16,48,128]{2,1,0:T(8,128)S(1)}, u32[]{:S(2)}, u32[]{:S(2)}) collective-permute-start(f32[16,48,128]{2,1,0:T(8,128)S(1)} %all_to_all.50.parts.mine), channel_id=1, source_target_pairs={{0,1},{1,0},{2,3},{3,2},{4,5},{5,4},{6,7},{7,6},{8,9},{9,8},{10,11... | collective-permute-start | bytes 1179656 | tf_op jit(solution)/shard_map/ppermute | solution.py:399
  66.1 12.2 %all-to-all-start.2 = ((f32[16,16,128]{2,1,0:T(8,128)}), f32[16,16,128]{2,1,0:T(8,128)S(1)}, u32[]{:S(2)}, u32[]{:S(2)}) async-start(f32[16,16,128]{2,1,0:T(8,128)} %shard_map.116), calls=%async_computation.2 | async-start | bytes 262144 | tf_op jit(solution)/shard_map/all_to_all | solution.py:380
  78.3 38.3 %copy-start = (bf16[512,512]{1,0:T(8,128)(2,1)S(1)}, bf16[512,512]{1,0:T(8,128)(2,1)}, u32[]{:S(2)}) copy-start(bf16[512,512]{1,0:T(8,128)(2,1)} %inverse.3) | copy-start | bytes 1572868
  78.3 38.3 %copy-start.2 = (bf16[512,2048]{1,0:T(8,128)(2,1)S(1)}, bf16[512,2048]{1,0:T(8,128)(2,1)}, u32[]{:S(2)}) copy-start(bf16[512,2048]{1,0:T(8,128)(2,1)} %get-tuple-element.20.columns) | copy-start | bytes 6291460
  78.3 38.3 %copy-start.3 = (f32[512,128]{1,0:T(8,128)S(1)}, f32[512,128]{1,0:T(8,128)}, u32[]{:S(2)}) copy-start(f32[512,128]{1,0:T(8,128)} %load.1) | copy-start | bytes 786436
  78.3 38.3 %copy-start.4 = (f32[512,128]{1,0:T(8,128)S(1)}, f32[512,128]{1,0:T(8,128)}, u32[]{:S(2)}) copy-start(f32[512,128]{1,0:T(8,128)} %get-tuple-element.16.after.solved) | copy-start | bytes 786436
  78.3 38.3 %copy-start.5 = (bf16[512,512]{1,0:T(8,128)(2,1)S(1)}, bf16[512,512]{1,0:T(8,128)(2,1)}, u32[]{:S(2)}) copy-start(bf16[512,512]{1,0:T(8,128)(2,1)} %matrix.1) | copy-start | bytes 1572868
  78.3 38.3 %copy-start.7 = (f32[512]{0:T(512)S(1)}, f32[512]{0:T(512)}, u32[]{:S(2)}) copy-start(f32[512]{0:T(512)} %param.13) | copy-start | bytes 6148
  120.2 5.7 %copy-start.9 = (f32[8,128]{1,0:T(8,128)S(1)}, f32[8,128]{1,0:T(8,128)}, u32[]{:S(2)}) copy-start(f32[8,128]{1,0:T(8,128)} %sep_in.1) | copy-start | bytes 12292
  120.2 5.8 %copy-start.8 = (f32[4,2048]{1,0:T(4,128)S(1)}, f32[4,2048]{1,0:T(4,128)}, u32[]{:S(2)}) copy-start(f32[4,2048]{1,0:T(4,128)} %param.16) | copy-start | bytes 98308
  120.3 17.6 %all-to-all-start.5 = ((f32[16,128,128]{2,1,0:T(8,128)}), f32[16,128,128]{2,1,0:T(8,128)S(1)}, u32[]{:S(2)}, u32[]{:S(2)}) async-start(f32[16,128,128]{2,1,0:T(8,128)} %get-tuple-element.21.after), calls=%async_computation.5 | async-start | bytes 2097152 | tf_op jit(solution)/shard_map/all_to_all | solution.py:380
  167.6 35.6 %copy-start.1 = (bf16[512,2048]{1,0:T(8,128)(2,1)S(1)}, bf16[512,2048]{1,0:T(8,128)(2,1)}, u32[]{:S(2)}) copy-start(bf16[512,2048]{1,0:T(8,128)(2,1)} %get-tuple-element.26.columns) | copy-start | bytes 6291460
  167.6 35.6 %copy-start.6 = (f32[512,128]{1,0:T(8,128)S(1)}, f32[512,128]{1,0:T(8,128)}, u32[]{:S(2)}) copy-start(f32[512,128]{1,0:T(8,128)} %get-tuple-element.27.mixed) | copy-start | bytes 786436

commit v7 on v6

--- a/solution.py
+++ b/solution.py
@@ -157,12 +157,17 @@
 
 
 def permute_kernel(
-    mask_in, owner_in, own_in, coupling_in, after, columns_out, columns_again, packed,
-    mask, owner, own, coupling, columns, in_sems, out_sems,
+    mask_in, owner_in, own_in, matrix_in, coupling_in, after, columns_out, columns_again, packed, matrix_rows,
+    mask, owner, own, matrix, coupling, columns, in_sems, out_sems,
 ):
-    waits = fetch((mask_in, owner_in, own_in, coupling_in), (mask, owner, own, coupling), in_sems)
+    waits = fetch(
+        (mask_in, owner_in, own_in, matrix_in, coupling_in), (mask, owner, own, matrix, coupling), in_sems
+    )
     for wait in waits:
         wait.wait()
+    matrix_rows[...] = jnp.zeros(matrix_rows.shape, F32)
+    for t in range(NXY):
+        matrix_rows[t, :OWN] = matrix[:, t * BLOCK : (t + 1) * BLOCK]
     masked(mask, coupling)
     terms = join(split3(own[...]))
     rows = jnp.zeros((3 * OWN, owner.shape[1]), F32)
@@ -186,23 +191,24 @@
         copy.wait()
 
 
-def permute(mask, owner, own, coupling, after):
+def permute(mask, owner, own, matrix, coupling, after):
     return call(
         permute_kernel,
-        [far(coupling.shape, BF16)] * 2 + [f32(SPLIT, NXY * PART, BLOCK)],
-        [HBM, HBM, VMEM],
-        [HBM] * 5,
+        [far(coupling.shape, BF16)] * 2 + [f32(SPLIT, NXY * PART, BLOCK), f32(NXY, 2 * OWN, BLOCK)],
+        [HBM, HBM, VMEM, VMEM],
+        [HBM] * 6,
         [
             pltpu.SMEM(mask.shape, jnp.int32),
             pltpu.VMEM(owner.shape, jnp.int32),
             pltpu.VMEM(own.shape, F32),
+            pltpu.VMEM(matrix.shape, F32),
             pltpu.VMEM(coupling.shape, BF16),
             pltpu.VMEM(coupling.shape, BF16),
-            DMA((4,)),
+            DMA((5,)),
             DMA((2, coupling.shape[1] // TILE)),
         ],
         PERMUTE_MIB,
-        mask, owner, own, coupling, after,
+        mask, owner, own, matrix, coupling, after,
     )
 
 
@@ -219,8 +225,8 @@
 
     gather = (left == by_block(right)).astype(BF16)
     scatter = (right == by_block(left)).astype(F32)
-    base = mine.shape[1] - NXY * PART
     for n, source in enumerate((mine, other)):
+        base = source.shape[1] - NXY * PART
         for i in range(NXY // span):
             tile = source[:, base + 8 * i : base + 8 * (i + 1)].reshape(BLOCK, BLOCK)
             for m, term in enumerate(split3(tile)):
@@ -248,11 +254,29 @@
         reorder_kernel,
         [f32(*shape)] * 2 + [f32(8, BLOCK)],
         [VMEM] * 3,
-        [HBM, VMEM, VMEM, HBM],
+        [HBM, VMEM, VMEM, VMEM],
         [pltpu.VMEM(owner.shape, jnp.int32), pltpu.VMEM((6 * NZ * PART, NXY * BLOCK), BF16), DMA],
         PERMUTE_MIB,
         owner, mine, other, after,
     )
+
+
+def local_kernel(core, place, sep, own, other, delta, after, out, rows, buf):
+    first = core[0] == 0
+    for t in range(NXY):
+        mine, swapped = own[t], other[t, : 2 * OWN]
+        low, high = jnp.where(first, mine, swapped), jnp.where(first, swapped, mine)
+        rows[:, t * BLOCK : (t + 1) * BLOCK] = low + pltpu.roll(high, OWN, 0)
+    left = split3(rows[...])
+    total = sep[...]
+    count = total.shape[0]
+    for i, term in enumerate(split3(delta[...])):
+        part = dot(join(left[: 3 - i]), term)
+        for j in range(3 - i):
+            total = total - part[j * count : (j + 1) * count]
+    buf[...] = jnp.zeros(buf.shape, F32)
+    buf[pl.ds(pl.multiple_of(place[0], 8), count), :] = total
+    out[...] = buf[...].T
 
 
 def case_group(total, z):
@@ -280,17 +304,26 @@
     out[...] = jnp.broadcast_to(total[None], out.shape)
 
 
+def sum_send_kernel(parts, matrix_rows, out, send):
+    sum_cases_kernel(parts, out)
+    send[:, : 2 * OWN] = matrix_rows[...]
+    send[:, 2 * OWN :] = parts[:, out.shape[1] :]
+
+
+def row_tile(rows, i):
+    base = rows.shape[1] - NXY * PART
+    return rows[:, base + 8 * i : base + 8 * (i + 1)].reshape(BLOCK, BLOCK)
+
+
 def delta_kernel(core, rhs, mine, other, out):
     cases = rhs.shape[1]
     span = BLOCK // (NZ * PART)
-    base = mine.shape[1] - NXY * PART
     acc_mine = jnp.zeros((span * cases, BLOCK), F32)
     acc_other = jnp.zeros((span * cases, BLOCK), F32)
     for i in range(NXY // span):
         left = split3(rhs[span * i : span * (i + 1)].reshape(span * cases, BLOCK))
-        rows = slice(base + 8 * i, base + 8 * (i + 1))
-        acc_mine = acc_mine + rows_dot(left, mine[:, rows].reshape(BLOCK, BLOCK))
-        acc_other = acc_other + rows_dot(left, other[:, rows].reshape(BLOCK, BLOCK))
+        acc_mine = acc_mine + rows_dot(left, row_tile(mine, i))
+        acc_other = acc_other + rows_dot(left, row_tile(other, i))
     low = lax.broadcasted_iota(jnp.int32, (cases, BLOCK), 1) % 8 < PART
 
     def fold(acc):
@@ -380,32 +413,47 @@
     return lax.all_to_all(parts, axes, 0, 0, tiled=True)
 
 
-def correction(contrib, local, place, core, packed, rows, owner):
+def correction(contrib, core, packed, matrix_rows):
     cases = contrib.shape[1]
     group = cases * SPLIT // NZ
     parts = exchange(contrib, ("x", "y"))
-    first = rows is None
-    if first:
-        sent = (NZ, group + packed.shape[1], BLOCK)
-        parts = call(pack_sum_kernel, f32(*sent), VMEM, [VMEM] * 2, [], 8, parts, packed)
-    else:
-        local_t = lax.dynamic_update_slice_in_dim(jnp.zeros((BLOCK, cases), F32), local, place, 0).T
-        *rows, token = reorder(owner, *rows, contrib)
-        parts = call(sum_rows_kernel, f32(NZ, group, BLOCK), VMEM, [VMEM] * 3, [], 8, parts, local_t, token)
+    sent = f32(NZ, group + packed.shape[1], BLOCK)
+    mine = exchange(call(pack_sum_kernel, sent, VMEM, [VMEM] * 2, [], 8, parts, packed), "z")
+    rhs, send = call(
+        sum_send_kernel,
+        [f32(NXY, group, BLOCK), f32(NZ, 2 * OWN + packed.shape[1], BLOCK)],
+        [VMEM] * 2,
+        [VMEM] * 2,
+        [],
+        4,
+        mine, matrix_rows,
+    )
+    other = lax.ppermute(send, "c", [(0, 1), (1, 0)])
+    return solve(rhs, core, mine, other), mine, other
+
+
+def second_correction(contrib, local_t, core, mine, other, owner):
+    group = contrib.shape[1] * SPLIT // NZ
+    parts = exchange(contrib, ("x", "y"))
+    mine, other, token = reorder(owner, mine, other, local_t)
+    parts = call(sum_rows_kernel, f32(NZ, group, BLOCK), VMEM, [VMEM] * 3, [], 8, parts, local_t, token)
     parts = exchange(parts, "z")
     rhs = call(sum_cases_kernel, f32(NXY, group, BLOCK), VMEM, [VMEM], [], 4, parts)
-    if first:
-        parts, rhs = lax.optimization_barrier((parts, rhs))
-        rows = (parts, lax.ppermute(parts, "c", [(0, 1), (1, 0)]))
+    return solve(rhs, core, mine, other)
+
+
+def solve(rhs, core, mine, other):
+    group = rhs.shape[1]
+    cases = group * NZ // SPLIT
     rhs = exchange(rhs, ("x", "y"))
     delta = call(
-        delta_kernel, f32(NZ, group // SPLIT, BLOCK), VMEM, [SMEM] + [VMEM] * 3, [], 8, core, rhs, *rows
+        delta_kernel, f32(NZ, group // SPLIT, BLOCK), VMEM, [SMEM] + [VMEM] * 3, [], 8, core, rhs, mine, other
     )
     delta = exchange(delta, "z")
     delta = call(
         spread_kernel, f32(NXY, BLOCK, cases), VMEM, [VMEM], [pltpu.VMEM((cases, BLOCK), F32)], 4, delta
     )
-    return exchange(delta, ("x", "y")).reshape(NXY * BLOCK, cases), rows
+    return exchange(delta, ("x", "y")).reshape(NXY * BLOCK, cases)
 
 
 def on_device(
@@ -422,16 +470,16 @@
 ):
     owned, cases = sep_load.shape
     width, sep_width = coupling.shape
-    matrix_rows = lax.all_gather(sep_matrix, "c", axis=0, tiled=True)
     core = lax.axis_index("c").astype(jnp.int32)[None]
-    place = lax.axis_index("z") * owned
+    place = (lax.axis_index("z") * owned).astype(jnp.int32)[None]
     first = (lax.axis_index(("x", "y", "z")) * owned).astype(jnp.int32)[None]
     owner = owner_map[None, :]
     solved, contrib = start(first, block_mask, leaf_inverse, coupling, leaf_load, owner, sep_load)
-    columns, columns_again, packed = permute(block_mask, owner, sep_inverse, coupling, solved)
-
-    delta, rows = correction(contrib, None, place, core, packed, None, owner)
-    local = sep_load - jnp.dot(matrix_rows, delta, precision=HIGHEST, preferred_element_type=F32)
+    columns, columns_again, packed, matrix_rows = permute(
+        block_mask, owner, sep_inverse, sep_matrix, coupling, solved
+    )
+
+    delta, mine, other = correction(contrib, core, packed, matrix_rows)
     mixed, contrib, sep_rows = call(
         middle_kernel,
         [far((width, cases)), far((NXY, cases, BLOCK)), f32(owned, cases)],
@@ -441,7 +489,16 @@
         MIDDLE_MIB,
         first, delta, cubic_coeff[None, :], columns, leaf_inverse, solved, leaf_matrix, leaf_load,
     )
-    delta, rows = correction(contrib, local, place, core, None, rows, owner)
+    local_t = call(
+        local_kernel,
+        f32(cases, BLOCK),
+        VMEM,
+        [SMEM] * 2 + [VMEM] * 4 + [HBM],
+        [pltpu.VMEM((owned, sep_width), F32), pltpu.VMEM((BLOCK, cases), F32)],
+        8,
+        core, place, sep_load, matrix_rows, other, delta, contrib,
+    )
+    delta = second_correction(contrib, local_t, core, mine, other, owner)
     return call(
         end_kernel,
         [far((width, cases)), f32(owned, cases)],

time: 207 us -> 204 us (0.986)
  waiting for transfers between devices: 10.7 us -> 16.8 us
  blocking collectives: 140 us -> 135 us
  matrix products: 2.44 us -> 0 us
  local copies, waits for them, and re-layouts: 2.14 us -> 0.04 us
    all_to_all x3, waiting for transfers between devices: 10.7 us -> 16.8 us  [exchange(): return lax.all_to_all(parts, axes, 0, 0, tiled=True)]
    all_to_all x7, blocking collectives: 138 us -> 135 us  [exchange(): return lax.all_to_all(parts, axes, 0, 0, tiled=True)]
    dot_general x1 -> x0, matrix products: 2.44 us -> none  [on_device(): jnp.dot(matrix_rows, delta, precision=HIGHEST, preferred_element_type=F32)]
    all_gather x1 -> x0, blocking collectives: 2.17 us -> none  [on_device(): matrix_rows = lax.all_gather(sep_matrix, 'c', axis=0, tiled=True)]
    pallas_call x13 -> x14, Pallas kernels: 26 us -> 26.6 us  [call(): pl.pallas_call(kernel, out_shape=out_shape, out_specs=out_specs, in_specs...]
  transfers between devices with their start and end apart: 4 -> 4, of which waited for: 3 -> 3; matrix products, arithmetic and copies ran while one was open for 2% -> 0% of each run, Pallas kernels for 7% -> 7%
where the time goes in v7:
time: 204 us; the launch traced here: 203 us
  blocking collectives  135 us (66%)
  Pallas kernels  26.6 us (13%)
  starting transfers between devices  23.3 us (11%)
  waiting for transfers between devices  16.8 us (8%)
    all_to_all x7, blocking collectives, exchange(): return lax.all_to_all(parts, axes, 0, 0, tiled=True)  135 us
    pallas_call x14, Pallas kernels, call(): pl.pallas_call(kernel, out_shape=out_shape, out_specs=out_specs, in_specs...  26.6 us
    all_to_all x3, starting transfers between devices, exchange(): return lax.all_to_all(parts, axes, 0, 0, tiled=True)  21.4 us
    all_to_all x3, waiting for transfers between devices, exchange(): return lax.all_to_all(parts, axes, 0, 0, tiled=True)  16.8 us
  transfers between devices with their start and end apart: 4, of which 3 were waited for; matrix products, arithmetic and copies ran while one was open for 0% of the time, Pallas kernels for 7%

profile of v7, /device:TPU:6, one launch (start us, length us, event | category | flops | bytes accessed | tf_op | source)
XLA Modules:
  0.0 202.6 jit_solution(12403032965196881488)
XLA Ops:
  0.6 3.4 %shard_map.113 = (f32[512,128]{1,0:T(8,128)}, f32[16,128,128]{2,1,0:T(8,128)}) custom-call(s32[1]{0:T(128)} %bitcast.first, s32[1,16]{1,0:T(1,128)} %mask_in.3, bf16[512,512]{1,0:T(8,128)(2,1)} %inverse.3, f32[512,128]{1,0:T(8,128)} %load.1, s32[1,2048]{1,0:T(1,128)} %bitcast.11, f32[8,128]{1,0:T(8,128)} %sep.1, bf16[512,2048]{1,0:T(8,128)(2,1)} %coupling_in.3), custom_call_target="tpu_custom_call" | custom-call | tf_op jit(solution)/shard_map/pallas_call | solution.py:43
  4.1 9.4 %all-to-all-start = ((f32[16,128,128]{2,1,0:T(8,128)}), f32[16,128,128]{2,1,0:T(8,128)S(1)}, u32[]{:S(2)}, u32[]{:S(2)}) async-start(f32[16,128,128]{2,1,0:T(8,128)} %get-tuple-element.16), calls=%async_computation | async-start | bytes 2097152 | tf_op jit(solution)/shard_map/all_to_all | solution.py:413
  13.4 9.8 %shard_map.114 = (bf16[512,2048]{1,0:T(8,128)(2,1)}, bf16[512,2048]{1,0:T(8,128)(2,1)}, f32[2,32,128]{2,1,0:T(8,128)S(1)}, f32[16,8,128]{2,1,0:T(8,128)S(1)}) custom-call(s32[1,16]{1,0:T(1,128)} %mask_in.3, s32[1,2048]{1,0:T(1,128)} %bitcast.12, f32[4,2048]{1,0:T(4,128)} %own_in.1, f32[4,2048]{1,0:T(4,128)} %matrix_in.1, bf16[512,2048]{1,0:T(8,128)(2,1)} %coupling_in.3, ...), custom_call_target="tpu_custom_call" | custom-call | tf_op jit(solution)/shard_map/pallas_call | solution.py:43
  23.2 3.5 %all-to-all-done.parts = f32[16,128,128]{2,1,0:T(8,128)S(1)} async-done(((f32[16,128,128]{2,1,0:T(8,128)}), f32[16,128,128]{2,1,0:T(8,128)S(1)}, u32[]{:S(2)}, u32[]{:S(2)}) %all-to-all-start) | async-done | bytes 1048608 | tf_op jit(solution)/shard_map/all_to_all | solution.py:413
  26.8 36.7 %all_to_all.50.parts.mine = f32[16,48,128]{2,1,0:T(8,128)S(1)} all-to-all(f32[16,48,128]{2,1,0:T(8,128)S(1)} %shard_map.115), channel_id=1, replica_groups=mesh['x'=4,'y'=4,'z'=16,'c'=2] {'z'}, dimensions={0} | all-to-all | bytes 786432 | tf_op jit(solution)/shard_map/all_to_all | solution.py:413
  63.5 0.7 shard_map.116
  64.2 1.9 collective-permute-start
  66.1 6.4 %all-to-all-start.2 = ((f32[16,16,128]{2,1,0:T(8,128)}), f32[16,16,128]{2,1,0:T(8,128)S(1)}, u32[]{:S(2)}, u32[]{:S(2)}) async-start(f32[16,16,128]{2,1,0:T(8,128)} %get-tuple-element.20), calls=%async_computation.2 | async-start | bytes 262144 | tf_op jit(solution)/shard_map/all_to_all | solution.py:413
  72.4 5.9 %all-to-all-done.2.rhs = f32[16,16,128]{2,1,0:T(8,128)S(1)} async-done(((f32[16,16,128]{2,1,0:T(8,128)}), f32[16,16,128]{2,1,0:T(8,128)S(1)}, u32[]{:S(2)}, u32[]{:S(2)}) %all-to-all-start.2) | async-done | bytes 131104 | tf_op jit(solution)/shard_map/all_to_all | solution.py:413
  78.4 0.8 shard_map.117
  79.2 18.8 %all_to_all.51.parts = f32[16,8,128]{2,1,0:T(8,128)S(1)} all-to-all(f32[16,8,128]{2,1,0:T(8,128)S(1)} %shard_map.117), channel_id=1, replica_groups=mesh['x'=4,'y'=4,'z'=16,'c'=2] {'z'}, dimensions={0} | all-to-all | bytes 131072 | tf_op jit(solution)/shard_map/all_to_all | solution.py:413
  98.0 0.2 shard_map.118
  98.2 18.4 %all_to_all.52 = f32[16,128,128]{2,1,0:T(8,128)S(1)} all-to-all(f32[16,128,128]{2,1,0:T(8,128)S(1)} %shard_map.118), channel_id=1, replica_groups=mesh['x'=4,'y'=4,'z'=16,'c'=2] {'x','y'}, dimensions={0} | all-to-all | bytes 2097152 | tf_op jit(solution)/shard_map/all_to_all | solution.py:413
  116.7 3.6 %shard_map.119 = (f32[512,128]{1,0:T(8,128)}, f32[16,128,128]{2,1,0:T(8,128)}, f32[8,128]{1,0:T(8,128)S(1)}) custom-call(s32[1]{0:T(128)} %bitcast.first, f32[2048,128]{1,0:T(8,128)S(1)} %bitcast.7, f32[1,512]{1,0:T(1,128)S(1)} %bitcast.10, bf16[512,2048]{1,0:T(8,128)(2,1)S(1)} %copy-done.2, bf16[512,512]{1,0:T(8,128)(2,1)S(1)} %copy-done, ...), custom_call_target="tpu_custom_call" | custom-call | tf_op jit(solution)/shard_map/pallas_call | solution.py:43
  120.3 5.7 %all-to-all-start.5 = ((f32[16,128,128]{2,1,0:T(8,128)}), f32[16,128,128]{2,1,0:T(8,128)S(1)}, u32[]{:S(2)}, u32[]{:S(2)}) async-start(f32[16,128,128]{2,1,0:T(8,128)} %get-tuple-element.23.after), calls=%async_computation.5 | async-start | bytes 2097152 | tf_op jit(solution)/shard_map/all_to_all | solution.py:413
  125.9 0.5 shard_map.120.after.local_t
  126.4 3.9 %shard_map.121 = (f32[16,32,128]{2,1,0:T(8,128)S(1)}, f32[16,32,128]{2,1,0:T(8,128)S(1)}, f32[8,128]{1,0:T(8,128)S(1)}) custom-call(s32[1,2048]{1,0:T(1,128)} %bitcast.13, f32[16,48,128]{2,1,0:T(8,128)S(1)} %all_to_all.50.parts.mine, f32[16,40,128]{2,1,0:T(8,128)S(1)} %collective-permute-done.other, f32[128,128]{1,0:T(8,128)S(1)} %shard_map.120.after.local_t), custom_call_target="tpu_custom_call" | custom-call | tf_op jit(solution)/shard_map/pallas_call | solution.py:43
  130.4 7.4 %all-to-all-done.5.parts = f32[16,128,128]{2,1,0:T(8,128)S(1)} async-done(((f32[16,128,128]{2,1,0:T(8,128)}), f32[16,128,128]{2,1,0:T(8,128)S(1)}, u32[]{:S(2)}, u32[]{:S(2)}) %all-to-all-start.5) | async-done | bytes 1048608 | tf_op jit(solution)/shard_map/all_to_all | solution.py:413
  137.9 17.0 %all_to_all.53.parts = f32[16,16,128]{2,1,0:T(8,128)S(1)} all-to-all(f32[16,16,128]{2,1,0:T(8,128)S(1)} %shard_map.122), channel_id=1, replica_groups=mesh['x'=4,'y'=4,'z'=16,'c'=2] {'z'}, dimensions={0} | all-to-all | bytes 262144 | tf_op jit(solution)/shard_map/all_to_all | solution.py:413
  154.9 11.2 %all_to_all.54.rhs = f32[16,16,128]{2,1,0:T(8,128)S(1)} all-to-all(f32[16,16,128]{2,1,0:T(8,128)S(1)} %shard_map.123), channel_id=1, replica_groups=mesh['x'=4,'y'=4,'z'=16,'c'=2] {'x','y'}, dimensions={0} | all-to-all | bytes 262144 | tf_op jit(solution)/shard_map/all_to_all | solution.py:413
  166.1 0.8 shard_map.124
  166.9 16.6 %all_to_all.55.parts = f32[16,8,128]{2,1,0:T(8,128)S(1)} all-to-all(f32[16,8,128]{2,1,0:T(8,128)S(1)} %shard_map.124), channel_id=1, replica_groups=mesh['x'=4,'y'=4,'z'=16,'c'=2] {'z'}, dimensions={0} | all-to-all | bytes 131072 | tf_op jit(solution)/shard_map/all_to_all | solution.py:413
  183.8 16.2 %all_to_all.56 = f32[16,128,128]{2,1,0:T(8,128)S(1)} all-to-all(f32[16,128,128]{2,1,0:T(8,128)S(1)} %shard_map.125), channel_id=1, replica_groups=mesh['x'=4,'y'=4,'z'=16,'c'=2] {'x','y'}, dimensions={0} | all-to-all | bytes 2097152 | tf_op jit(solution)/shard_map/all_to_all | solution.py:413
  200.0 2.4 %shard_map.126 = (f32[512,128]{1,0:T(8,128)}, f32[8,128]{1,0:T(8,128)}) custom-call(s32[1]{0:T(128)} %bitcast.first, f32[2048,128]{1,0:T(8,128)S(1)} %bitcast.9, f32[8,128]{1,0:T(8,128)S(1)} %get-tuple-element.27.sep_in, bf16[512,2048]{1,0:T(8,128)(2,1)S(1)} %copy-done.1, bf16[512,512]{1,0:T(8,128)(2,1)S(1)} %copy-done, f32[512,128]{1,0:T(8,128)S(1)} %copy-done.6), custom_call_target="tpu_custom_call" | custom-call | tf_op jit(solution)/shard_map/pallas_call | solution.py:43
  (23 shorter events, 0.4 us)
Async XLA Ops:
  4.1 22.7 %all-to-all-start = ((f32[16,128,128]{2,1,0:T(8,128)}), f32[16,128,128]{2,1,0:T(8,128)S(1)}, u32[]{:S(2)}, u32[]{:S(2)}) async-start(f32[16,128,128]{2,1,0:T(8,128)} %get-tuple-element.16), calls=%async_computation | async-start | bytes 2097152 | tf_op jit(solution)/shard_map/all_to_all | solution.py:413
  64.2 14.2 %collective-permute-start = (f32[16,40,128]{2,1,0:T(8,128)S(1)}, f32[16,40,128]{2,1,0:T(8,128)S(1)}, u32[]{:S(2)}, u32[]{:S(2)}) collective-permute-start(f32[16,40,128]{2,1,0:T(8,128)S(1)} %get-tuple-element.21), channel_id=1, source_target_pairs={{0,1},{1,0},{2,3},{3,2},{4,5},{5,4},{6,7},{7,6},{8,9},{9,8},{10,11... | collective-permute-start | bytes 983048 | tf_op jit(solution)/shard_map/ppermute | solution.py:431
  66.1 12.2 %all-to-all-start.2 = ((f32[16,16,128]{2,1,0:T(8,128)}), f32[16,16,128]{2,1,0:T(8,128)S(1)}, u32[]{:S(2)}, u32[]{:S(2)}) async-start(f32[16,16,128]{2,1,0:T(8,128)} %get-tuple-element.20), calls=%async_computation.2 | async-start | bytes 262144 | tf_op jit(solution)/shard_map/all_to_all | solution.py:413
  78.3 38.3 %copy-start = (bf16[512,512]{1,0:T(8,128)(2,1)S(1)}, bf16[512,512]{1,0:T(8,128)(2,1)}, u32[]{:S(2)}) copy-start(bf16[512,512]{1,0:T(8,128)(2,1)} %inverse.3) | copy-start | bytes 1572868
  78.3 38.3 %copy-start.2 = (bf16[512,2048]{1,0:T(8,128)(2,1)S(1)}, bf16[512,2048]{1,0:T(8,128)(2,1)}, u32[]{:S(2)}) copy-start(bf16[512,2048]{1,0:T(8,128)(2,1)} %get-tuple-element.22.columns) | copy-start | bytes 6291460
  78.3 38.3 %copy-start.3 = (f32[512,128]{1,0:T(8,128)S(1)}, f32[512,128]{1,0:T(8,128)}, u32[]{:S(2)}) copy-start(f32[512,128]{1,0:T(8,128)} %load.1) | copy-start | bytes 786436
  78.3 38.3 %copy-start.4 = (f32[512,128]{1,0:T(8,128)S(1)}, f32[512,128]{1,0:T(8,128)}, u32[]{:S(2)}) copy-start(f32[512,128]{1,0:T(8,128)} %get-tuple-element.17.after.solved) | copy-start | bytes 786436
  78.3 38.3 %copy-start.5 = (bf16[512,512]{1,0:T(8,128)(2,1)S(1)}, bf16[512,512]{1,0:T(8,128)(2,1)}, u32[]{:S(2)}) copy-start(bf16[512,512]{1,0:T(8,128)(2,1)} %matrix.1) | copy-start | bytes 1572868
  78.3 38.3 %copy-start.8 = (f32[512]{0:T(512)S(1)}, f32[512]{0:T(512)}, u32[]{:S(2)}) copy-start(f32[512]{0:T(512)} %param.13) | copy-start | bytes 6148
  120.2 5.7 %copy-start.7 = (f32[8,128]{1,0:T(8,128)S(1)}, f32[8,128]{1,0:T(8,128)}, u32[]{:S(2)}) copy-start(f32[8,128]{1,0:T(8,128)} %sep.1) | copy-start | bytes 12292
  120.3 17.6 %all-to-all-start.5 = ((f32[16,128,128]{2,1,0:T(8,128)}), f32[16,128,128]{2,1,0:T(8,128)S(1)}, u32[]{:S(2)}, u32[]{:S(2)}) async-start(f32[16,128,128]{2,1,0:T(8,128)} %get-tuple-element.23.after), calls=%async_computation.5 | async-start | bytes 2097152 | tf_op jit(solution)/shard_map/all_to_all | solution.py:413
  166.1 33.9 %copy-start.1 = (bf16[512,2048]{1,0:T(8,128)(2,1)S(1)}, bf16[512,2048]{1,0:T(8,128)(2,1)}, u32[]{:S(2)}) copy-start(bf16[512,2048]{1,0:T(8,128)(2,1)} %get-tuple-element.28.columns) | copy-start | bytes 6291460
  166.1 33.9 %copy-start.6 = (f32[512,128]{1,0:T(8,128)S(1)}, f32[512,128]{1,0:T(8,128)}, u32[]{:S(2)}) copy-start(f32[512,128]{1,0:T(8,128)} %get-tuple-element.29.mixed) | copy-start | bytes 786436

commit v8 on v7

--- a/solution.py
+++ b/solution.py
@@ -91,7 +91,7 @@
 
 
 def start_kernel(
-    first, mask_in, inverse_in, load_in, owner_in, sep_in, coupling_in, solved_out, contrib,
+    first, core, place, mask_in, inverse_in, load_in, owner_in, sep_in, coupling_in, solved_out, contrib,
     mask, inverse, load, owner, sep, coupling, solved, part_buf, in_sems, out_sem, part_sems,
 ):
     waits = fetch(
@@ -131,13 +131,13 @@
         copy.wait()
 
 
-def start(first, mask, inverse, coupling, load, owner, sep):
+def start(scalars, mask, inverse, coupling, load, owner, sep):
     cases = load.shape[1]
     return call(
         start_kernel,
         [far(load.shape), far((NXY, cases, BLOCK))],
         [HBM] * 2,
-        [SMEM] + [HBM] * 6,
+        [SMEM] * 3 + [HBM] * 6,
         [
             pltpu.SMEM(mask.shape, jnp.int32),
             pltpu.VMEM(inverse.shape, BF16),
@@ -152,7 +152,7 @@
             DMA((OUT_TILES,)),
         ],
         START_MIB,
-        first, mask, inverse, load, owner, sep, coupling,
+        *scalars, mask, inverse, load, owner, sep, coupling,
     )
 
 
@@ -315,7 +315,8 @@
     return rows[:, base + 8 * i : base + 8 * (i + 1)].reshape(BLOCK, BLOCK)
 
 
-def delta_kernel(core, rhs, mine, other, out):
+def delta_kernel(core, rhs, mine, other, *after_and_out):
+    out = after_and_out[-1]
     cases = rhs.shape[1]
     span = BLOCK // (NZ * PART)
     acc_mine = jnp.zeros((span * cases, BLOCK), F32)
@@ -429,7 +430,7 @@
         mine, matrix_rows,
     )
     other = lax.ppermute(send, "c", [(0, 1), (1, 0)])
-    return solve(rhs, core, mine, other), mine, other
+    return solve(rhs, core, mine, other, between(rhs)), mine, other
 
 
 def second_correction(contrib, local_t, core, mine, other, owner):
@@ -442,12 +443,35 @@
     return solve(rhs, core, mine, other)
 
 
-def solve(rhs, core, mine, other):
+def between_kernel(rhs, out, sem):
+    copy = pltpu.make_async_copy(rhs.at[0, :8], out, sem)
+    copy.start()
+    copy.wait()
+
+
+def between(rhs):
+    return pl.pallas_call(
+        between_kernel,
+        out_shape=far((8, BLOCK)),
+        in_specs=[HBM],
+        out_specs=HBM,
+        scratch_shapes=[DMA],
+        cost_estimate=pl.CostEstimate(flops=10**10, transcendentals=0, bytes_accessed=8192),
+    )(pltpu.with_memory_space_constraint(rhs, pltpu.HBM))
+
+
+def solve(rhs, core, mine, other, *after):
     group = rhs.shape[1]
     cases = group * NZ // SPLIT
     rhs = exchange(rhs, ("x", "y"))
     delta = call(
-        delta_kernel, f32(NZ, group // SPLIT, BLOCK), VMEM, [SMEM] + [VMEM] * 3, [], 8, core, rhs, mine, other
+        delta_kernel,
+        f32(NZ, group // SPLIT, BLOCK),
+        VMEM,
+        [SMEM] + [VMEM] * 3 + [HBM] * len(after),
+        [],
+        8,
+        core, rhs, mine, other, *after,
     )
     delta = exchange(delta, "z")
     delta = call(
@@ -474,7 +498,7 @@
     place = (lax.axis_index("z") * owned).astype(jnp.int32)[None]
     first = (lax.axis_index(("x", "y", "z")) * owned).astype(jnp.int32)[None]
     owner = owner_map[None, :]
-    solved, contrib = start(first, block_mask, leaf_inverse, coupling, leaf_load, owner, sep_load)
+    solved, contrib = start((first, core, place), block_mask, leaf_inverse, coupling, leaf_load, owner, sep_load)
     columns, columns_again, packed, matrix_rows = permute(
         block_mask, owner, sep_inverse, sep_matrix, coupling, solved
     )

time: 204 us -> 203 us (level)
  waiting for transfers between devices: 16.8 us -> 14.2 us
    all_to_all x3, waiting for transfers between devices: 16.8 us -> 14.2 us  [exchange(): return lax.all_to_all(parts, axes, 0, 0, tiled=True)]
  transfers between devices with their start and end apart: 4 -> 4, of which waited for: 3 -> 3; matrix products, arithmetic and copies ran while one was open for 0% -> 0% of each run, Pallas kernels for 7% -> 8%
where the time goes in v8:
time: 203 us; the launch traced here: 201 us
  blocking collectives  135 us (67%)
  Pallas kernels  27.8 us (14%)
  starting transfers between devices  23.3 us (11%)
  waiting for transfers between devices  14.2 us (7%)
    all_to_all x7, blocking collectives, exchange(): return lax.all_to_all(parts, axes, 0, 0, tiled=True)  135 us
    pallas_call x14, Pallas kernels, call(): pl.pallas_call(kernel, out_shape=out_shape, out_specs=out_specs, in_specs...  26.5 us
    all_to_all x3, starting transfers between devices, exchange(): return lax.all_to_all(parts, axes, 0, 0, tiled=True)  21.4 us
    all_to_all x3, waiting for transfers between devices, exchange(): return lax.all_to_all(parts, axes, 0, 0, tiled=True)  14.2 us
  transfers between devices with their start and end apart: 4, of which 3 were waited for; matrix products, arithmetic and copies ran while one was open for 0% of the time, Pallas kernels for 8%

profile of v8, /device:TPU:6, one launch (start us, length us, event | category | flops | bytes accessed | tf_op | source)
XLA Modules:
  0.0 201.3 jit_solution(247106535435732785)
XLA Ops:
  0.6 3.4 %shard_map.113 = (f32[512,128]{1,0:T(8,128)}, f32[16,128,128]{2,1,0:T(8,128)}) custom-call(s32[1]{0:T(128)} %bitcast.first, s32[1]{0:T(128)} %bitcast.1.core, s32[1]{0:T(128)} %bitcast.2.place, s32[1,16]{1,0:T(1,128)} %mask_in.3, bf16[512,512]{1,0:T(8,128)(2,1)} %inverse.3, f32[512,128]{1,0:T(8,128)} %load.1, s32[1,2048]{1,0:T(1,128)} %bitcast.11, ...), custom_call_target="tpu_custom_call" | custom-call | tf_op jit(solution)/shard_map/pallas_call | solution.py:43
  4.1 9.4 %all-to-all-start = ((f32[16,128,128]{2,1,0:T(8,128)}), f32[16,128,128]{2,1,0:T(8,128)S(1)}, u32[]{:S(2)}, u32[]{:S(2)}) async-start(f32[16,128,128]{2,1,0:T(8,128)} %get-tuple-element.16), calls=%async_computation | async-start | bytes 2097152 | tf_op jit(solution)/shard_map/all_to_all | solution.py:414
  13.4 9.8 %shard_map.114 = (bf16[512,2048]{1,0:T(8,128)(2,1)}, bf16[512,2048]{1,0:T(8,128)(2,1)}, f32[2,32,128]{2,1,0:T(8,128)S(1)}, f32[16,8,128]{2,1,0:T(8,128)S(1)}) custom-call(s32[1,16]{1,0:T(1,128)} %mask_in.3, s32[1,2048]{1,0:T(1,128)} %bitcast.12, f32[4,2048]{1,0:T(4,128)} %own_in.1, f32[4,2048]{1,0:T(4,128)} %matrix_in.1, bf16[512,2048]{1,0:T(8,128)(2,1)} %coupling_in.3, ...), custom_call_target="tpu_custom_call" | custom-call | tf_op jit(solution)/shard_map/pallas_call | solution.py:43
  23.2 3.5 %all-to-all-done.parts = f32[16,128,128]{2,1,0:T(8,128)S(1)} async-done(((f32[16,128,128]{2,1,0:T(8,128)}), f32[16,128,128]{2,1,0:T(8,128)S(1)}, u32[]{:S(2)}, u32[]{:S(2)}) %all-to-all-start) | async-done | bytes 1048608 | tf_op jit(solution)/shard_map/all_to_all | solution.py:414
  26.8 36.7 %all_to_all.50.parts.mine = f32[16,48,128]{2,1,0:T(8,128)S(1)} all-to-all(f32[16,48,128]{2,1,0:T(8,128)S(1)} %shard_map.115), channel_id=1, replica_groups=mesh['x'=4,'y'=4,'z'=16,'c'=2] {'z'}, dimensions={0} | all-to-all | bytes 786432 | tf_op jit(solution)/shard_map/all_to_all | solution.py:414
  63.5 0.7 shard_map.116
  64.2 6.4 %all-to-all-start.2 = ((f32[16,16,128]{2,1,0:T(8,128)}), f32[16,16,128]{2,1,0:T(8,128)S(1)}, u32[]{:S(2)}, u32[]{:S(2)}) async-start(f32[16,16,128]{2,1,0:T(8,128)} %get-tuple-element.20.rhs), calls=%async_computation.2 | async-start | bytes 262144 | tf_op jit(solution)/shard_map/all_to_all | solution.py:414
  70.5 1.9 collective-permute-start
  72.4 1.2 shard_map.117.after_and_out_0_
  73.7 2.6 %all-to-all-done.2.rhs = f32[16,16,128]{2,1,0:T(8,128)S(1)} async-done(((f32[16,16,128]{2,1,0:T(8,128)}), f32[16,16,128]{2,1,0:T(8,128)S(1)}, u32[]{:S(2)}, u32[]{:S(2)}) %all-to-all-start.2) | async-done | bytes 131104 | tf_op jit(solution)/shard_map/all_to_all | solution.py:414
  76.4 0.8 shard_map.118
  77.2 18.7 %all_to_all.51.parts = f32[16,8,128]{2,1,0:T(8,128)S(1)} all-to-all(f32[16,8,128]{2,1,0:T(8,128)S(1)} %shard_map.118), channel_id=1, replica_groups=mesh['x'=4,'y'=4,'z'=16,'c'=2] {'z'}, dimensions={0} | all-to-all | bytes 131072 | tf_op jit(solution)/shard_map/all_to_all | solution.py:414
  96.1 18.7 %all_to_all.52 = f32[16,128,128]{2,1,0:T(8,128)S(1)} all-to-all(f32[16,128,128]{2,1,0:T(8,128)S(1)} %shard_map.119), channel_id=1, replica_groups=mesh['x'=4,'y'=4,'z'=16,'c'=2] {'x','y'}, dimensions={0} | all-to-all | bytes 2097152 | tf_op jit(solution)/shard_map/all_to_all | solution.py:414
  114.8 3.6 %shard_map.120 = (f32[512,128]{1,0:T(8,128)}, f32[16,128,128]{2,1,0:T(8,128)}, f32[8,128]{1,0:T(8,128)S(1)}) custom-call(s32[1]{0:T(128)} %bitcast.first, f32[2048,128]{1,0:T(8,128)S(1)} %bitcast.7, f32[1,512]{1,0:T(1,128)S(1)} %bitcast.10, bf16[512,2048]{1,0:T(8,128)(2,1)S(1)} %copy-done.2, bf16[512,512]{1,0:T(8,128)(2,1)S(1)} %copy-done, ...), custom_call_target="tpu_custom_call" | custom-call | tf_op jit(solution)/shard_map/pallas_call | solution.py:43
  118.4 5.7 %all-to-all-start.5 = ((f32[16,128,128]{2,1,0:T(8,128)}), f32[16,128,128]{2,1,0:T(8,128)S(1)}, u32[]{:S(2)}, u32[]{:S(2)}) async-start(f32[16,128,128]{2,1,0:T(8,128)} %get-tuple-element.23.after), calls=%async_computation.5 | async-start | bytes 2097152 | tf_op jit(solution)/shard_map/all_to_all | solution.py:414
  124.1 0.5 shard_map.121.after.local_t
  124.6 3.9 %shard_map.122 = (f32[16,32,128]{2,1,0:T(8,128)S(1)}, f32[16,32,128]{2,1,0:T(8,128)S(1)}, f32[8,128]{1,0:T(8,128)S(1)}) custom-call(s32[1,2048]{1,0:T(1,128)} %bitcast.13, f32[16,48,128]{2,1,0:T(8,128)S(1)} %all_to_all.50.parts.mine, f32[16,40,128]{2,1,0:T(8,128)S(1)} %collective-permute-done.other, f32[128,128]{1,0:T(8,128)S(1)} %shard_map.121.after.local_t), custom_call_target="tpu_custom_call" | custom-call | tf_op jit(solution)/shard_map/pallas_call | solution.py:43
  128.6 8.0 %all-to-all-done.5.parts = f32[16,128,128]{2,1,0:T(8,128)S(1)} async-done(((f32[16,128,128]{2,1,0:T(8,128)}), f32[16,128,128]{2,1,0:T(8,128)S(1)}, u32[]{:S(2)}, u32[]{:S(2)}) %all-to-all-start.5) | async-done | bytes 1048608 | tf_op jit(solution)/shard_map/all_to_all | solution.py:414
  136.6 16.8 %all_to_all.53.parts = f32[16,16,128]{2,1,0:T(8,128)S(1)} all-to-all(f32[16,16,128]{2,1,0:T(8,128)S(1)} %shard_map.123), channel_id=1, replica_groups=mesh['x'=4,'y'=4,'z'=16,'c'=2] {'z'}, dimensions={0} | all-to-all | bytes 262144 | tf_op jit(solution)/shard_map/all_to_all | solution.py:414
  153.4 11.4 %all_to_all.54.rhs = f32[16,16,128]{2,1,0:T(8,128)S(1)} all-to-all(f32[16,16,128]{2,1,0:T(8,128)S(1)} %shard_map.124), channel_id=1, replica_groups=mesh['x'=4,'y'=4,'z'=16,'c'=2] {'x','y'}, dimensions={0} | all-to-all | bytes 262144 | tf_op jit(solution)/shard_map/all_to_all | solution.py:414
  164.8 0.8 shard_map.125
  165.6 16.6 %all_to_all.55.parts = f32[16,8,128]{2,1,0:T(8,128)S(1)} all-to-all(f32[16,8,128]{2,1,0:T(8,128)S(1)} %shard_map.125), channel_id=1, replica_groups=mesh['x'=4,'y'=4,'z'=16,'c'=2] {'z'}, dimensions={0} | all-to-all | bytes 131072 | tf_op jit(solution)/shard_map/all_to_all | solution.py:414
  182.5 16.2 %all_to_all.56 = f32[16,128,128]{2,1,0:T(8,128)S(1)} all-to-all(f32[16,128,128]{2,1,0:T(8,128)S(1)} %shard_map.126), channel_id=1, replica_groups=mesh['x'=4,'y'=4,'z'=16,'c'=2] {'x','y'}, dimensions={0} | all-to-all | bytes 2097152 | tf_op jit(solution)/shard_map/all_to_all | solution.py:414
  198.7 2.4 %shard_map.127 = (f32[512,128]{1,0:T(8,128)}, f32[8,128]{1,0:T(8,128)}) custom-call(s32[1]{0:T(128)} %bitcast.first, f32[2048,128]{1,0:T(8,128)S(1)} %bitcast.9, f32[8,128]{1,0:T(8,128)S(1)} %get-tuple-element.27.sep_in, bf16[512,2048]{1,0:T(8,128)(2,1)S(1)} %copy-done.1, bf16[512,512]{1,0:T(8,128)(2,1)S(1)} %copy-done, f32[512,128]{1,0:T(8,128)S(1)} %copy-done.6), custom_call_target="tpu_custom_call" | custom-call | tf_op jit(solution)/shard_map/pallas_call | solution.py:43
  (24 shorter events, 0.7 us)
Async XLA Ops:
  4.1 22.7 %all-to-all-start = ((f32[16,128,128]{2,1,0:T(8,128)}), f32[16,128,128]{2,1,0:T(8,128)S(1)}, u32[]{:S(2)}, u32[]{:S(2)}) async-start(f32[16,128,128]{2,1,0:T(8,128)} %get-tuple-element.16), calls=%async_computation | async-start | bytes 2097152 | tf_op jit(solution)/shard_map/all_to_all | solution.py:414
  64.2 12.2 %all-to-all-start.2 = ((f32[16,16,128]{2,1,0:T(8,128)}), f32[16,16,128]{2,1,0:T(8,128)S(1)}, u32[]{:S(2)}, u32[]{:S(2)}) async-start(f32[16,16,128]{2,1,0:T(8,128)} %get-tuple-element.20.rhs), calls=%async_computation.2 | async-start | bytes 262144 | tf_op jit(solution)/shard_map/all_to_all | solution.py:414
  70.5 5.9 %collective-permute-start = (f32[16,40,128]{2,1,0:T(8,128)S(1)}, f32[16,40,128]{2,1,0:T(8,128)S(1)}, u32[]{:S(2)}, u32[]{:S(2)}) collective-permute-start(f32[16,40,128]{2,1,0:T(8,128)S(1)} %get-tuple-element.21), channel_id=1, source_target_pairs={{0,1},{1,0},{2,3},{3,2},{4,5},{5,4},{6,7},{7,6},{8,9},{9,8},{10,11... | collective-permute-start | bytes 983048 | tf_op jit(solution)/shard_map/ppermute | solution.py:432
  73.7 41.1 %copy-start = (bf16[512,512]{1,0:T(8,128)(2,1)S(1)}, bf16[512,512]{1,0:T(8,128)(2,1)}, u32[]{:S(2)}) copy-start(bf16[512,512]{1,0:T(8,128)(2,1)} %inverse.3) | copy-start | bytes 1572868
  73.7 41.1 %copy-start.3 = (f32[512,128]{1,0:T(8,128)S(1)}, f32[512,128]{1,0:T(8,128)}, u32[]{:S(2)}) copy-start(f32[512,128]{1,0:T(8,128)} %load.1) | copy-start | bytes 786436
  73.7 41.1 %copy-start.4 = (f32[512,128]{1,0:T(8,128)S(1)}, f32[512,128]{1,0:T(8,128)}, u32[]{:S(2)}) copy-start(f32[512,128]{1,0:T(8,128)} %get-tuple-element.17.after.solved) | copy-start | bytes 786436
  73.7 41.1 %copy-start.5 = (bf16[512,512]{1,0:T(8,128)(2,1)S(1)}, bf16[512,512]{1,0:T(8,128)(2,1)}, u32[]{:S(2)}) copy-start(bf16[512,512]{1,0:T(8,128)(2,1)} %matrix.1) | copy-start | bytes 1572868
  73.7 41.1 %copy-start.8 = (f32[512]{0:T(512)S(1)}, f32[512]{0:T(512)}, u32[]{:S(2)}) copy-start(f32[512]{0:T(512)} %param.13) | copy-start | bytes 6148
  76.4 38.5 %copy-start.2 = (bf16[512,2048]{1,0:T(8,128)(2,1)S(1)}, bf16[512,2048]{1,0:T(8,128)(2,1)}, u32[]{:S(2)}) copy-start(bf16[512,2048]{1,0:T(8,128)(2,1)} %get-tuple-element.22.columns) | copy-start | bytes 6291460
  118.4 5.7 %copy-start.7 = (f32[8,128]{1,0:T(8,128)S(1)}, f32[8,128]{1,0:T(8,128)}, u32[]{:S(2)}) copy-start(f32[8,128]{1,0:T(8,128)} %sep.1) | copy-start | bytes 12292
  118.4 18.1 %all-to-all-start.5 = ((f32[16,128,128]{2,1,0:T(8,128)}), f32[16,128,128]{2,1,0:T(8,128)S(1)}, u32[]{:S(2)}, u32[]{:S(2)}) async-start(f32[16,128,128]{2,1,0:T(8,128)} %get-tuple-element.23.after), calls=%async_computation.5 | async-start | bytes 2097152 | tf_op jit(solution)/shard_map/all_to_all | solution.py:414
  164.8 33.9 %copy-start.1 = (bf16[512,2048]{1,0:T(8,128)(2,1)S(1)}, bf16[512,2048]{1,0:T(8,128)(2,1)}, u32[]{:S(2)}) copy-start(bf16[512,2048]{1,0:T(8,128)(2,1)} %get-tuple-element.28.columns) | copy-start | bytes 6291460
  164.8 33.9 %copy-start.6 = (f32[512,128]{1,0:T(8,128)S(1)}, f32[512,128]{1,0:T(8,128)}, u32[]{:S(2)}) copy-start(f32[512,128]{1,0:T(8,128)} %get-tuple-element.29.mixed) | copy-start | bytes 786436

commit v9 on v8

--- a/solution.py
+++ b/solution.py
@@ -90,8 +90,29 @@
     return jnp.concatenate([x.astype(F32) for x in terms], axis=0).astype(BF16)
 
 
+def targets(first, owner, own, size):
+    index = lax.broadcasted_iota(jnp.int32, (own, size), 0)
+    target = jnp.zeros((own, size), jnp.int32)
+    for j in range(own):
+        target = jnp.where(index == j, owner[0, first[0] + j], target)
+    return target
+
+
+def part_tile(mixed_t, coupling, mask, terms, target, tile):
+    own, size = target.shape
+    lanes = lax.broadcasted_iota(jnp.int32, (own, size), 1) + tile * size
+    place = (lanes == target).astype(F32)
+    loads = lax.dot_general(terms, join([place] * 3), (((0,), (0,)), ((), ())), preferred_element_type=F32)
+    part = dot(mixed_t, coupling[:, tile * size : (tile + 1) * size])
+    count = size // BLOCK
+    kept = [
+        jnp.where(mask[0, tile * count + i] != 0, part[:, i * BLOCK : (i + 1) * BLOCK], 0.0) for i in range(count)
+    ]
+    return jnp.concatenate(kept, axis=1) - loads
+
+
 def start_kernel(
-    first, core, place, mask_in, inverse_in, load_in, owner_in, sep_in, coupling_in, solved_out, contrib,
+    first, core, mask_in, inverse_in, load_in, owner_in, sep_in, coupling_in, solved_out, contrib,
     mask, inverse, load, owner, sep, coupling, solved, part_buf, in_sems, out_sem, part_sems,
 ):
     waits = fetch(
@@ -107,25 +128,10 @@
     mixed_t = solved[...].T.astype(BF16)
     for wait in waits[:1] + waits[3:]:
         wait.wait()
-    own, sep_width = sep.shape[0], coupling.shape[1]
-    loads_in = join(split3(sep[...]))
-    size = sep_width // part_sems.shape[0]
-    index = lax.broadcasted_iota(jnp.int32, (own, size), 0)
-    target = jnp.zeros((own, size), jnp.int32)
-    for j in range(own):
-        target = jnp.where(index == j, owner[0, first[0] + j], target)
+    terms = join(split3(sep[...]))
+    target = targets(first, owner, sep.shape[0], coupling.shape[1] // part_sems.shape[0])
     for tile in range(part_sems.shape[0]):
-        lanes = lax.broadcasted_iota(jnp.int32, (own, size), 1) + tile * size
-        place = (lanes == target).astype(F32)
-        loads = lax.dot_general(
-            loads_in, join([place] * 3), (((0,), (0,)), ((), ())), preferred_element_type=F32
-        )
-        part = dot(mixed_t, coupling[:, tile * size : (tile + 1) * size])
-        count = size // BLOCK
-        kept = [
-            jnp.where(mask[0, tile * count + i] != 0, part[:, i * BLOCK : (i + 1) * BLOCK], 0.0) for i in range(count)
-        ]
-        part = jnp.concatenate(kept, axis=1) - loads
+        part = part_tile(mixed_t, coupling, mask, terms, target, tile)
         copies.append(send_tile(part, tile, part_buf, contrib, part_sems))
     for copy in copies:
         copy.wait()
@@ -137,7 +143,7 @@
         start_kernel,
         [far(load.shape), far((NXY, cases, BLOCK))],
         [HBM] * 2,
-        [SMEM] * 3 + [HBM] * 6,
+        [SMEM] * 2 + [HBM] * 6,
         [
             pltpu.SMEM(mask.shape, jnp.int32),
             pltpu.VMEM(inverse.shape, BF16),
@@ -212,56 +218,7 @@
     )
 
 
-def reorder_kernel(owner_in, mine, other, after, mine_out, other_out, token, owner, terms, sem):
-    copy = pltpu.make_async_copy(owner_in, owner, sem)
-    copy.start()
-    span, count = BLOCK // (NZ * PART), NZ * PART
-    token[...] = jnp.zeros(token.shape, F32)
-    left = lax.broadcasted_iota(jnp.int32, (BLOCK, BLOCK), 0)
-    right = lax.broadcasted_iota(jnp.int32, (BLOCK, BLOCK), 1)
-
-    def by_block(k):
-        return (k // PART) % span * count + k // (span * PART) * PART + k % PART
-
-    gather = (left == by_block(right)).astype(BF16)
-    scatter = (right == by_block(left)).astype(F32)
-    for n, source in enumerate((mine, other)):
-        base = source.shape[1] - NXY * PART
-        for i in range(NXY // span):
-            tile = source[:, base + 8 * i : base + 8 * (i + 1)].reshape(BLOCK, BLOCK)
-            for m, term in enumerate(split3(tile)):
-                moved = dot(gather, term).astype(BF16)
-                for j in range(span):
-                    row = (2 * m + n) * count
-                    col = (span * i + j) * BLOCK
-                    terms[row : row + count, col : col + BLOCK] = moved[j * count : (j + 1) * count]
-    copy.wait()
-    size = span * BLOCK
-    for i in range(NXY // span):
-        part = dot(terms[...], picks(owner, i, size))
-        part = part[: 2 * count] + part[2 * count : 4 * count] + part[4 * count :]
-        for n, out in enumerate((mine_out, other_out)):
-            stack = jnp.concatenate(
-                [part[n * count : (n + 1) * count, j * BLOCK : (j + 1) * BLOCK] for j in range(span)], axis=0
-            )
-            tile = jnp.dot(scatter, stack, precision=HIGHEST, preferred_element_type=F32)
-            out[:, 8 * i : 8 * (i + 1)] = tile.reshape(NZ, 8, BLOCK)
-
-
-def reorder(owner, mine, other, after):
-    shape = (NZ, NXY * PART, BLOCK)
-    return call(
-        reorder_kernel,
-        [f32(*shape)] * 2 + [f32(8, BLOCK)],
-        [VMEM] * 3,
-        [HBM, VMEM, VMEM, VMEM],
-        [pltpu.VMEM(owner.shape, jnp.int32), pltpu.VMEM((6 * NZ * PART, NXY * BLOCK), BF16), DMA],
-        PERMUTE_MIB,
-        owner, mine, other, after,
-    )
-
-
-def local_kernel(core, place, sep, own, other, delta, after, out, rows, buf):
+def local_rows(core, sep, own, other, delta, rows):
     first = core[0] == 0
     for t in range(NXY):
         mine, swapped = own[t], other[t, : 2 * OWN]
@@ -274,9 +231,7 @@
         part = dot(join(left[: 3 - i]), term)
         for j in range(3 - i):
             total = total - part[j * count : (j + 1) * count]
-    buf[...] = jnp.zeros(buf.shape, F32)
-    buf[pl.ds(pl.multiple_of(place[0], 8), count), :] = total
-    out[...] = buf[...].T
+    return total
 
 
 def case_group(total, z):
@@ -293,8 +248,8 @@
         out[z, group:] = packed[z % SPLIT]
 
 
-def sum_rows_kernel(parts, local_t, after, out):
-    total = local_t[...] - jnp.sum(parts[...], axis=0)
+def sum_rows_kernel(parts, out):
+    total = -jnp.sum(parts[...], axis=0)
     for z in range(NZ):
         out[z] = case_group(total, z)
 
@@ -372,26 +327,30 @@
 
 
 def middle_kernel(
-    first, delta, cubic_row, columns, inverse, solved, matrix, load, mixed_out, contrib, sep_out,
-    mixed, part_buf, mixed_sem, part_sems,
+    first, core, mask_in, owner_in, coupling_in, delta, cubic_row, columns, inverse, solved, matrix, load,
+    sep, matrix_rows, other, mixed_out, contrib, sep_out, mask, owner, coupling, mixed, rows, in_sems, mixed_sem,
 ):
+    waits = fetch((mask_in, owner_in, coupling_in), (mask, owner, coupling), in_sems)
     sep_out[...] = own_rows(first, delta, sep_out.shape[0])
     cubic = jnp.broadcast_to(cubic_row[...], (8, cubic_row.shape[1])).T[:, :1]
     coupled = dot(columns[...], delta[...].astype(BF16))
+    terms = join(split3(local_rows(core, sep, matrix_rows, other, delta, rows)))
     state = solved[...] - dot(inverse[...], coupled.astype(BF16))
     resid = load[...] - dot(matrix[...], state.astype(BF16)) - coupled
     resid = resid - cubic * state * state * state
     mixed[...] = state + dot(inverse[...], resid.astype(BF16))
+    copy = pltpu.make_async_copy(mixed, mixed_out, mixed_sem)
+    copy.start()
     mixed_t = mixed[...].T.astype(BF16)
-    count = part_sems.shape[0]
-    size = columns.shape[1] // count
-    copies = [pltpu.make_async_copy(mixed, mixed_out, mixed_sem)]
-    copies[0].start()
-    for i in range(count):
-        part = dot(mixed_t, columns[:, i * size : (i + 1) * size])
-        copies.append(send_tile(part, i, part_buf, contrib, part_sems))
-    for copy in copies:
-        copy.wait()
+    for wait in waits:
+        wait.wait()
+    size = coupling.shape[1] // OUT_TILES
+    target = targets(first, owner, sep.shape[0], size)
+    for tile in range(OUT_TILES):
+        part = part_tile(mixed_t, coupling, mask, terms, target, tile)
+        for i in range(size // BLOCK):
+            contrib[tile * (size // BLOCK) + i] = part[:, i * BLOCK : (i + 1) * BLOCK]
+    copy.wait()
 
 
 def end_kernel(first, delta, sep_in, columns, inverse, mixed, out, sep_out, state, out_sems):
@@ -433,11 +392,10 @@
     return solve(rhs, core, mine, other, between(rhs)), mine, other
 
 
-def second_correction(contrib, local_t, core, mine, other, owner):
+def second_correction(contrib, core, mine, other):
     group = contrib.shape[1] * SPLIT // NZ
     parts = exchange(contrib, ("x", "y"))
-    mine, other, token = reorder(owner, mine, other, local_t)
-    parts = call(sum_rows_kernel, f32(NZ, group, BLOCK), VMEM, [VMEM] * 3, [], 8, parts, local_t, token)
+    parts = call(sum_rows_kernel, f32(NZ, group, BLOCK), VMEM, [VMEM], [], 8, parts)
     parts = exchange(parts, "z")
     rhs = call(sum_cases_kernel, f32(NXY, group, BLOCK), VMEM, [VMEM], [], 4, parts)
     return solve(rhs, core, mine, other)
@@ -495,10 +453,9 @@
     owned, cases = sep_load.shape
     width, sep_width = coupling.shape
     core = lax.axis_index("c").astype(jnp.int32)[None]
-    place = (lax.axis_index("z") * owned).astype(jnp.int32)[None]
     first = (lax.axis_index(("x", "y", "z")) * owned).astype(jnp.int32)[None]
     owner = owner_map[None, :]
-    solved, contrib = start((first, core, place), block_mask, leaf_inverse, coupling, leaf_load, owner, sep_load)
+    solved, contrib = start((first, core), block_mask, leaf_inverse, coupling, leaf_load, owner, sep_load)
     columns, columns_again, packed, matrix_rows = permute(
         block_mask, owner, sep_inverse, sep_matrix, coupling, solved
     )
@@ -506,23 +463,23 @@
     delta, mine, other = correction(contrib, core, packed, matrix_rows)
     mixed, contrib, sep_rows = call(
         middle_kernel,
-        [far((width, cases)), far((NXY, cases, BLOCK)), f32(owned, cases)],
-        [HBM, HBM, VMEM],
-        [SMEM] + [VMEM] * 7,
-        [pltpu.VMEM((width, cases), F32), pltpu.VMEM((NXY, cases, BLOCK), F32), DMA, DMA((OUT_TILES,))],
+        [far((width, cases)), f32(NXY, cases, BLOCK), f32(owned, cases)],
+        [HBM, VMEM, VMEM],
+        [SMEM] * 2 + [HBM] * 3 + [VMEM] * 10,
+        [
+            pltpu.SMEM(block_mask.shape, jnp.int32),
+            pltpu.SMEM(owner.shape, jnp.int32),
+            pltpu.VMEM(coupling.shape, BF16),
+            pltpu.VMEM((width, cases), F32),
+            pltpu.VMEM((owned, sep_width), F32),
+            DMA((3,)),
+            DMA,
+        ],
         MIDDLE_MIB,
-        first, delta, cubic_coeff[None, :], columns, leaf_inverse, solved, leaf_matrix, leaf_load,
-    )
-    local_t = call(
-        local_kernel,
-        f32(cases, BLOCK),
-        VMEM,
-        [SMEM] * 2 + [VMEM] * 4 + [HBM],
-        [pltpu.VMEM((owned, sep_width), F32), pltpu.VMEM((BLOCK, cases), F32)],
-        8,
-        core, place, sep_load, matrix_rows, other, delta, contrib,
-    )
-    delta = second_correction(contrib, local_t, core, mine, other, owner)
+        first, core, block_mask, owner, coupling, delta, cubic_coeff[None, :], columns, leaf_inverse, solved, leaf_matrix,
+        leaf_load, sep_load, matrix_rows, other,
+    )
+    delta = second_correction(contrib, core, mine, other)
     return call(
         end_kernel,
         [far((width, cases)), f32(owned, cases)],

time: 203 us -> 203 us (level)
  blocking collectives: 135 us -> 152 us
  waiting for transfers between devices: 14.2 us -> 6.15 us
  starting transfers between devices: 23.3 us -> 17.6 us
  Pallas kernels: 27.8 us -> 24.4 us
    all_to_all x7 -> x8, blocking collectives: 135 us -> 152 us  [exchange(): return lax.all_to_all(parts, axes, 0, 0, tiled=True)]
    all_to_all x3 -> x2, waiting for transfers between devices: 14.2 us -> 6.15 us  [exchange(): return lax.all_to_all(parts, axes, 0, 0, tiled=True)]
    all_to_all x3 -> x2, starting transfers between devices: 21.4 us -> 15.7 us  [exchange(): return lax.all_to_all(parts, axes, 0, 0, tiled=True)]
    pallas_call x14 -> x12, Pallas kernels: 26.5 us -> 23.2 us  [call(): pl.pallas_call(kernel, out_shape=out_shape, out_specs=out_specs, in_specs...]
  transfers between devices with their start and end apart: 4 -> 3, of which waited for: 3 -> 2; matrix products, arithmetic and copies ran while one was open for 0% -> 0% of each run, Pallas kernels for 8% -> 5%
where the time goes in v9:
time: 203 us; the launch traced here: 201 us
  blocking collectives  152 us (75%)
  Pallas kernels  24.4 us (12%)
  starting transfers between devices  17.6 us (9%)
  waiting for transfers between devices  6.15 us (3%)
    all_to_all x8, blocking collectives, exchange(): return lax.all_to_all(parts, axes, 0, 0, tiled=True)  152 us
    pallas_call x12, Pallas kernels, call(): pl.pallas_call(kernel, out_shape=out_shape, out_specs=out_specs, in_specs...  23.2 us
    all_to_all x2, starting transfers between devices, exchange(): return lax.all_to_all(parts, axes, 0, 0, tiled=True)  15.7 us
    all_to_all x2, waiting for transfers between devices, exchange(): return lax.all_to_all(parts, axes, 0, 0, tiled=True)  6.15 us
  transfers between devices with their start and end apart: 3, of which 2 were waited for; matrix products, arithmetic and copies ran while one was open for 0% of the time, Pallas kernels for 5%

profile of v9, /device:TPU:6, one launch (start us, length us, event | category | flops | bytes accessed | tf_op | source)
XLA Modules:
  0.0 201.5 jit_solution(13527508226070024275)
XLA Ops:
  0.6 3.4 %shard_map.113 = (f32[512,128]{1,0:T(8,128)}, f32[16,128,128]{2,1,0:T(8,128)}) custom-call(s32[1]{0:T(128)} %bitcast.first, s32[1]{0:T(128)} %bitcast.1.core, s32[1,16]{1,0:T(1,128)} %mask_in.5, bf16[512,512]{1,0:T(8,128)(2,1)} %inverse.3, f32[512,128]{1,0:T(8,128)} %load.1, s32[1,2048]{1,0:T(1,128)} %bitcast.9, f32[8,128]{1,0:T(8,128)} %sep.1, ...), custom_call_target="tpu_custom_call" | custom-call | tf_op jit(solution)/shard_map/pallas_call | solution.py:43
  4.1 9.4 %all-to-all-start = ((f32[16,128,128]{2,1,0:T(8,128)}), f32[16,128,128]{2,1,0:T(8,128)S(1)}, u32[]{:S(2)}, u32[]{:S(2)}) async-start(f32[16,128,128]{2,1,0:T(8,128)} %get-tuple-element.13), calls=%async_computation | async-start | bytes 2097152 | tf_op jit(solution)/shard_map/all_to_all | solution.py:373
  13.5 9.8 %shard_map.114 = (bf16[512,2048]{1,0:T(8,128)(2,1)}, bf16[512,2048]{1,0:T(8,128)(2,1)}, f32[2,32,128]{2,1,0:T(8,128)S(1)}, f32[16,8,128]{2,1,0:T(8,128)S(1)}) custom-call(s32[1,16]{1,0:T(1,128)} %mask_in.5, s32[1,2048]{1,0:T(1,128)} %bitcast.10, f32[4,2048]{1,0:T(4,128)} %own_in.1, f32[4,2048]{1,0:T(4,128)} %matrix_in.1, bf16[512,2048]{1,0:T(8,128)(2,1)} %coupling_in.5, ...), custom_call_target="tpu_custom_call" | custom-call | tf_op jit(solution)/shard_map/pallas_call | solution.py:43
  23.3 3.5 %all-to-all-done.parts = f32[16,128,128]{2,1,0:T(8,128)S(1)} async-done(((f32[16,128,128]{2,1,0:T(8,128)}), f32[16,128,128]{2,1,0:T(8,128)S(1)}, u32[]{:S(2)}, u32[]{:S(2)}) %all-to-all-start) | async-done | bytes 1048608 | tf_op jit(solution)/shard_map/all_to_all | solution.py:373
  26.7 0.1 shard_map.115
  26.8 36.7 %all_to_all.50.parts.mine = f32[16,48,128]{2,1,0:T(8,128)S(1)} all-to-all(f32[16,48,128]{2,1,0:T(8,128)S(1)} %shard_map.115), channel_id=1, replica_groups=mesh['x'=4,'y'=4,'z'=16,'c'=2] {'z'}, dimensions={0} | all-to-all | bytes 786432 | tf_op jit(solution)/shard_map/all_to_all | solution.py:373
  63.5 0.8 shard_map.116
  64.3 6.4 %all-to-all-start.2 = ((f32[16,16,128]{2,1,0:T(8,128)}), f32[16,16,128]{2,1,0:T(8,128)S(1)}, u32[]{:S(2)}, u32[]{:S(2)}) async-start(f32[16,16,128]{2,1,0:T(8,128)} %get-tuple-element.17.rhs), calls=%async_computation.2 | async-start | bytes 262144 | tf_op jit(solution)/shard_map/all_to_all | solution.py:373
  70.7 1.9 collective-permute-start
  72.6 1.2 shard_map.117.after_and_out_0_
  73.9 2.7 %all-to-all-done.2.rhs = f32[16,16,128]{2,1,0:T(8,128)S(1)} async-done(((f32[16,16,128]{2,1,0:T(8,128)}), f32[16,16,128]{2,1,0:T(8,128)S(1)}, u32[]{:S(2)}, u32[]{:S(2)}) %all-to-all-start.2) | async-done | bytes 131104 | tf_op jit(solution)/shard_map/all_to_all | solution.py:373
  76.5 0.8 shard_map.118
  77.4 18.6 %all_to_all.51.parts = f32[16,8,128]{2,1,0:T(8,128)S(1)} all-to-all(f32[16,8,128]{2,1,0:T(8,128)S(1)} %shard_map.118), channel_id=1, replica_groups=mesh['x'=4,'y'=4,'z'=16,'c'=2] {'z'}, dimensions={0} | all-to-all | bytes 131072 | tf_op jit(solution)/shard_map/all_to_all | solution.py:373
  96.0 0.2 shard_map.119
  96.2 18.8 %all_to_all.52 = f32[16,128,128]{2,1,0:T(8,128)S(1)} all-to-all(f32[16,128,128]{2,1,0:T(8,128)S(1)} %shard_map.119), channel_id=1, replica_groups=mesh['x'=4,'y'=4,'z'=16,'c'=2] {'x','y'}, dimensions={0} | all-to-all | bytes 2097152 | tf_op jit(solution)/shard_map/all_to_all | solution.py:373
  115.1 4.5 %shard_map.120 = (f32[512,128]{1,0:T(8,128)}, f32[16,128,128]{2,1,0:T(8,128)S(1)}, f32[8,128]{1,0:T(8,128)S(1)}) custom-call(s32[1]{0:T(128)} %bitcast.first, s32[1]{0:T(128)} %bitcast.1.core, s32[1,16]{1,0:T(1,128)} %mask_in.5, s32[1,2048]{1,0:T(1,128)} %bitcast.11, bf16[512,2048]{1,0:T(8,128)(2,1)} %coupling_in.5, f32[2048,128]{1,0:T(8,128)S(1)} %bitcast.7, ...), custom_call_target="tpu_custom_call" | custom-call | tf_op jit(solution)/shard_map/pallas_call | solution.py:43
  119.6 17.7 %all_to_all.53.parts = f32[16,128,128]{2,1,0:T(8,128)S(1)} all-to-all(f32[16,128,128]{2,1,0:T(8,128)S(1)} %get-tuple-element.20), channel_id=1, replica_groups=mesh['x'=4,'y'=4,'z'=16,'c'=2] {'x','y'}, dimensions={0} | all-to-all | bytes 2097152 | tf_op jit(solution)/shard_map/all_to_all | solution.py:373
  137.3 16.6 %all_to_all.54.parts = f32[16,16,128]{2,1,0:T(8,128)S(1)} all-to-all(f32[16,16,128]{2,1,0:T(8,128)S(1)} %shard_map.121), channel_id=1, replica_groups=mesh['x'=4,'y'=4,'z'=16,'c'=2] {'z'}, dimensions={0} | all-to-all | bytes 262144 | tf_op jit(solution)/shard_map/all_to_all | solution.py:373
  154.0 11.0 %all_to_all.55.rhs = f32[16,16,128]{2,1,0:T(8,128)S(1)} all-to-all(f32[16,16,128]{2,1,0:T(8,128)S(1)} %shard_map.122), channel_id=1, replica_groups=mesh['x'=4,'y'=4,'z'=16,'c'=2] {'x','y'}, dimensions={0} | all-to-all | bytes 262144 | tf_op jit(solution)/shard_map/all_to_all | solution.py:373
  165.1 0.8 shard_map.123
  165.9 16.7 %all_to_all.56.parts = f32[16,8,128]{2,1,0:T(8,128)S(1)} all-to-all(f32[16,8,128]{2,1,0:T(8,128)S(1)} %shard_map.123), channel_id=1, replica_groups=mesh['x'=4,'y'=4,'z'=16,'c'=2] {'z'}, dimensions={0} | all-to-all | bytes 131072 | tf_op jit(solution)/shard_map/all_to_all | solution.py:373
  182.6 0.2 shard_map.124
  182.8 16.2 %all_to_all.57 = f32[16,128,128]{2,1,0:T(8,128)S(1)} all-to-all(f32[16,128,128]{2,1,0:T(8,128)S(1)} %shard_map.124), channel_id=1, replica_groups=mesh['x'=4,'y'=4,'z'=16,'c'=2] {'x','y'}, dimensions={0} | all-to-all | bytes 2097152 | tf_op jit(solution)/shard_map/all_to_all | solution.py:373
  199.0 2.4 %shard_map.125 = (f32[512,128]{1,0:T(8,128)}, f32[8,128]{1,0:T(8,128)}) custom-call(s32[1]{0:T(128)} %bitcast.first, f32[2048,128]{1,0:T(8,128)S(1)} %bitcast.6, f32[8,128]{1,0:T(8,128)S(1)} %get-tuple-element.21.sep_in, bf16[512,2048]{1,0:T(8,128)(2,1)S(1)} %copy-done.2, bf16[512,512]{1,0:T(8,128)(2,1)S(1)} %copy-done, f32[512,128]{1,0:T(8,128)S(1)} %copy-done.6), custom_call_target="tpu_custom_call" | custom-call | tf_op jit(solution)/shard_map/pallas_call | solution.py:43
  (21 shorter events, 0.1 us)
Async XLA Ops:
  4.1 22.7 %all-to-all-start = ((f32[16,128,128]{2,1,0:T(8,128)}), f32[16,128,128]{2,1,0:T(8,128)S(1)}, u32[]{:S(2)}, u32[]{:S(2)}) async-start(f32[16,128,128]{2,1,0:T(8,128)} %get-tuple-element.13), calls=%async_computation | async-start | bytes 2097152 | tf_op jit(solution)/shard_map/all_to_all | solution.py:373
  64.3 12.2 %all-to-all-start.2 = ((f32[16,16,128]{2,1,0:T(8,128)}), f32[16,16,128]{2,1,0:T(8,128)S(1)}, u32[]{:S(2)}, u32[]{:S(2)}) async-start(f32[16,16,128]{2,1,0:T(8,128)} %get-tuple-element.17.rhs), calls=%async_computation.2 | async-start | bytes 262144 | tf_op jit(solution)/shard_map/all_to_all | solution.py:373
  70.7 5.9 %collective-permute-start = (f32[16,40,128]{2,1,0:T(8,128)}, f32[16,40,128]{2,1,0:T(8,128)S(1)}, u32[]{:S(2)}, u32[]{:S(2)}) collective-permute-start(f32[16,40,128]{2,1,0:T(8,128)} %get-tuple-element.18), channel_id=1, source_target_pairs={{0,1},{1,0},{2,3},{3,2},{4,5},{5,4},{6,7},{7,6},{8,9},{9,8},{10,11... | collective-permute-start | bytes 983048 | tf_op jit(solution)/shard_map/ppermute | solution.py:391
  73.8 41.2 %copy-start = (bf16[512,512]{1,0:T(8,128)(2,1)S(1)}, bf16[512,512]{1,0:T(8,128)(2,1)}, u32[]{:S(2)}) copy-start(bf16[512,512]{1,0:T(8,128)(2,1)} %inverse.3) | copy-start | bytes 1572868
  73.8 41.2 %copy-start.1 = (bf16[512,2048]{1,0:T(8,128)(2,1)S(1)}, bf16[512,2048]{1,0:T(8,128)(2,1)}, u32[]{:S(2)}) copy-start(bf16[512,2048]{1,0:T(8,128)(2,1)} %get-tuple-element.19.columns) | copy-start | bytes 6291460
  73.8 41.2 %copy-start.7 = (f32[8,128]{1,0:T(8,128)S(1)}, f32[8,128]{1,0:T(8,128)}, u32[]{:S(2)}) copy-start(f32[8,128]{1,0:T(8,128)} %sep.1) | copy-start | bytes 12292
  73.8 41.2 %copy-start.8 = (f32[512]{0:T(512)S(1)}, f32[512]{0:T(512)}, u32[]{:S(2)}) copy-start(f32[512]{0:T(512)} %param.13) | copy-start | bytes 6148
  76.5 38.5 %copy-start.3 = (f32[512,128]{1,0:T(8,128)S(1)}, f32[512,128]{1,0:T(8,128)}, u32[]{:S(2)}) copy-start(f32[512,128]{1,0:T(8,128)} %load.1) | copy-start | bytes 786436
  76.5 38.5 %copy-start.4 = (f32[512,128]{1,0:T(8,128)S(1)}, f32[512,128]{1,0:T(8,128)}, u32[]{:S(2)}) copy-start(f32[512,128]{1,0:T(8,128)} %get-tuple-element.14.after.solved) | copy-start | bytes 786436
  76.5 38.5 %copy-start.5 = (bf16[512,512]{1,0:T(8,128)(2,1)S(1)}, bf16[512,512]{1,0:T(8,128)(2,1)}, u32[]{:S(2)}) copy-start(bf16[512,512]{1,0:T(8,128)(2,1)} %matrix.1) | copy-start | bytes 1572868
  165.1 34.0 %copy-start.2 = (bf16[512,2048]{1,0:T(8,128)(2,1)S(1)}, bf16[512,2048]{1,0:T(8,128)(2,1)}, u32[]{:S(2)}) copy-start(bf16[512,2048]{1,0:T(8,128)(2,1)} %get-tuple-element.22.columns) | copy-start | bytes 6291460
  165.1 34.0 %copy-start.6 = (f32[512,128]{1,0:T(8,128)S(1)}, f32[512,128]{1,0:T(8,128)}, u32[]{:S(2)}) copy-start(f32[512,128]{1,0:T(8,128)} %get-tuple-element.23.mixed) | copy-start | bytes 786436

commit v10 on v9

--- a/solution.py
+++ b/solution.py
@@ -401,10 +401,8 @@
     return solve(rhs, core, mine, other)
 
 
-def between_kernel(rhs, out, sem):
-    copy = pltpu.make_async_copy(rhs.at[0, :8], out, sem)
-    copy.start()
-    copy.wait()
+def between_kernel(rhs, out):
+    pass
 
 
 def between(rhs):
@@ -413,7 +411,6 @@
         out_shape=far((8, BLOCK)),
         in_specs=[HBM],
         out_specs=HBM,
-        scratch_shapes=[DMA],
         cost_estimate=pl.CostEstimate(flops=10**10, transcendentals=0, bytes_accessed=8192),
     )(pltpu.with_memory_space_constraint(rhs, pltpu.HBM))
 

time: 203 us -> 203 us (level)
  no operation moved by 1% of the time
where the time goes in v10:
time: 203 us; the launch traced here: 201 us
  blocking collectives  152 us (75%)
  Pallas kernels  23.2 us (11%)
  starting transfers between devices  17.6 us (9%)
  waiting for transfers between devices  7.38 us (4%)
    all_to_all x8, blocking collectives, exchange(): return lax.all_to_all(parts, axes, 0, 0, tiled=True)  152 us
    pallas_call x12, Pallas kernels, call(): pl.pallas_call(kernel, out_shape=out_shape, out_specs=out_specs, in_specs...  23.2 us
    all_to_all x2, starting transfers between devices, exchange(): return lax.all_to_all(parts, axes, 0, 0, tiled=True)  15.7 us
    all_to_all x2, waiting for transfers between devices, exchange(): return lax.all_to_all(parts, axes, 0, 0, tiled=True)  7.38 us
  transfers between devices with their start and end apart: 3, of which 2 were waited for; matrix products, arithmetic and copies ran while one was open for 0% of the time, Pallas kernels for 5%

profile of v10, /device:TPU:6, one launch (start us, length us, event | category | flops | bytes accessed | tf_op | source)
XLA Modules:
  0.0 201.3 jit_solution(12951552398601410678)
XLA Ops:
  0.6 3.4 %shard_map.113 = (f32[512,128]{1,0:T(8,128)}, f32[16,128,128]{2,1,0:T(8,128)}) custom-call(s32[1]{0:T(128)} %bitcast.first, s32[1]{0:T(128)} %bitcast.1.core, s32[1,16]{1,0:T(1,128)} %mask_in.5, bf16[512,512]{1,0:T(8,128)(2,1)} %inverse.3, f32[512,128]{1,0:T(8,128)} %load.1, s32[1,2048]{1,0:T(1,128)} %bitcast.9, f32[8,128]{1,0:T(8,128)} %sep.1, ...), custom_call_target="tpu_custom_call" | custom-call | tf_op jit(solution)/shard_map/pallas_call | solution.py:43
  4.1 9.4 %all-to-all-start = ((f32[16,128,128]{2,1,0:T(8,128)}), f32[16,128,128]{2,1,0:T(8,128)S(1)}, u32[]{:S(2)}, u32[]{:S(2)}) async-start(f32[16,128,128]{2,1,0:T(8,128)} %get-tuple-element.13), calls=%async_computation | async-start | bytes 2097152 | tf_op jit(solution)/shard_map/all_to_all | solution.py:373
  13.5 9.8 %shard_map.114 = (bf16[512,2048]{1,0:T(8,128)(2,1)}, bf16[512,2048]{1,0:T(8,128)(2,1)}, f32[2,32,128]{2,1,0:T(8,128)S(1)}, f32[16,8,128]{2,1,0:T(8,128)S(1)}) custom-call(s32[1,16]{1,0:T(1,128)} %mask_in.5, s32[1,2048]{1,0:T(1,128)} %bitcast.10, f32[4,2048]{1,0:T(4,128)} %own_in.1, f32[4,2048]{1,0:T(4,128)} %matrix_in.1, bf16[512,2048]{1,0:T(8,128)(2,1)} %coupling_in.5, ...), custom_call_target="tpu_custom_call" | custom-call | tf_op jit(solution)/shard_map/pallas_call | solution.py:43
  23.3 3.5 %all-to-all-done.parts = f32[16,128,128]{2,1,0:T(8,128)S(1)} async-done(((f32[16,128,128]{2,1,0:T(8,128)}), f32[16,128,128]{2,1,0:T(8,128)S(1)}, u32[]{:S(2)}, u32[]{:S(2)}) %all-to-all-start) | async-done | bytes 1048608 | tf_op jit(solution)/shard_map/all_to_all | solution.py:373
  26.7 0.1 shard_map.115
  26.8 36.7 %all_to_all.50.parts.mine = f32[16,48,128]{2,1,0:T(8,128)S(1)} all-to-all(f32[16,48,128]{2,1,0:T(8,128)S(1)} %shard_map.115), channel_id=1, replica_groups=mesh['x'=4,'y'=4,'z'=16,'c'=2] {'z'}, dimensions={0} | all-to-all | bytes 786432 | tf_op jit(solution)/shard_map/all_to_all | solution.py:373
  63.5 0.8 shard_map.116
  64.3 6.4 %all-to-all-start.2 = ((f32[16,16,128]{2,1,0:T(8,128)}), f32[16,16,128]{2,1,0:T(8,128)S(1)}, u32[]{:S(2)}, u32[]{:S(2)}) async-start(f32[16,16,128]{2,1,0:T(8,128)} %get-tuple-element.17.rhs), calls=%async_computation.2 | async-start | bytes 262144 | tf_op jit(solution)/shard_map/all_to_all | solution.py:373
  70.7 1.9 collective-permute-start
  72.6 3.9 %all-to-all-done.2.rhs = f32[16,16,128]{2,1,0:T(8,128)S(1)} async-done(((f32[16,16,128]{2,1,0:T(8,128)}), f32[16,16,128]{2,1,0:T(8,128)S(1)}, u32[]{:S(2)}, u32[]{:S(2)}) %all-to-all-start.2) | async-done | bytes 131104 | tf_op jit(solution)/shard_map/all_to_all | solution.py:373
  76.5 0.8 shard_map.118
  77.4 18.7 %all_to_all.51.parts = f32[16,8,128]{2,1,0:T(8,128)S(1)} all-to-all(f32[16,8,128]{2,1,0:T(8,128)S(1)} %shard_map.118), channel_id=1, replica_groups=mesh['x'=4,'y'=4,'z'=16,'c'=2] {'z'}, dimensions={0} | all-to-all | bytes 131072 | tf_op jit(solution)/shard_map/all_to_all | solution.py:373
  96.0 0.2 shard_map.119
  96.3 18.7 %all_to_all.52 = f32[16,128,128]{2,1,0:T(8,128)S(1)} all-to-all(f32[16,128,128]{2,1,0:T(8,128)S(1)} %shard_map.119), channel_id=1, replica_groups=mesh['x'=4,'y'=4,'z'=16,'c'=2] {'x','y'}, dimensions={0} | all-to-all | bytes 2097152 | tf_op jit(solution)/shard_map/all_to_all | solution.py:373
  115.0 4.5 %shard_map.120 = (f32[512,128]{1,0:T(8,128)}, f32[16,128,128]{2,1,0:T(8,128)S(1)}, f32[8,128]{1,0:T(8,128)S(1)}) custom-call(s32[1]{0:T(128)} %bitcast.first, s32[1]{0:T(128)} %bitcast.1.core, s32[1,16]{1,0:T(1,128)} %mask_in.5, s32[1,2048]{1,0:T(1,128)} %bitcast.11, bf16[512,2048]{1,0:T(8,128)(2,1)} %coupling_in.5, f32[2048,128]{1,0:T(8,128)S(1)} %bitcast.7, ...), custom_call_target="tpu_custom_call" | custom-call | tf_op jit(solution)/shard_map/pallas_call | solution.py:43
  119.5 17.6 %all_to_all.53.parts = f32[16,128,128]{2,1,0:T(8,128)S(1)} all-to-all(f32[16,128,128]{2,1,0:T(8,128)S(1)} %get-tuple-element.20), channel_id=1, replica_groups=mesh['x'=4,'y'=4,'z'=16,'c'=2] {'x','y'}, dimensions={0} | all-to-all | bytes 2097152 | tf_op jit(solution)/shard_map/all_to_all | solution.py:373
  137.0 0.1 shard_map.121
  137.1 16.7 %all_to_all.54.parts = f32[16,16,128]{2,1,0:T(8,128)S(1)} all-to-all(f32[16,16,128]{2,1,0:T(8,128)S(1)} %shard_map.121), channel_id=1, replica_groups=mesh['x'=4,'y'=4,'z'=16,'c'=2] {'z'}, dimensions={0} | all-to-all | bytes 262144 | tf_op jit(solution)/shard_map/all_to_all | solution.py:373
  153.8 11.0 %all_to_all.55.rhs = f32[16,16,128]{2,1,0:T(8,128)S(1)} all-to-all(f32[16,16,128]{2,1,0:T(8,128)S(1)} %shard_map.122), channel_id=1, replica_groups=mesh['x'=4,'y'=4,'z'=16,'c'=2] {'x','y'}, dimensions={0} | all-to-all | bytes 262144 | tf_op jit(solution)/shard_map/all_to_all | solution.py:373
  164.9 0.8 shard_map.123
  165.7 16.7 %all_to_all.56.parts = f32[16,8,128]{2,1,0:T(8,128)S(1)} all-to-all(f32[16,8,128]{2,1,0:T(8,128)S(1)} %shard_map.123), channel_id=1, replica_groups=mesh['x'=4,'y'=4,'z'=16,'c'=2] {'z'}, dimensions={0} | all-to-all | bytes 131072 | tf_op jit(solution)/shard_map/all_to_all | solution.py:373
  182.4 0.2 shard_map.124
  182.6 16.2 %all_to_all.57 = f32[16,128,128]{2,1,0:T(8,128)S(1)} all-to-all(f32[16,128,128]{2,1,0:T(8,128)S(1)} %shard_map.124), channel_id=1, replica_groups=mesh['x'=4,'y'=4,'z'=16,'c'=2] {'x','y'}, dimensions={0} | all-to-all | bytes 2097152 | tf_op jit(solution)/shard_map/all_to_all | solution.py:373
  198.9 2.4 %shard_map.125 = (f32[512,128]{1,0:T(8,128)}, f32[8,128]{1,0:T(8,128)}) custom-call(s32[1]{0:T(128)} %bitcast.first, f32[2048,128]{1,0:T(8,128)S(1)} %bitcast.6, f32[8,128]{1,0:T(8,128)S(1)} %get-tuple-element.21.sep_in, bf16[512,2048]{1,0:T(8,128)(2,1)S(1)} %copy-done.2, bf16[512,512]{1,0:T(8,128)(2,1)S(1)} %copy-done, f32[512,128]{1,0:T(8,128)S(1)} %copy-done.6), custom_call_target="tpu_custom_call" | custom-call | tf_op jit(solution)/shard_map/pallas_call | solution.py:43
  (21 shorter events, 0.1 us)
Async XLA Ops:
  4.1 22.7 %all-to-all-start = ((f32[16,128,128]{2,1,0:T(8,128)}), f32[16,128,128]{2,1,0:T(8,128)S(1)}, u32[]{:S(2)}, u32[]{:S(2)}) async-start(f32[16,128,128]{2,1,0:T(8,128)} %get-tuple-element.13), calls=%async_computation | async-start | bytes 2097152 | tf_op jit(solution)/shard_map/all_to_all | solution.py:373
  64.3 12.2 %all-to-all-start.2 = ((f32[16,16,128]{2,1,0:T(8,128)}), f32[16,16,128]{2,1,0:T(8,128)S(1)}, u32[]{:S(2)}, u32[]{:S(2)}) async-start(f32[16,16,128]{2,1,0:T(8,128)} %get-tuple-element.17.rhs), calls=%async_computation.2 | async-start | bytes 262144 | tf_op jit(solution)/shard_map/all_to_all | solution.py:373
  70.7 5.9 %collective-permute-start = (f32[16,40,128]{2,1,0:T(8,128)}, f32[16,40,128]{2,1,0:T(8,128)S(1)}, u32[]{:S(2)}, u32[]{:S(2)}) collective-permute-start(f32[16,40,128]{2,1,0:T(8,128)} %get-tuple-element.18), channel_id=1, source_target_pairs={{0,1},{1,0},{2,3},{3,2},{4,5},{5,4},{6,7},{7,6},{8,9},{9,8},{10,11... | collective-permute-start | bytes 983048 | tf_op jit(solution)/shard_map/ppermute | solution.py:391
  72.6 42.3 %copy-start = (bf16[512,512]{1,0:T(8,128)(2,1)S(1)}, bf16[512,512]{1,0:T(8,128)(2,1)}, u32[]{:S(2)}) copy-start(bf16[512,512]{1,0:T(8,128)(2,1)} %inverse.3) | copy-start | bytes 1572868
  72.6 42.3 %copy-start.1 = (bf16[512,2048]{1,0:T(8,128)(2,1)S(1)}, bf16[512,2048]{1,0:T(8,128)(2,1)}, u32[]{:S(2)}) copy-start(bf16[512,2048]{1,0:T(8,128)(2,1)} %get-tuple-element.19.columns) | copy-start | bytes 6291460
  72.6 42.3 %copy-start.7 = (f32[8,128]{1,0:T(8,128)S(1)}, f32[8,128]{1,0:T(8,128)}, u32[]{:S(2)}) copy-start(f32[8,128]{1,0:T(8,128)} %sep.1) | copy-start | bytes 12292
  72.6 42.3 %copy-start.8 = (f32[512]{0:T(512)S(1)}, f32[512]{0:T(512)}, u32[]{:S(2)}) copy-start(f32[512]{0:T(512)} %param.13) | copy-start | bytes 6148
  76.5 38.4 %copy-start.3 = (f32[512,128]{1,0:T(8,128)S(1)}, f32[512,128]{1,0:T(8,128)}, u32[]{:S(2)}) copy-start(f32[512,128]{1,0:T(8,128)} %load.1) | copy-start | bytes 786436
  76.5 38.4 %copy-start.4 = (f32[512,128]{1,0:T(8,128)S(1)}, f32[512,128]{1,0:T(8,128)}, u32[]{:S(2)}) copy-start(f32[512,128]{1,0:T(8,128)} %get-tuple-element.14.after.solved) | copy-start | bytes 786436
  76.5 38.4 %copy-start.5 = (bf16[512,512]{1,0:T(8,128)(2,1)S(1)}, bf16[512,512]{1,0:T(8,128)(2,1)}, u32[]{:S(2)}) copy-start(bf16[512,512]{1,0:T(8,128)(2,1)} %matrix.1) | copy-start | bytes 1572868
  164.9 34.0 %copy-start.2 = (bf16[512,2048]{1,0:T(8,128)(2,1)S(1)}, bf16[512,2048]{1,0:T(8,128)(2,1)}, u32[]{:S(2)}) copy-start(bf16[512,2048]{1,0:T(8,128)(2,1)} %get-tuple-element.22.columns) | copy-start | bytes 6291460
  164.9 34.0 %copy-start.6 = (f32[512,128]{1,0:T(8,128)S(1)}, f32[512,128]{1,0:T(8,128)}, u32[]{:S(2)}) copy-start(f32[512,128]{1,0:T(8,128)} %get-tuple-element.23.mixed) | copy-start | bytes 786436
